TPU v7x, 32 devices: a whole 2x2x4 slice. The times are simulated.
32 devices in a mesh: dp: 4 (over z), seq: 4 (over y, x), mp: 2 (over core).
Axes of the slice: x: 2, y: 2, z: 4, core: 2. Of those that a mesh axis runs over, the one named last changes fastest.
Arguments:
- tokens: bfloat16 [4, 1024, 896], P('dp', 'seq')
- neighbours: bfloat16 [4, 16, 2, 128, 896], P('dp', 'seq'), may hold values from -6 to 6
- neighbour_lengths: int32 [4, 16, 2], P('dp', 'seq'), may hold values from 1 to 128, as said below
- segment_ids: int32 [4, 1024], P('dp', 'seq'), may hold values from 0 to 7, never falling along the last dimension, each value on 1 to 512 neighbouring positions
- out_grad: bfloat16 [4, 1024, 896], P('dp', 'seq'), may hold values from -6 to 6
- self_weights: float32 [4, 896, 1024], P(None, ('dp', 'seq'), 'mp')
- cross_weights: float32 [4, 896, 1024], P(None, ('dp', 'seq'), 'mp')
- feed_weights: float32 [2, 896, 3584], P(None, ('dp', 'seq'), 'mp')
- norm_gains: float32 [3, 896], P(None, ('dp', 'seq'))
- self_first: float32 [4, 896, 1024], P(None, ('dp', 'seq'), 'mp'), may hold values from -0.0004272461 to 0.0004272461
- cross_first: float32 [4, 896, 1024], P(None, ('dp', 'seq'), 'mp'), may hold values from -0.0004272461 to 0.0004272461
- feed_first: float32 [2, 896, 3584], P(None, ('dp', 'seq'), 'mp'), may hold values from -0.0004272461 to 0.0004272461
- gains_first: float32 [3, 896], P(None, ('dp', 'seq')), may hold values from -0.0012207031 to 0.0012207031
- self_second: float32 [4, 896, 1024], P(None, ('dp', 'seq'), 'mp'), may hold values from 2.1794013e-09 to 2.9058684e-08
- cross_second: float32 [4, 896, 1024], P(None, ('dp', 'seq'), 'mp'), may hold values from 2.1794013e-09 to 2.9058684e-08
- feed_second: float32 [2, 896, 3584], P(None, ('dp', 'seq'), 'mp'), may hold values from 2.1794013e-09 to 2.9058684e-08
- gains_second: float32 [3, 896], P(None, ('dp', 'seq')), may hold values from 1.9614612e-08 to 2.6152816e-07
Outputs:
- out: bfloat16 [4, 1024, 896], P('dp', 'seq')
- in_grad: float32 [4, 1024, 896], P('dp', 'seq')
- grad_norm: float32 [], replicated
- self_new: float32 [4, 896, 1024], P(None, ('dp', 'seq'), 'mp')
- cross_new: float32 [4, 896, 1024], P(None, ('dp', 'seq'), 'mp')
- feed_new: float32 [2, 896, 3584], P(None, ('dp', 'seq'), 'mp')
- gains_new: float32 [3, 896], P(None, ('dp', 'seq'))
- self_first_new: float32 [4, 896, 1024], P(None, ('dp', 'seq'), 'mp')
- cross_first_new: float32 [4, 896, 1024], P(None, ('dp', 'seq'), 'mp')
- feed_first_new: float32 [2, 896, 3584], P(None, ('dp', 'seq'), 'mp')
- gains_first_new: float32 [3, 896], P(None, ('dp', 'seq'))
- self_second_new: float32 [4, 896, 1024], P(None, ('dp', 'seq'), 'mp')
- cross_second_new: float32 [4, 896, 1024], P(None, ('dp', 'seq'), 'mp')
- feed_second_new: float32 [2, 896, 3584], P(None, ('dp', 'seq'), 'mp')
- gains_second_new: float32 [3, 896], P(None, ('dp', 'seq'))
Inputs may be any that keep to these rules, and one draw needn't show every extreme that they name: `segment_ids`: segment ids never fall along a row; each of the 8 documents of a row has 1 to 512 tokens. `neighbour_lengths`: the valid tokens of a neighbour are its first ones; in every row, both neighbours of some retrieval block are full.
All inputs are finite; a program needn't handle non-finite values.
Results may differ from a plain program's by a relative error of at most 0.018.
Values may be sent and summed in bfloat16 or wider, within the bound.
No kernel may reach another device: no remote copies, remote signals or barrier semaphores. Data moves between devices by JAX's collectives and lax.ppermute only.
A program may use at most 192 MiB of HBM per device.

v0:
```python
from functools import partial

import jax
import jax.numpy as jnp
from jax import lax
from jax.sharding import PartitionSpec as P

HEAD_DIM = 64
BLOCK = 64
NEIGHBOURS = 2
NEIGH_LEN = 128
STEP = 10


norm_eps = 1e-05
rope_base = 10000.0
beta_one = 0.9
beta_two = 0.95
adam_eps = 1e-08
weight_decay = 0.1
learn_rate = 0.1
gain_rate = 0.5
clip_limit = 1.0
masked_fill = -1e30


def passed_along(value, axis, by):
    count = lax.axis_size(axis)
    pairs = [(i, i + by) for i in range(count) if 0 <= i + by < count]
    return lax.ppermute(value, axis, pairs)


def to_low(array_in):
    return array_in.astype(jnp.bfloat16)


def rms_apply(inputs, gain_row):
    factor = lax.rsqrt(jnp.mean(inputs * inputs, axis=-1, keepdims=True) + norm_eps)
    return inputs * factor * gain_row


def rope_apply(field_in, positions):
    half_dim = field_in.shape[-1] // 2
    frequency = rope_base ** (-jnp.arange(half_dim, dtype=jnp.float32) / half_dim)
    angles = positions[:, None] * frequency[None, :]
    cosine = jnp.cos(angles)[:, None, :]
    sine_part = jnp.sin(angles)[:, None, :]
    lead_half = field_in[..., :half_dim]
    tail_half = field_in[..., half_dim:]
    return jnp.concatenate(
        [lead_half * cosine - tail_half * sine_part, lead_half * sine_part + tail_half * cosine],
        axis=-1,
    )


def head_sum(partial_out):
    share = lax.psum_scatter(partial_out, "mp", scatter_dimension=1, tiled=True)
    return lax.all_gather(share, "mp", axis=1, tiled=True)


def norm_sum(partial_grad):
    share = lax.psum_scatter(partial_grad, "mp", scatter_dimension=1, tiled=True)
    return lax.all_gather(share, "mp", axis=1, tiled=True)


def adam_step(weight, gradient, first_old, second_old, factor, step_rate, decay_coef):
    clipped = gradient * factor
    first_new = beta_one * first_old + (1.0 - beta_one) * clipped
    second_new = beta_two * second_old + (1.0 - beta_two) * clipped * clipped
    first_hat = first_new / (1.0 - beta_one**STEP)
    second_hat = second_new / (1.0 - beta_two**STEP)
    weight_new = weight - step_rate * (
        first_hat / (jnp.sqrt(second_hat) + adam_eps) + decay_coef * weight
    )
    return (weight_new, first_new, second_new)


def per_device(
    tokens,
    neighbours,
    neighbour_lengths,
    segment_ids,
    out_grad,
    self_weights,
    cross_weights,
    feed_weights,
    norm_gains,
    self_first,
    cross_first,
    feed_first,
    gains_first,
    self_second,
    cross_second,
    feed_second,
    gains_second,
):
    f32 = jnp.float32
    row_count, span_len, model_width = tokens.shape
    token_count = row_count * span_len
    local_width = self_weights.shape[2]
    heads_here = local_width // HEAD_DIM
    score_scale = HEAD_DIM ** (-0.5)
    piece_count = lax.axis_size("seq")
    blocks_here = span_len // BLOCK
    key_count = NEIGHBOURS * NEIGH_LEN
    head_shape = (row_count, span_len, heads_here, HEAD_DIM)
    full_self, full_cross, full_feed, full_gains = (
        lax.all_gather(to_low(self_weights), ("dp", "seq"), axis=1, tiled=True),
        lax.all_gather(to_low(cross_weights), ("dp", "seq"), axis=1, tiled=True),
        lax.all_gather(to_low(feed_weights), ("dp", "seq"), axis=1, tiled=True),
        lax.all_gather(to_low(norm_gains), ("dp", "seq"), axis=1, tiled=True),
    )
    gain_values = full_gains.astype(f32)
    inputs = tokens.astype(f32).reshape(token_count, model_width)
    first_pos = lax.axis_index("seq") * span_len
    query_pos = first_pos + jnp.arange(span_len, dtype=jnp.int32)
    angle_pos = query_pos.astype(f32)
    normed_one, norm_back_one = jax.vjp(rms_apply, inputs, gain_values[0])
    normed_one = to_low(normed_one)
    projected = jnp.einsum("td,kde->kte", normed_one, full_self[:3], preferred_element_type=f32)
    query_raw = projected[0].reshape(head_shape)
    query_rot, rope_back = jax.vjp(lambda field_in: rope_apply(field_in, angle_pos), query_raw)
    key_rot = rope_apply(projected[1].reshape(head_shape), angle_pos)
    query_low = to_low(query_rot)
    key_low = to_low(key_rot)
    value_low = to_low(projected[2].reshape(head_shape))
    segs_low = segment_ids.astype(jnp.bfloat16)
    keys_all, values_all, segs_all = (
        lax.all_gather(key_low, "seq", axis=1, tiled=True),
        lax.all_gather(value_low, "seq", axis=1, tiled=True),
        lax.all_gather(segs_low, "seq", axis=1, tiled=True),
    )

    def self_piece(piece_index):
        piece_start = piece_index * span_len
        keys_piece = keys_all[:, piece_start : piece_start + span_len]
        values_piece = values_all[:, piece_start : piece_start + span_len]
        scores = (
            jnp.einsum("rqhd,rkhd->rhqk", query_low, keys_piece, preferred_element_type=f32)
            * score_scale
        )
        key_pos = piece_start + jnp.arange(span_len, dtype=jnp.int32)
        causal = key_pos[None, :] <= query_pos[:, None]
        same_doc = segs_all[:, None, piece_start : piece_start + span_len] == segs_low[:, :, None]
        allowed = jnp.logical_and(causal[None], same_doc)[:, None]
        return (scores, allowed, keys_piece, values_piece)

    row_max = jnp.full((row_count, heads_here, span_len, 1), masked_fill, f32)
    row_total = jnp.zeros((row_count, heads_here, span_len, 1), f32)
    for piece_index in range(piece_count):
        scores, allowed, keys_piece, values_piece = self_piece(piece_index)
        new_max = jnp.maximum(
            row_max, jnp.max(jnp.where(allowed, scores, masked_fill), axis=-1, keepdims=True)
        )
        row_total = row_total * jnp.exp(row_max - new_max) + jnp.sum(
            jnp.where(allowed, jnp.exp(scores - new_max), 0.0), axis=-1, keepdims=True
        )
        row_max = new_max
    self_lse = row_max + jnp.log(row_total)
    attn_acc = jnp.zeros(head_shape, f32)
    for piece_index in range(piece_count):
        scores, allowed, keys_piece, values_piece = self_piece(piece_index)
        prob_piece = jnp.where(allowed, jnp.exp(scores - self_lse), 0.0)
        attn_acc = attn_acc + jnp.einsum(
            "rhqk,rkhd->rqhd", to_low(prob_piece), values_piece, preferred_element_type=f32
        )
    attn_low = to_low(attn_acc).reshape(token_count, local_width)
    hidden_one = inputs + head_sum(jnp.dot(attn_low, full_self[3].T, preferred_element_type=f32))
    normed_two, norm_back_two = jax.vjp(rms_apply, hidden_one, gain_values[1])
    normed_two = to_low(normed_two)
    cross_query = to_low(jnp.dot(normed_two, full_cross[0], preferred_element_type=f32)).reshape(
        head_shape
    )
    neighbour_flat = neighbours.reshape(-1, model_width)
    cross_kv = to_low(
        jnp.einsum("nd,kde->kne", neighbour_flat, full_cross[1:3], preferred_element_type=f32)
    ).reshape(2, row_count, blocks_here, key_count, heads_here, HEAD_DIM)
    key_valid = (
        jnp.arange(NEIGH_LEN, dtype=jnp.int32)[None, None, None, :]
        < neighbour_lengths[:, :, :, None]
    )
    valid_low = key_valid.reshape(row_count, blocks_here, key_count).astype(jnp.bfloat16)
    prev_keys, prev_values, prev_valid, prev_seg = passed_along(
        (cross_kv[0, :, -1], cross_kv[1, :, -1], valid_low[:, -1], segs_low[:, -1]), "seq", 1
    )
    block_keys = jnp.concatenate([prev_keys[:, None], cross_kv[0]], axis=1)
    block_values = jnp.concatenate([prev_values[:, None], cross_kv[1]], axis=1)
    block_valid = jnp.concatenate([prev_valid[:, None], valid_low], axis=1) > 0.5
    allowed_cross = block_valid[:, :, None, None, :]
    seg_pad = jnp.concatenate(
        [prev_seg[:, None], segs_low, jnp.zeros((row_count, BLOCK - 1), jnp.bfloat16)], axis=1
    ).reshape(row_count, blocks_here + 1, BLOCK)
    keep_mask = seg_pad == seg_pad[:, :, :1]
    keep_float = keep_mask.astype(f32)[:, :, :, None, None]
    keep_low = keep_mask.astype(jnp.bfloat16)[:, :, :, None, None]

    def to_blocks(field_in):
        tail_shape = field_in.shape[2:]
        padded = jnp.concatenate(
            [
                jnp.zeros((row_count, 1) + tail_shape, field_in.dtype),
                field_in,
                jnp.zeros((row_count, BLOCK - 1) + tail_shape, field_in.dtype),
            ],
            axis=1,
        )
        return padded.reshape(row_count, blocks_here + 1, BLOCK, heads_here, HEAD_DIM)

    def from_blocks(blocks_in):
        return blocks_in.reshape(row_count, (blocks_here + 1) * BLOCK, heads_here, HEAD_DIM)[
            :, 1 : span_len + 1
        ]

    query_blocks = to_blocks(cross_query)

    def cross_scores():
        return (
            jnp.einsum("rbqhd,rbkhd->rbhqk", query_blocks, block_keys, preferred_element_type=f32)
            * score_scale
        )

    scores = cross_scores()
    cross_max = jnp.max(jnp.where(allowed_cross, scores, masked_fill), axis=-1, keepdims=True)
    cross_total = jnp.sum(
        jnp.where(allowed_cross, jnp.exp(scores - cross_max), 0.0), axis=-1, keepdims=True
    )
    cross_lse = cross_max + jnp.log(cross_total)
    cross_prob = jnp.where(allowed_cross, jnp.exp(scores - cross_lse), 0.0)
    cross_out = from_blocks(
        jnp.einsum(
            "rbhqk,rbkhd->rbqhd", to_low(cross_prob), block_values, preferred_element_type=f32
        )
        * keep_float
    )
    cross_low = to_low(cross_out).reshape(token_count, local_width)
    hidden_two = hidden_one + head_sum(
        jnp.dot(cross_low, full_cross[3].T, preferred_element_type=f32)
    )
    normed_three, norm_back_three = jax.vjp(rms_apply, hidden_two, gain_values[2])
    normed_three = to_low(normed_three)
    upward = jnp.dot(normed_three, full_feed[0], preferred_element_type=f32)
    active, gelu_back = jax.vjp(partial(jax.nn.gelu, approximate=True), upward)
    active_low = to_low(active)
    result = hidden_two + head_sum(jnp.dot(active_low, full_feed[1].T, preferred_element_type=f32))
    out = to_low(result).reshape(row_count, span_len, model_width)
    back_self, back_cross, back_feed = (
        lax.all_gather(to_low(self_weights), ("dp", "seq"), axis=1, tiled=True),
        lax.all_gather(to_low(cross_weights), ("dp", "seq"), axis=1, tiled=True),
        lax.all_gather(to_low(feed_weights), ("dp", "seq"), axis=1, tiled=True),
    )
    cotangent = out_grad.astype(f32).reshape(token_count, model_width)
    cot_low = to_low(cotangent)
    grad_down = jnp.einsum("td,tf->df", cot_low, active_low, preferred_element_type=f32)
    grad_active = jnp.dot(cot_low, back_feed[1], preferred_element_type=f32)
    grad_upward = to_low(gelu_back(grad_active)[0])
    grad_up = jnp.einsum("td,tf->df", normed_three, grad_upward, preferred_element_type=f32)
    grad_normed = norm_sum(
        jnp.einsum("tf,df->td", grad_upward, back_feed[0], preferred_element_type=f32)
    )
    from_norm, grad_gain_three = norm_back_three(grad_normed)
    grad_two = cotangent + from_norm
    feed_grads = jnp.stack([grad_up, grad_down])
    resid_low = to_low(grad_two)
    grad_cross_out = jnp.einsum("td,te->de", resid_low, cross_low, preferred_element_type=f32)
    grad_cross_att = to_low(jnp.dot(resid_low, back_cross[3], preferred_element_type=f32)).reshape(
        head_shape
    )
    grad_blocks = to_blocks(grad_cross_att) * keep_low
    scores = cross_scores()
    cross_prob = jnp.where(allowed_cross, jnp.exp(scores - cross_lse), 0.0)
    grad_prob = jnp.einsum(
        "rbqhd,rbkhd->rbhqk", grad_blocks, block_values, preferred_element_type=f32
    )
    dot_sum = jnp.sum(cross_prob * grad_prob, axis=-1, keepdims=True)
    grad_score = to_low(cross_prob * (grad_prob - dot_sum))
    grad_cross_query = (
        from_blocks(
            jnp.einsum("rbhqk,rbkhd->rbqhd", grad_score, block_keys, preferred_element_type=f32)
        )
        * score_scale
    )
    grad_keys = (
        jnp.einsum("rbhqk,rbqhd->rbkhd", grad_score, query_blocks, preferred_element_type=f32)
        * score_scale
    )
    grad_values = jnp.einsum(
        "rbhqk,rbqhd->rbkhd", to_low(cross_prob), grad_blocks, preferred_element_type=f32
    )
    back_keys, back_values = (
        passed_along(grad_keys[:, 0].astype(jnp.bfloat16), "seq", -1).astype(jnp.float32),
        passed_along(grad_values[:, 0].astype(jnp.bfloat16), "seq", -1).astype(jnp.float32),
    )
    own_keys = grad_keys[:, 1:].at[:, -1].add(back_keys)
    own_values = grad_values[:, 1:].at[:, -1].add(back_values)
    kv_grads = to_low(jnp.stack([own_keys, own_values]).reshape(2, -1, local_width))
    grad_kv = jnp.einsum("nd,kne->kde", neighbour_flat, kv_grads, preferred_element_type=f32)
    grad_cq_low = to_low(grad_cross_query).reshape(token_count, local_width)
    grad_cq = jnp.einsum("td,te->de", normed_two, grad_cq_low, preferred_element_type=f32)
    grad_normed = norm_sum(jnp.dot(grad_cq_low, back_cross[0].T, preferred_element_type=f32))
    from_norm, grad_gain_two = norm_back_two(grad_normed)
    grad_one = grad_two + from_norm
    cross_grads = jnp.stack([grad_cq, grad_kv[0], grad_kv[1], grad_cross_out])
    att_grad_low = to_low(grad_one)
    grad_self_out = jnp.einsum("td,te->de", att_grad_low, attn_low, preferred_element_type=f32)
    grad_attn = to_low(jnp.dot(att_grad_low, back_self[3], preferred_element_type=f32)).reshape(
        head_shape
    )
    saved_pieces = []
    self_dot = jnp.zeros((row_count, heads_here, span_len, 1), f32)
    for piece_index in range(piece_count):
        scores, allowed, keys_piece, values_piece = self_piece(piece_index)
        prob_piece = jnp.where(allowed, jnp.exp(scores - self_lse), 0.0)
        grad_piece = jnp.einsum(
            "rqhd,rkhd->rhqk", grad_attn, values_piece, preferred_element_type=f32
        )
        self_dot = self_dot + jnp.sum(prob_piece * grad_piece, axis=-1, keepdims=True)
        saved_pieces.append((prob_piece, grad_piece, keys_piece))
    grad_query = jnp.zeros(head_shape, f32)
    key_terms = []
    value_terms = []
    for prob_piece, grad_piece, keys_piece in saved_pieces:
        score_grad = to_low(prob_piece * (grad_piece - self_dot))
        grad_query = grad_query + jnp.einsum(
            "rhqk,rkhd->rqhd", score_grad, keys_piece, preferred_element_type=f32
        )
        key_terms.append(
            jnp.einsum("rhqk,rqhd->rkhd", score_grad, query_low, preferred_element_type=f32)
        )
        value_terms.append(
            jnp.einsum("rhqk,rqhd->rkhd", to_low(prob_piece), grad_attn, preferred_element_type=f32)
        )
    own_key_grad, own_value_grad = (
        lax.psum_scatter(
            (jnp.concatenate(key_terms, axis=1) * score_scale).astype(jnp.bfloat16),
            "seq",
            scatter_dimension=1,
            tiled=True,
        ).astype(jnp.float32),
        lax.psum_scatter(
            jnp.concatenate(value_terms, axis=1).astype(jnp.bfloat16),
            "seq",
            scatter_dimension=1,
            tiled=True,
        ).astype(jnp.float32),
    )
    grad_q_low = to_low(rope_back(grad_query * score_scale)[0]).reshape(token_count, local_width)
    grad_k_low = to_low(rope_back(own_key_grad)[0]).reshape(token_count, local_width)
    grad_v_low = to_low(own_value_grad).reshape(token_count, local_width)
    proj_grads = jnp.stack([grad_q_low, grad_k_low, grad_v_low])
    grad_proj = jnp.einsum("td,kte->kde", normed_one, proj_grads, preferred_element_type=f32)
    grad_normed = norm_sum(
        jnp.einsum("kte,kde->td", proj_grads, back_self[:3], preferred_element_type=f32)
    )
    from_norm, grad_gain_one = norm_back_one(grad_normed)
    in_grad = (grad_one + from_norm).reshape(row_count, span_len, model_width)
    self_grads = jnp.concatenate([grad_proj, grad_self_out[None]], axis=0)
    self_part, cross_part, feed_part, gains_part = (
        lax.psum_scatter(self_grads, ("dp", "seq"), scatter_dimension=1, tiled=True),
        lax.psum_scatter(cross_grads, ("dp", "seq"), scatter_dimension=1, tiled=True),
        lax.psum_scatter(feed_grads, ("dp", "seq"), scatter_dimension=1, tiled=True),
        lax.psum_scatter(
            jnp.stack([grad_gain_one, grad_gain_two, grad_gain_three]),
            ("dp", "seq"),
            scatter_dimension=1,
            tiled=True,
        ),
    )
    first_model = (lax.axis_index("mp") == 0).astype(f32)
    local_squares = (
        jnp.sum(self_part * self_part)
        + jnp.sum(cross_part * cross_part)
        + jnp.sum(feed_part * feed_part)
        + first_model * jnp.sum(gains_part * gains_part)
    )
    grad_norm = jnp.sqrt(lax.psum(local_squares, ("dp", "seq", "mp")))
    factor = jnp.minimum(1.0, clip_limit / (grad_norm + 1e-06))
    self_new, self_first_new, self_second_new = adam_step(
        self_weights, self_part, self_first, self_second, factor, learn_rate, weight_decay
    )
    cross_new, cross_first_new, cross_second_new = adam_step(
        cross_weights, cross_part, cross_first, cross_second, factor, learn_rate, weight_decay
    )
    feed_new, feed_first_new, feed_second_new = adam_step(
        feed_weights, feed_part, feed_first, feed_second, factor, learn_rate, weight_decay
    )
    gains_new, gains_first_new, gains_second_new = adam_step(
        norm_gains, gains_part, gains_first, gains_second, factor, gain_rate, 0.0
    )
    return (
        out,
        in_grad,
        grad_norm,
        self_new,
        cross_new,
        feed_new,
        gains_new,
        self_first_new,
        cross_first_new,
        feed_first_new,
        gains_first_new,
        self_second_new,
        cross_second_new,
        feed_second_new,
        gains_second_new,
    )


def solution(mesh):
    in_specs = (
        P("dp", "seq", None),
        P("dp", "seq", None, None, None),
        P("dp", "seq", None),
        P("dp", "seq"),
        P("dp", "seq", None),
        P(None, ("dp", "seq"), "mp"),
        P(None, ("dp", "seq"), "mp"),
        P(None, ("dp", "seq"), "mp"),
        P(None, ("dp", "seq")),
        P(None, ("dp", "seq"), "mp"),
        P(None, ("dp", "seq"), "mp"),
        P(None, ("dp", "seq"), "mp"),
        P(None, ("dp", "seq")),
        P(None, ("dp", "seq"), "mp"),
        P(None, ("dp", "seq"), "mp"),
        P(None, ("dp", "seq"), "mp"),
        P(None, ("dp", "seq")),
    )
    out_specs = (
        P("dp", "seq", None),
        P("dp", "seq", None),
        P(),
        P(None, ("dp", "seq"), "mp"),
        P(None, ("dp", "seq"), "mp"),
        P(None, ("dp", "seq"), "mp"),
        P(None, ("dp", "seq")),
        P(None, ("dp", "seq"), "mp"),
        P(None, ("dp", "seq"), "mp"),
        P(None, ("dp", "seq"), "mp"),
        P(None, ("dp", "seq")),
        P(None, ("dp", "seq"), "mp"),
        P(None, ("dp", "seq"), "mp"),
        P(None, ("dp", "seq"), "mp"),
        P(None, ("dp", "seq")),
    )
    return jax.shard_map(
        per_device, mesh=mesh, in_specs=in_specs, out_specs=out_specs, check_vma=False
    )
```

profile of v0, /device:TPU:0, one launch (start us, length us, event | category | flops | bytes accessed | tf_op | source)
XLA Modules:
  0.0 1338.3 jit_solution(9158452721141465043)
XLA Ops:
  12.6 5.4 collective-permute-start.3
  18.8 2.9 collective-permute-start.1
  21.9 37.3 %all-gather = bf16[16,56,3]{1,2,0:T(4,128)(2,1)S(1)} all-gather(bf16[1,56,3]{1,2,0:T(4,128)(2,1)S(1)} %convert_bitcast_fusion.1), channel_id=1, replica_groups=mesh['dp'=4,'seq'=4,'mp'=2] {'dp','seq'}, dimensions={0}, use_global_device_ids=true | all-gather | bytes 5712 | tf_op jit(solution)/shard_map/all_gather | solution.py:111
  59.4 6.8 all_gather.45
  67.3 19.3 %all-gather.7.cloned.1.call-done = bf16[4,896,512]{2,1,0:T(8,128)(2,1)} async-done(((bf16[4,56,512]{2,1,0:T(8,128)(2,1)}), bf16[4,896,512]{2,1,0:T(8,128)(2,1)}) %all-gather.7.cloned.1.call-update) | async-done | bytes 3670032 | tf_op jit(solution)/shard_map/all_gather | solution.py:108
  86.5 2.9 fusion.24
  100.4 60.1 %all-gather.13.cloned.1.call-done = bf16[4,896,512]{2,0,1:T(4,128)(2,1)} async-done(((bf16[4,56,512]{2,0,1:T(4,128)(2,1)}), bf16[4,896,512]{2,0,1:T(4,128)(2,1)}) %all-gather.13.cloned.1.call-update) | async-done | bytes 3670032 | tf_op jit(solution)/shard_map/all_gather | solution.py:109
  160.5 4.1 slice.307
  164.6 3.7 convert_bitcast_fusion
  168.4 4.5 reshape.1407
  173.3 14.7 %all-gather.11.cloned.1.call-done = bf16[1,1024,8,64]{1,3,2,0:T(8,128)(2,1)} async-done(((bf16[1,256,8,64]{1,3,2,0:T(8,128)(2,1)}), bf16[1,1024,8,64]{1,3,2,0:T(8,128)(2,1)}) %all-gather.11.cloned.1.call-update) | async-done | bytes 1048592 | tf_op jit(solution)/shard_map/all_gather | solution.py:129
  193.8 23.0 %all-gather.9.cloned.1.call-done = bf16[1,1024,8,64]{1,3,2,0:T(8,128)(2,1)} async-done(((bf16[1,256,8,64]{1,3,2,0:T(8,128)(2,1)}), bf16[1,1024,8,64]{1,3,2,0:T(8,128)(2,1)}) %all-gather.9.cloned.1.call-update) | async-done | bytes 1048592 | tf_op jit(solution)/shard_map/all_gather | solution.py:130
  223.7 2.5 fusion.57
  226.3 3.1 fusion.130
  229.4 2.7 squeeze.45
  232.1 2.5 copy.329
  236.5 4.1 collective-permute-start
  240.6 2.6 squeeze.50
  243.2 2.4 copy.335
  246.4 3.2 collective-permute-start.2
  249.6 8.2 fusion.128
  257.8 2.8 all_gather.47
  269.8 2.6 fusion.33
  276.0 2.8 fusion.69
  279.8 6.7 reduce-scatter.13.cloned.1.call-done
  286.5 2.8 all_gather.49
  291.9 94.6 %all-gather.15.cloned.1.call-done = bf16[2,896,1792]{2,1,0:T(8,128)(2,1)} async-done(((bf16[2,56,1792]{2,1,0:T(8,128)(2,1)}), bf16[2,896,1792]{2,1,0:T(8,128)(2,1)}) %all-gather.15.cloned.1.call-update) | async-done | bytes 6422544 | tf_op jit(solution)/shard_map/all_gather | solution.py:110
  386.5 3.3 fusion.1
  389.8 4.5 fusion.22
  397.3 4.5 fusion.3
  404.1 2.7 all_gather.52
  410.6 5.5 reduce-scatter.15.cloned.1.call-done
  416.1 2.7 all_gather.51
  418.7 2.5 fusion.49
  433.9 3.7 multiply_reduce_fusion
  441.2 2.8 copy.345
  450.4 2.8 fusion.70
  453.3 2.6 convolution_bitcast_fusion.3
  462.9 2.8 all_gather.53
  483.8 4.3 multiply_reduce_fusion.3
  488.1 2.5 multiply_convert_fusion.4
  498.0 3.0 convolution_bitcast_fusion.5
  501.1 2.7 slice_bitcast_fusion.7
  506.7 2.6 stack.52
  516.0 26.6 %reduce-scatter.21.cloned.1.call-done = bf16[1,256,8,64]{1,3,2,0:T(8,128)(2,1)} async-done(((bf16[1,1024,8,64]{1,3,2,0:T(8,128)(2,1)}), bf16[1,256,8,64]{1,3,2,0:T(8,128)(2,1)}) %reduce-scatter.21.cloned.1.call-update) | async-done | bytes 262160 | tf_op jit(solution)/shard_map/reduce_scatter | solution.py:333
  550.8 3.8 fusion.30
  556.6 3.1 copy.368
  559.7 2.6 stack.49
  562.3 4.1 fusion.13
  566.4 3.2 pad_maximum_fusion.2
  569.6 9.8 copy.373
  582.4 3.4 pad_maximum_fusion.1
  585.8 9.8 copy.366
  596.3 5.1 convolution_bitcast_fusion.1
  601.4 3.8 convolution_bitcast_fusion
  605.2 10.2 pad_maximum_fusion
  619.4 2.7 all_gather.54
  623.4 80.5 %all-reduce.6 = f32[3,896]{1,0:T(4,128)S(1)} all-reduce(f32[3,896]{1,0:T(4,128)S(1)} %pad_maximum_fusion.9), channel_id=13, replica_groups=mesh['dp'=4,'seq'=4,'mp'=2] {'dp','seq'}, use_global_device_ids=true, to_apply=%region_38.39.clone | all-reduce | flops 2688 | bytes 21504
  707.6 298.5 %all-reduce.10.cloned.1.call-done = (f32[4,896,512]{2,0,1:T(4,128)}, f32[4,896,512]{2,0,1:T(4,128)}) async-done(((f32[4,896,512]{2,0,1:T(4,128)}, f32[4,896,512]{2,0,1:T(4,128)}), (f32[4,896,512]{2,0,1:T(4,128)}, f32[4,896,512]{2,0,1:T(4,128)})) %all-reduce.10.cloned.1.call-update) | async-done | bytes 14680080
  1006.1 2.6 multiply_reduce_fusion.13
  1008.7 2.6 multiply_reduce_fusion.12
  1012.6 262.0 %reduce-scatter.27.cloned.1.call-done = f32[2,56,1792]{2,1,0:T(8,128)} async-done(((f32[2,896,1792]{2,1,0:T(8,128)}), f32[2,56,1792]{2,1,0:T(8,128)}) %reduce-scatter.27.cloned.1.call-update) | async-done | bytes 802832 | tf_op jit(solution)/shard_map/reduce_scatter | solution.py:360
  1278.4 43.7 %psum.7 = f32[]{:T(128)} all-reduce(f32[]{:T(128)S(6)} %add.360), channel_id=1, replica_groups=mesh['dp'=4,'seq'=4,'mp'=2] {'dp','seq','mp'}, use_global_device_ids=true, to_apply=%region_40.41 | all-reduce | flops 1 | bytes 8 | tf_op jit(solution)/shard_map/psum | solution.py:375
  1323.6 2.7 multiply_subtract_fusion.2
  (429 shorter events, 153.0 us)
Async XLA Ops:
  7.2 157.4 %copy-start = (bf16[1,4,2,128,896]{4,3,2,1,0:T(8,128)(2,1)S(1)}, bf16[1,4,2,128,896]{4,3,2,1,0:T(8,128)(2,1)}, u32[]{:S(2)}) copy-start(bf16[1,4,2,128,896]{4,3,2,1,0:T(8,128)(2,1)} %param.22) | copy-start | bytes 5505028
  7.2 59.0 %copy-start.116 = (s32[1,256]{1,0:T(1,128)S(1)}, s32[1,256]{1,0:T(1,128)}, u32[]{:S(2)}) copy-start(s32[1,256]{1,0:T(1,128)} %param.24) | copy-start | bytes 3076
  7.2 14.5 %copy-start.83 = (bf16[1,256,896]{2,1,0:T(8,128)(2,1)S(1)}, bf16[1,256,896]{2,1,0:T(8,128)(2,1)}, u32[]{:S(2)}) copy-start(bf16[1,256,896]{2,1,0:T(8,128)(2,1)} %param.21) | copy-start | bytes 1376260
  7.2 14.7 %copy-start.111 = (f32[3,56]{1,0:T(4,128)S(1)}, f32[3,56]{1,0:T(4,128)}, u32[]{:S(2)}) copy-start(f32[3,56]{1,0:T(4,128)} %param.29) | copy-start | bytes 2020
  7.2 79.3 %all-gather.7.cloned.1.call-start = ((), (), s32[]{:S(2)}) async-start(), calls=%async_computation.9 | async-start | bytes 3899392 | tf_op jit(solution)/shard_map/all_gather | solution.py:108
  9.2 151.3 %all-gather.13.cloned.1.call-start = ((), (), s32[]{:S(2)}) async-start(), calls=%async_computation.13 | async-start | bytes 3899392 | tf_op jit(solution)/shard_map/all_gather | solution.py:109
  11.3 176.7 %all-gather.11.cloned.1.call-start = ((), (), s32[]{:S(2)}) async-start(), calls=%async_computation.11 | async-start | bytes 1310720 | tf_op jit(solution)/shard_map/all_gather | solution.py:129
  12.6 84.2 %collective-permute-start.3 = (bf16[1]{0:T(256)(128)(2,1)}, bf16[1]{0:T(256)(128)(2,1)}, u32[]{:S(2)}, u32[]{:S(2)}) collective-permute-start(bf16[1]{0:T(256)(128)(2,1)} %bitcast.40), channel_id=1, source_target_pairs={{0,2},{2,4},{4,6},{1,3},{3,5},{5,7},{8,10},{10,12},{12,14},{9,11},... | collective-permute-start | bytes 14 | tf_op jit(solution)/shard_map/ppermute | solution.py:30
  18.8 79.7 %collective-permute-start.1 = (bf16[1,256]{1,0:T(2,128)(2,1)S(1)}, bf16[1,256]{1,0:T(2,128)(2,1)S(1)}, u32[]{:S(2)}, u32[]{:S(2)}) collective-permute-start(bf16[1,256]{1,0:T(2,128)(2,1)S(1)} %fusion.97), channel_id=1, source_target_pairs={{0,2},{2,4},{4,6},{1,3},{3,5},{5,7},{8,10},{10,12},{12,14},{9,11},... | collective-permute-start | bytes 1544 | tf_op jit(solution)/shard_map/ppermute | solution.py:30
  66.3 23.1 %copy-start.92 = (f32[896]{0:T(1024)}, f32[896]{0:T(1024)S(1)}, u32[]{:S(2)}) copy-start(f32[896]{0:T(1024)S(1)} %get-tuple-element.122) | copy-start | bytes 10756
  66.3 194.5 %copy-start.94 = (f32[896]{0:T(1024)}, f32[896]{0:T(1024)S(1)}, u32[]{:S(2)}) copy-start(f32[896]{0:T(1024)S(1)} %get-tuple-element.121) | copy-start | bytes 10756
  67.1 22.4 %copy-start.100 = (f32[256]{0:T(256)}, f32[256]{0:T(256)S(1)}, u32[]{:S(2)}) copy-start(f32[256]{0:T(256)S(1)} %fusion.98) | copy-start | bytes 3076
  67.3 26.9 %copy-start.88 = (f32[256,32]{0,1:T(8,128)}, f32[256,32]{0,1:T(8,128)S(1)}, u32[]{:S(2)}) copy-start(f32[256,32]{0,1:T(8,128)S(1)} %get-tuple-element.189) | copy-start | bytes 98308
  67.3 26.9 %copy-start.90 = (f32[256,32]{0,1:T(8,128)}, f32[256,32]{0,1:T(8,128)S(1)}, u32[]{:S(2)}) copy-start(f32[256,32]{0,1:T(8,128)S(1)} %get-tuple-element.190) | copy-start | bytes 98308
  95.4 95.3 %copy-start.48 = (bf16[256,8,32]{0,2,1:T(8,128)(2,1)}, bf16[256,8,32]{0,2,1:T(8,128)(2,1)S(1)}, u32[]{:S(2)}) copy-start(bf16[256,8,32]{0,2,1:T(8,128)(2,1)S(1)} %get-tuple-element.170) | copy-start | bytes 393220
  95.4 95.2 %copy-start.50 = (bf16[256,8,32]{0,2,1:T(8,128)(2,1)}, bf16[256,8,32]{0,2,1:T(8,128)(2,1)S(1)}, u32[]{:S(2)}) copy-start(bf16[256,8,32]{0,2,1:T(8,128)(2,1)S(1)} %get-tuple-element.171) | copy-start | bytes 393220
  96.2 120.6 %all-gather.9.cloned.1.call-start = ((), (), s32[]{:S(2)}) async-start(), calls=%async_computation.10 | async-start | bytes 1310720 | tf_op jit(solution)/shard_map/all_gather | solution.py:130
  96.4 166.2 %copy-start.97 = (bf16[320]{0:T(512)(128)(2,1)}, bf16[320]{0:T(512)(128)(2,1)S(1)}, u32[]{:S(2)}) copy-start(bf16[320]{0:T(512)(128)(2,1)S(1)} %pad.53.clone) | copy-start | bytes 1924
  96.4 166.2 %copy-start.106 = (bf16[320]{0:T(512)(128)(2,1)}, bf16[320]{0:T(512)(128)(2,1)S(1)}, u32[]{:S(2)}) copy-start(bf16[320]{0:T(512)(128)(2,1)S(1)} %pad.51.clone) | copy-start | bytes 1924
  96.8 120.0 %copy-start.68 = (pred[256,256]{0,1:T(8,128)(4,1)}, pred[256,256]{0,1:T(8,128)(4,1)S(1)}, u32[]{:S(2)}) copy-start(pred[256,256]{0,1:T(8,128)(4,1)S(1)} %get-tuple-element.185) | copy-start | bytes 196612
  96.8 122.3 %copy-start.64 = (pred[256,256]{0,1:T(8,128)(4,1)}, pred[256,256]{0,1:T(8,128)(4,1)S(1)}, u32[]{:S(2)}) copy-start(pred[256,256]{0,1:T(8,128)(4,1)S(1)} %get-tuple-element.188) | copy-start | bytes 196612
  96.8 124.7 %copy-start.71 = (pred[256,256]{0,1:T(8,128)(4,1)}, pred[256,256]{0,1:T(8,128)(4,1)S(1)}, u32[]{:S(2)}) copy-start(pred[256,256]{0,1:T(8,128)(4,1)S(1)} %get-tuple-element.187) | copy-start | bytes 196612
  172.9 84.9 %reduce-scatter.11.cloned.1.call-start = ((), (), s32[]{:S(2)}) async-start(), calls=%async_computation.12 | async-start | bytes 1376256 | tf_op jit(solution)/shard_map/reduce_scatter | solution.py:57
  226.3 60.3 %reduce-scatter.13.cloned.1.call-start = ((), (), s32[]{:S(2)}) async-start(), calls=%async_computation.14 | async-start | bytes 1376256 | tf_op jit(solution)/shard_map/reduce_scatter | solution.py:57
  236.5 32.3 %collective-permute-start = (bf16[1,256,8,64]{1,3,2,0:T(8,128)(2,1)}, bf16[1,256,8,64]{1,3,2,0:T(8,128)(2,1)}, u32[]{:S(2)}, u32[]{:S(2)}) collective-permute-start(bf16[1,256,8,64]{1,3,2,0:T(8,128)(2,1)} %bitcast.308), channel_id=1, source_target_pairs={{0,2},{2,4},{4,6},{1,3},{3,5},{5,7},{8,10},{10,12},{12,14},{9,11},... | collective-permute-start | bytes 786440 | tf_op jit(solution)/shard_map/ppermute | solution.py:30
  246.4 19.1 %collective-permute-start.2 = (bf16[1,256,8,64]{1,3,2,0:T(8,128)(2,1)}, bf16[1,256,8,64]{1,3,2,0:T(8,128)(2,1)S(1)}, u32[]{:S(2)}, u32[]{:S(2)}) collective-permute-start(bf16[1,256,8,64]{1,3,2,0:T(8,128)(2,1)} %bitcast.307), channel_id=1, source_target_pairs={{0,2},{2,4},{4,6},{1,3},{3,5},{5,7},{8,10},{10,12},{12,14},{9,11},... | collective-permute-start | bytes 786440 | tf_op jit(solution)/shard_map/ppermute | solution.py:30
  274.6 4.3 copy-start.52
  278.9 107.6 %all-gather.15.cloned.1.call-start = ((), (), s32[]{:S(2)}) async-start(), calls=%async_computation.15 | async-start | bytes 6823936 | tf_op jit(solution)/shard_map/all_gather | solution.py:110
  279.8 124.3 %reduce-scatter.17.cloned.1.call-start = ((), (), s32[]{:S(2)}) async-start(), calls=%async_computation.17 | async-start | bytes 1376256 | tf_op jit(solution)/shard_map/reduce_scatter | solution.py:62
  386.5 8.8 slice-start
  389.8 4.5 copy-start.40
  389.8 5.4 slice-start.1
  397.3 18.8 %reduce-scatter.15.cloned.1.call-start = ((), (), s32[]{:S(2)}) async-start(), calls=%async_computation.16 | async-start | bytes 1376256 | tf_op jit(solution)/shard_map/reduce_scatter | solution.py:57
  401.9 61.0 %reduce-scatter.19.cloned.1.call-start = ((), (), s32[]{:S(2)}) async-start(), calls=%async_computation.18 | async-start | bytes 1376256 | tf_op jit(solution)/shard_map/reduce_scatter | solution.py:62
  453.2 61.0 %reduce-scatter.23.cloned.1.call-start = ((), (), s32[]{:S(2)}) async-start(), calls=%async_computation.20 | async-start | bytes 1310720 | tf_op jit(solution)/shard_map/reduce_scatter | solution.py:339
  453.3 5.2 copy-start.20
  456.7 47.2 %collective-permute-start.5 = (bf16[1,256,8,64]{1,3,2,0:T(8,128)(2,1)}, bf16[1,256,8,64]{1,3,2,0:T(8,128)(2,1)}, u32[]{:S(2)}, u32[]{:S(2)}) collective-permute-start(bf16[1,256,8,64]{1,3,2,0:T(8,128)(2,1)} %fusion.72), channel_id=1, source_target_pairs={{2,0},{4,2},{6,4},{3,1},{5,3},{7,5},{10,8},{12,10},{14,12},{11,9},... | collective-permute-start | bytes 786440 | tf_op jit(solution)/shard_map/ppermute | solution.py:30
  460.2 5.5 copy-start.95
  460.2 5.5 copy-start.103
  462.1 5.8 copy-start.110
  462.9 5.0 copy-start.12
  462.9 5.0 copy-start.21
  479.7 62.9 %reduce-scatter.21.cloned.1.call-start = ((), (), s32[]{:S(2)}) async-start(), calls=%async_computation.19 | async-start | bytes 1310720 | tf_op jit(solution)/shard_map/reduce_scatter | solution.py:333
  483.8 4.3 copy-start.18
  493.0 4.9 copy-start.60
  493.0 4.9 copy-start.104
  494.3 125.1 %reduce-scatter.25.cloned.1.call-start = ((), (), s32[]{:S(2)}) async-start(), calls=%async_computation.21 | async-start | bytes 1376256 | tf_op jit(solution)/shard_map/reduce_scatter | solution.py:62
  494.3 6.6 copy-start.36
  496.2 58.4 %collective-permute-start.4 = (bf16[1,256,8,64]{1,3,2,0:T(8,128)(2,1)}, bf16[1,256,8,64]{1,3,2,0:T(8,128)(2,1)}, u32[]{:S(2)}, u32[]{:S(2)}) collective-permute-start(bf16[1,256,8,64]{1,3,2,0:T(8,128)(2,1)} %fusion.71), channel_id=1, source_target_pairs={{2,0},{4,2},{6,4},{3,1},{5,3},{7,5},{10,8},{12,10},{14,12},{11,9},... | collective-permute-start | bytes 786440 | tf_op jit(solution)/shard_map/ppermute | solution.py:30
  513.1 30.5 %copy-start.89 = (f32[256,32]{0,1:T(8,128)S(1)}, f32[256,32]{0,1:T(8,128)}, u32[]{:S(2)}) copy-start(f32[256,32]{0,1:T(8,128)} %copy-done.88) | copy-start | bytes 98308
  513.1 30.5 %copy-start.91 = (f32[256,32]{0,1:T(8,128)S(1)}, f32[256,32]{0,1:T(8,128)}, u32[]{:S(2)}) copy-start(f32[256,32]{0,1:T(8,128)} %copy-done.90) | copy-start | bytes 98308
  554.6 451.5 %all-reduce.10.cloned.1.call-start = ((), (), s32[]{:S(2)}) async-start(), calls=%async_computation.23 | async-start | bytes 29360128
  595.7 678.9 %reduce-scatter.27.cloned.1.call-start = ((), (), s32[]{:S(2)}) async-start(), calls=%async_computation.22 | async-start | bytes 13647872 | tf_op jit(solution)/shard_map/reduce_scatter | solution.py:360
  596.3 5.1 copy-start.41
  596.3 5.1 copy-start.56
  615.4 89.8 %copy-start.108 = (f32[256]{0:T(256)S(1)}, f32[256]{0:T(256)}, u32[]{:S(2)}) copy-start(f32[256]{0:T(256)} %copy-done.107) | copy-start | bytes 3076
  615.4 89.8 %copy-start.23 = (f32[256,896]{0,1:T(8,128)S(1)}, f32[256,896]{0,1:T(8,128)}, u32[]{:S(2)}) copy-start(f32[256,896]{0,1:T(8,128)} %copy-done.22) | copy-start | bytes 2752516
  707.6 569.6 %copy-start.47 = (f32[1,256,896]{1,2,0:T(8,128)S(1)}, f32[1,256,896]{1,2,0:T(8,128)}, u32[]{:S(2)}) copy-start(f32[1,256,896]{1,2,0:T(8,128)} %fusion.52) | copy-start | bytes 2752516
  1006.1 316.7 %copy-start.112 = (f32[3,56]{1,0:T(4,128)S(1)}, f32[3,56]{1,0:T(4,128)}, u32[]{:S(2)}) copy-start(f32[3,56]{1,0:T(4,128)} %param.29) | copy-start | bytes 2020
  1006.1 316.7 %copy-start.114 = (f32[3,56]{1,0:T(4,128)S(1)}, f32[3,56]{1,0:T(4,128)}, u32[]{:S(2)}) copy-start(f32[3,56]{1,0:T(4,128)} %param.33) | copy-start | bytes 2020
  1006.1 316.7 %copy-start.115 = (f32[3,56]{1,0:T(4,128)S(1)}, f32[3,56]{1,0:T(4,128)}, u32[]{:S(2)}) copy-start(f32[3,56]{1,0:T(4,128)} %param.37) | copy-start | bytes 2020
  1006.1 317.5 %copy-start.61 = (f32[4,56,512]{2,1,0:T(8,128)S(1)}, f32[4,56,512]{2,1,0:T(8,128)}, u32[]{:S(2)}) copy-start(f32[4,56,512]{2,1,0:T(8,128)} %param.26) | copy-start | bytes 1376260
  1278.4 47.9 %copy-start.62 = (f32[4,56,512]{2,1,0:T(8,128)S(1)}, f32[4,56,512]{2,1,0:T(8,128)}, u32[]{:S(2)}) copy-start(f32[4,56,512]{2,1,0:T(8,128)} %param.27) | copy-start | bytes 1376260
  1278.4 47.9 %copy-start.63 = (f32[4,56,512]{2,0,1:T(4,128)S(1)}, f32[4,56,512]{2,0,1:T(4,128)}, u32[]{:S(2)}) copy-start(f32[4,56,512]{2,0,1:T(4,128)} %get-tuple-element.146) | copy-start | bytes 1376260
  (77 other events, 167.7 us)
Sparse Core Ops, SparseCore 0:
  11.4 75.0 all-gather.6
  89.9 70.6 all-gather.12
  162.9 25.0 all-gather.10
  190.2 26.4 all-gather.8
  226.4 8.4 reduce-scatter.10
  279.0 7.4 reduce-scatter.12
  289.8 96.6 all-gather.14
  397.4 6.6 reduce-scatter.16
  406.5 9.5 reduce-scatter.14
  453.3 9.5 reduce-scatter.18
  479.8 30.9 reduce-scatter.22
  513.6 29.0 reduce-scatter.20
  554.8 8.3 reduce-scatter.24
  595.8 410.3 all-reduce.9
  1008.3 266.2 reduce-scatter.26
where the time goes:
time: 1350 us; the launch traced here: 1340 us
  waiting for transfers between devices  812 us (60%)
  blocking collectives  185 us (14%)
  local copies, waits for them, and re-layouts  129 us (10%)
  matrix products  97.6 us (7%)
  other arithmetic  73.7 us (5%)
  between operations  20.9 us (2%)
  starting transfers between devices  20.1 us (1%)
    unnamed x16, waiting for transfers between devices  299 us
    reduce_scatter x1, waiting for transfers between devices, per_device(): lax.psum_scatter(feed_grads, ('dp', 'seq'), scatter_dimension=1, tiled=True)  262 us
    all_gather x1, waiting for transfers between devices, per_device(): lax.all_gather(to_low(feed_weights), ('dp', 'seq'), axis=1, tiled=True)  94.6 us
    unnamed x1, blocking collectives  80.5 us
    all_gather x1, waiting for transfers between devices, per_device(): lax.all_gather(to_low(cross_weights), ('dp', 'seq'), axis=1, tiled=True)  60.1 us
    psum x1, blocking collectives, per_device(): grad_norm = jnp.sqrt(lax.psum(local_squares, ('dp', 'seq', 'mp')))  43.7 us
    all_gather x1, blocking collectives, per_device(): lax.all_gather(to_low(norm_gains), ('dp', 'seq'), axis=1, tiled=True)  37.3 us
    unnamed x251, local copies, waits for them, and re-layouts  30.9 us
  transfers between devices with their start and end apart: 21, of which 12 were waited for; matrix products, arithmetic and copies ran while one was open for 16% of the time, Pallas kernels for 0%

commit v1 on v0

v1 whole, which is shorter than its diff:
```python
from functools import partial

import jax
import jax.numpy as jnp
from jax import lax
from jax.sharding import PartitionSpec as P

HEAD_DIM = 64
BLOCK = 64
NEIGHBOURS = 2
NEIGH_LEN = 128
STEP = 10
DOC_MAX = 512

norm_eps = 1e-05
rope_base = 10000.0
beta_one = 0.9
beta_two = 0.95
adam_eps = 1e-08
weight_decay = 0.1
learn_rate = 0.1
gain_rate = 0.5
clip_limit = 1.0
masked_fill = -1e30

f32 = jnp.float32
bf16 = jnp.bfloat16


def to_low(array_in):
    return array_in.astype(bf16)


def shifted(value, axis, by):
    count = lax.axis_size(axis)
    return lax.ppermute(value, axis, [(i, i + by) for i in range(count) if 0 <= i + by < count])


def rotated(value, axis, by):
    count = lax.axis_size(axis)
    return lax.ppermute(value, axis, [(i, (i + by) % count) for i in range(count)])


def swapped(value, axis, by):
    count = lax.axis_size(axis)
    return lax.ppermute(value, axis, [(i, i ^ by) for i in range(count)])


def butterfly(value, axes):
    for axis in axes:
        step = 1
        while step < lax.axis_size(axis):
            value = value + swapped(value, axis, step)
            step *= 2
    return value


def core_sum(partial_out):
    return partial_out + swapped(partial_out, "mp", 1)


def small_mesh():
    return lax.axis_size("dp") == 4 and lax.axis_size("seq") == 4


def put(buffer, piece, starts):
    return lax.dynamic_update_slice(buffer, piece, starts)


def gather_rows(block):
    if not small_mesh():
        return lax.all_gather(block, ("dp", "seq"), axis=0, tiled=True)
    rows, cols = block.shape
    half = cols // 256 * 128
    z = lax.axis_index("dp")
    s = lax.axis_index("seq")
    pieces = [block] + [rotated(block, "dp", k) for k in (1, 2, 3)]
    column = jnp.zeros((4, rows, cols), block.dtype)
    for k, piece in enumerate(pieces):
        column = put(column, piece[None], ((z - k) % 4, 0, 0))
    from_x = swapped(column, "seq", 1)
    from_y = swapped(column, "seq", 2)
    diag_a = swapped(from_y[..., :half], "seq", 1)
    diag_b = swapped(from_x[..., half:], "seq", 2)
    out = jnp.zeros((4, 4, rows, cols), block.dtype)
    out = put(out, column[:, None], (0, s, 0, 0))
    out = put(out, from_x[:, None], (0, s ^ 1, 0, 0))
    out = put(out, from_y[:, None], (0, s ^ 2, 0, 0))
    out = put(out, diag_a[:, None], (0, s ^ 3, 0, 0))
    out = put(out, diag_b[:, None], (0, s ^ 3, 0, half))
    return out.reshape(16 * rows, cols)


def take(array_in, index, axis):
    return lax.dynamic_index_in_dim(array_in, index, axis, keepdims=False)


def scatter_rows(grads):
    low = to_low(grads)
    if not small_mesh():
        return lax.psum_scatter(low, ("dp", "seq"), scatter_dimension=0, tiled=True).astype(f32)
    rows, cols = low.shape[0] // 16, low.shape[1]
    half = cols // 256 * 128
    z = lax.axis_index("dp")
    s = lax.axis_index("seq")
    x, y = s % 2, s // 2
    view = low.reshape(4, 2, 2, rows, cols)
    left, right = view[..., :half], view[..., half:]
    got_a = swapped(take(left, 1 - x, 2), "seq", 1)
    got_b = swapped(take(right, 1 - y, 1), "seq", 2)
    sum_a = take(left, x, 2).astype(f32) + got_a.astype(f32)
    sum_b = take(right, y, 1).astype(f32) + got_b.astype(f32)
    got_a = swapped(to_low(take(sum_a, 1 - y, 1)), "seq", 2)
    got_b = swapped(to_low(take(sum_b, 1 - x, 1)), "seq", 1)
    sum_a = take(sum_a, y, 1) + got_a.astype(f32)
    sum_b = take(sum_b, x, 1) + got_b.astype(f32)
    column = jnp.concatenate([sum_a, sum_b], axis=-1)
    column_low = to_low(column)
    total = take(column, z, 0)
    for k in (1, 2, 3):
        total = total + rotated(take(column_low, (z + k) % 4, 0), "dp", k).astype(f32)
    return total


def rms_apply(inputs, gain_row):
    factor = lax.rsqrt(jnp.mean(inputs * inputs, axis=-1, keepdims=True) + norm_eps)
    return inputs * factor * gain_row


def rope_apply(field_in, positions):
    half_dim = field_in.shape[-1] // 2
    frequency = rope_base ** (-jnp.arange(half_dim, dtype=f32) / half_dim)
    angles = positions[:, None] * frequency[None, :]
    cosine = jnp.cos(angles)[:, None, :]
    sine_part = jnp.sin(angles)[:, None, :]
    lead_half = field_in[..., :half_dim]
    tail_half = field_in[..., half_dim:]
    return jnp.concatenate(
        [lead_half * cosine - tail_half * sine_part, lead_half * sine_part + tail_half * cosine],
        axis=-1,
    )


def adam_step(weight, gradient, first_old, second_old, factor, step_rate, decay_coef):
    clipped = gradient * factor
    first_new = beta_one * first_old + (1.0 - beta_one) * clipped
    second_new = beta_two * second_old + (1.0 - beta_two) * clipped * clipped
    first_hat = first_new / (1.0 - beta_one**STEP)
    second_hat = second_new / (1.0 - beta_two**STEP)
    weight_new = weight - step_rate * (
        first_hat / (jnp.sqrt(second_hat) + adam_eps) + decay_coef * weight
    )
    return (weight_new, first_new, second_new)


def per_device(
    tokens,
    neighbours,
    neighbour_lengths,
    segment_ids,
    out_grad,
    self_weights,
    cross_weights,
    feed_weights,
    norm_gains,
    self_first,
    cross_first,
    feed_first,
    gains_first,
    self_second,
    cross_second,
    feed_second,
    gains_second,
):
    row_count, span_len, model_width = tokens.shape
    local_width = self_weights.shape[2]
    hidden_width = feed_weights.shape[2]
    shard_rows = self_weights.shape[1]
    heads = local_width // HEAD_DIM
    score_scale = HEAD_DIM ** (-0.5)
    blocks_here = span_len // BLOCK
    key_count = NEIGHBOURS * NEIGH_LEN
    halo = min(-(-(DOC_MAX - 1) // span_len), lax.axis_size("seq") - 1)
    s_index = lax.axis_index("seq")

    def columns(*parts):
        return jnp.concatenate([to_low(p) for p in parts], axis=1)

    gain_cols = jnp.zeros((shard_rows, 128), f32).at[:, :3].set(norm_gains.T)
    full_qkv = gather_rows(columns(self_weights[0], self_weights[1], self_weights[2], gain_cols))
    full_kv2 = gather_rows(columns(cross_weights[1], cross_weights[2]))
    full_att = gather_rows(columns(self_weights[3], cross_weights[0], cross_weights[3]))
    full_up = gather_rows(to_low(feed_weights[0]))
    full_down = gather_rows(to_low(feed_weights[1]))
    w_qkv = full_qkv[:, : 3 * local_width]
    gain_values = full_qkv[:, 3 * local_width : 3 * local_width + 3].T.astype(f32)
    w_so = full_att[:, :local_width]
    w_cq = full_att[:, local_width : 2 * local_width]
    w_co = full_att[:, 2 * local_width :]

    def mm(a, b):
        return jnp.dot(a, b, preferred_element_type=f32)

    def mm_t(a, b):
        return lax.dot_general(a, b, (((1,), (1,)), ((), ())), preferred_element_type=f32)

    def t_mm(a, b):
        return lax.dot_general(a, b, (((0,), (0,)), ((), ())), preferred_element_type=f32)

    inputs = tokens.astype(f32).reshape(span_len, model_width)
    query_pos = s_index * span_len + jnp.arange(span_len, dtype=jnp.int32)
    angle_pos = query_pos.astype(f32)
    normed_one, norm_back_one = jax.vjp(rms_apply, inputs, gain_values[0])
    normed_one = to_low(normed_one)
    projected = mm(normed_one, w_qkv)
    head_shape = (span_len, heads, HEAD_DIM)
    query_raw = projected[:, :local_width].reshape(head_shape)
    query_rot, rope_back = jax.vjp(lambda field_in: rope_apply(field_in, angle_pos), query_raw)
    key_rot = rope_apply(projected[:, local_width : 2 * local_width].reshape(head_shape), angle_pos)
    query_low = to_low(query_rot)
    key_low = to_low(key_rot).reshape(span_len, local_width)
    value_low = to_low(projected[:, 2 * local_width :])
    kv_low = jnp.concatenate([key_low, value_low], axis=1)
    seg_here = segment_ids.reshape(1, span_len) + 1
    kv_pieces = [kv_low] + [shifted(kv_low, "seq", k) for k in range(1, halo + 1)]
    seg_pieces = [seg_here] + [shifted(seg_here, "seq", k) for k in range(1, halo + 1)]
    kv_all = jnp.concatenate(kv_pieces, axis=0)
    seg_all = jnp.concatenate(seg_pieces, axis=1)
    keys_all = kv_all[:, :local_width].reshape(-1, heads, HEAD_DIM)
    values_all = kv_all[:, local_width:].reshape(-1, heads, HEAD_DIM)
    offsets = jnp.concatenate(
        [jnp.arange(span_len, dtype=jnp.int32) - k * span_len for k in range(halo + 1)]
    )
    allowed = jnp.logical_and(
        offsets[None, :] <= jnp.arange(span_len, dtype=jnp.int32)[:, None],
        seg_all == seg_here.reshape(span_len, 1),
    )[None]

    def self_scores():
        return jnp.einsum("qhd,khd->hqk", query_low, keys_all, preferred_element_type=f32) * score_scale

    scores = jnp.where(allowed, self_scores(), masked_fill)
    row_max = jnp.max(scores, axis=-1, keepdims=True)
    row_total = jnp.sum(jnp.exp(scores - row_max), axis=-1, keepdims=True)
    self_lse = row_max + jnp.log(row_total)
    self_prob = jnp.where(allowed, jnp.exp(scores - self_lse), 0.0)
    attn_low = to_low(
        jnp.einsum("hqk,khd->qhd", to_low(self_prob), values_all, preferred_element_type=f32)
    ).reshape(span_len, local_width)
    hidden_one = inputs + core_sum(mm_t(attn_low, w_so))
    normed_two, norm_back_two = jax.vjp(rms_apply, hidden_one, gain_values[1])
    normed_two = to_low(normed_two)
    cross_query = to_low(mm(normed_two, w_cq)).reshape(head_shape)
    flat = neighbours.reshape(-1, model_width)
    edge = shifted(flat[-key_count:], "seq", 1)
    flat_all = jnp.concatenate([edge, flat], axis=0)
    kv2 = to_low(mm(flat_all, full_kv2))
    block_keys = kv2[:, :local_width].reshape(blocks_here + 1, key_count, heads, HEAD_DIM)
    block_values = kv2[:, local_width:].reshape(blocks_here + 1, key_count, heads, HEAD_DIM)
    lengths = neighbour_lengths.reshape(blocks_here, NEIGHBOURS)
    prev_info = shifted(jnp.concatenate([lengths[-1], seg_here[0, -1:]]), "seq", 1)
    lengths_all = jnp.concatenate([prev_info[None, :NEIGHBOURS], lengths], axis=0)
    key_valid = jnp.arange(NEIGH_LEN, dtype=jnp.int32)[None, None, :] < lengths_all[:, :, None]
    allowed_cross = key_valid.reshape(blocks_here + 1, 1, 1, key_count)
    seg_pad = jnp.concatenate(
        [prev_info[NEIGHBOURS:], seg_here[0], jnp.zeros((BLOCK - 1,), jnp.int32)]
    ).reshape(blocks_here + 1, BLOCK)
    keep_mask = seg_pad == seg_pad[:, :1]
    keep_float = keep_mask.astype(f32)[:, :, None, None]
    keep_low = keep_mask.astype(bf16)[:, :, None, None]

    def to_blocks(field_in):
        padded = jnp.pad(field_in, ((1, BLOCK - 1), (0, 0), (0, 0)))
        return padded.reshape(blocks_here + 1, BLOCK, heads, HEAD_DIM)

    def from_blocks(blocks_in):
        return blocks_in.reshape((blocks_here + 1) * BLOCK, heads, HEAD_DIM)[1 : span_len + 1]

    query_blocks = to_blocks(cross_query)
    scores = (
        jnp.einsum("bqhd,bkhd->bhqk", query_blocks, block_keys, preferred_element_type=f32)
        * score_scale
    )
    scores = jnp.where(allowed_cross, scores, masked_fill)
    cross_max = jnp.max(scores, axis=-1, keepdims=True)
    cross_total = jnp.sum(jnp.exp(scores - cross_max), axis=-1, keepdims=True)
    cross_lse = cross_max + jnp.log(cross_total)
    cross_prob = jnp.where(allowed_cross, jnp.exp(scores - cross_lse), 0.0)
    cross_out = from_blocks(
        jnp.einsum("bhqk,bkhd->bqhd", to_low(cross_prob), block_values, preferred_element_type=f32)
        * keep_float
    )
    cross_low = to_low(cross_out).reshape(span_len, local_width)
    hidden_two = hidden_one + core_sum(mm_t(cross_low, w_co))
    normed_three, norm_back_three = jax.vjp(rms_apply, hidden_two, gain_values[2])
    normed_three = to_low(normed_three)
    upward = mm(normed_three, full_up)
    active, gelu_back = jax.vjp(partial(jax.nn.gelu, approximate=True), upward)
    active_low = to_low(active)
    result = hidden_two + core_sum(mm_t(active_low, full_down))
    out = to_low(result).reshape(row_count, span_len, model_width)

    cot_low = out_grad.reshape(span_len, model_width)
    cotangent = cot_low.astype(f32)
    grad_active = mm(cot_low, full_down)
    grad_upward = to_low(gelu_back(grad_active)[0])
    down_part = scatter_rows(t_mm(cot_low, active_low))
    up_part = scatter_rows(t_mm(normed_three, grad_upward))
    from_norm, grad_gain_three = norm_back_three(core_sum(mm_t(grad_upward, full_up)))
    grad_two = cotangent + from_norm
    resid_low = to_low(grad_two)
    grad_cross_att = to_low(mm(resid_low, w_co)).reshape(head_shape)
    grad_blocks = to_blocks(grad_cross_att) * keep_low
    grad_prob = jnp.einsum("bqhd,bkhd->bhqk", grad_blocks, block_values, preferred_element_type=f32)
    dot_sum = jnp.sum(cross_prob * grad_prob, axis=-1, keepdims=True)
    grad_score = to_low(cross_prob * (grad_prob - dot_sum))
    grad_cross_query = (
        from_blocks(
            jnp.einsum("bhqk,bkhd->bqhd", grad_score, block_keys, preferred_element_type=f32)
        )
        * score_scale
    )
    grad_keys = to_low(
        jnp.einsum("bhqk,bqhd->bkhd", grad_score, query_blocks, preferred_element_type=f32)
        * score_scale
    ).reshape(-1, local_width)
    grad_values = to_low(
        jnp.einsum("bhqk,bqhd->bkhd", to_low(cross_prob), grad_blocks, preferred_element_type=f32)
    ).reshape(-1, local_width)
    grad_cq_low = to_low(grad_cross_query).reshape(span_len, local_width)
    from_norm, grad_gain_two = norm_back_two(core_sum(mm_t(grad_cq_low, w_cq)))
    cross_part = scatter_rows(
        jnp.concatenate(
            [
                to_low(t_mm(normed_two, grad_cq_low)),
                to_low(t_mm(flat_all, grad_keys)),
                to_low(t_mm(flat_all, grad_values)),
                to_low(t_mm(resid_low, cross_low)),
            ],
            axis=1,
        )
    )
    grad_one = grad_two + from_norm
    att_grad_low = to_low(grad_one)
    grad_attn = to_low(mm(att_grad_low, w_so)).reshape(head_shape)
    so_grad = to_low(t_mm(att_grad_low, attn_low))
    grad_piece = jnp.einsum("qhd,khd->hqk", grad_attn, values_all, preferred_element_type=f32)
    self_dot = jnp.sum(self_prob * grad_piece, axis=-1, keepdims=True)
    score_grad = to_low(self_prob * (grad_piece - self_dot))
    grad_query = jnp.einsum("hqk,khd->qhd", score_grad, keys_all, preferred_element_type=f32)
    key_terms = (
        jnp.einsum("hqk,qhd->khd", score_grad, query_low, preferred_element_type=f32) * score_scale
    ).reshape(-1, local_width)
    value_terms = jnp.einsum(
        "hqk,qhd->khd", to_low(self_prob), grad_attn, preferred_element_type=f32
    ).reshape(-1, local_width)
    terms = jnp.concatenate([key_terms, value_terms], axis=1)
    own_terms = terms[:span_len]
    for k in range(1, halo + 1):
        sent = to_low(terms[k * span_len : (k + 1) * span_len])
        own_terms = own_terms + shifted(sent, "seq", -k).astype(f32)
    grad_q_low = to_low(rope_back(grad_query * score_scale)[0]).reshape(span_len, local_width)
    grad_k_low = to_low(rope_back(own_terms[:, :local_width].reshape(head_shape))[0]).reshape(
        span_len, local_width
    )
    grad_v_low = to_low(own_terms[:, local_width:])
    proj_grads = jnp.concatenate([grad_q_low, grad_k_low, grad_v_low], axis=1)
    qkv_grad = to_low(t_mm(normed_one, proj_grads))
    self_part = scatter_rows(jnp.concatenate([qkv_grad, so_grad], axis=1))
    from_norm, grad_gain_one = norm_back_one(core_sum(mm_t(proj_grads, w_qkv)))
    in_grad = (grad_one + from_norm).reshape(row_count, span_len, model_width)

    gain_grads = butterfly(
        jnp.stack([grad_gain_one, grad_gain_two, grad_gain_three]), ("seq", "dp")
    )
    shard = lax.axis_index("dp") * lax.axis_size("seq") + s_index
    gains_part = lax.dynamic_slice_in_dim(gain_grads, shard * shard_rows, shard_rows, axis=1)
    first_model = (lax.axis_index("mp") == 0).astype(f32)
    local_squares = (
        jnp.sum(self_part * self_part)
        + jnp.sum(cross_part * cross_part)
        + jnp.sum(up_part * up_part)
        + jnp.sum(down_part * down_part)
        + first_model * jnp.sum(gains_part * gains_part)
    )
    grad_norm = jnp.sqrt(butterfly(local_squares.reshape(1, 1), ("mp", "seq", "dp")).reshape(()))
    factor = jnp.minimum(1.0, clip_limit / (grad_norm + 1e-06))

    def split_update(weights, part, first, second, width):
        news = [
            adam_step(
                weights[j],
                part[j],
                first[j],
                second[j],
                factor,
                learn_rate,
                weight_decay,
            )
            for j in range(weights.shape[0])
        ]
        return tuple(jnp.stack([n[i] for n in news]) for i in range(3))

    def cols_of(part, count):
        return [part[:, j * local_width : (j + 1) * local_width] for j in range(count)]

    self_new, self_first_new, self_second_new = split_update(
        self_weights, cols_of(self_part, 4), self_first, self_second, local_width
    )
    cross_new, cross_first_new, cross_second_new = split_update(
        cross_weights, cols_of(cross_part, 4), cross_first, cross_second, local_width
    )
    feed_new, feed_first_new, feed_second_new = split_update(
        feed_weights, [up_part, down_part], feed_first, feed_second, hidden_width
    )
    gains_new, gains_first_new, gains_second_new = adam_step(
        norm_gains, gains_part, gains_first, gains_second, factor, gain_rate, 0.0
    )
    return (
        out,
        in_grad,
        grad_norm,
        self_new,
        cross_new,
        feed_new,
        gains_new,
        self_first_new,
        cross_first_new,
        feed_first_new,
        gains_first_new,
        self_second_new,
        cross_second_new,
        feed_second_new,
        gains_second_new,
    )


def solution(mesh):
    tok = P("dp", "seq", None)
    mat = P(None, ("dp", "seq"), "mp")
    vec = P(None, ("dp", "seq"))
    in_specs = (
        tok,
        P("dp", "seq", None, None, None),
        tok,
        P("dp", "seq"),
        tok,
    ) + (mat, mat, mat, vec) * 3
    out_specs = (tok, tok, P()) + (mat, mat, mat, vec) * 3
    return jax.shard_map(
        per_device, mesh=mesh, in_specs=in_specs, out_specs=out_specs, check_vma=False
    )
```

time: 1350 us -> 639 us (0.47)
  waiting for transfers between devices: 812 us -> 175 us
  blocking collectives: 185 us -> 0 us
  starting transfers between devices: 20.1 us -> 161 us
  matrix products: 97.6 us -> 62.9 us
  local copies, waits for them, and re-layouts: 129 us -> 154 us
    reduce_scatter x9 -> x0, waiting for transfers between devices: 302 us -> none  [the longest x1 262 us: per_device(): lax.psum_scatter(feed_grads, ('dp', 'seq'), scatter_dimension=1, tiled=True)]
    unnamed x16 -> x0, waiting for transfers between devices: 299 us -> none
    all_gather x5 -> x0, waiting for transfers between devices: 212 us -> none  [the longest x1 94.6 us: per_device(): lax.all_gather(to_low(feed_weights), ('dp', 'seq'), axis=1, tiled=True)]
    ppermute x6 -> x86, waiting for transfers between devices: 0.02 us -> 175 us  [the longest x51 117 us: swapped(): return lax.ppermute(value, axis, [(i, i ^ by) for i in range(count)])]
    ppermute x6 -> x86, starting transfers between devices: 19 us -> 161 us  [the longest x51 78.3 us: swapped(): return lax.ppermute(value, axis, [(i, i ^ by) for i in range(count)])]
    unnamed x1 -> x0, blocking collectives: 80.5 us -> none
    all_gather x8 -> x0, blocking collectives: 60.5 us -> none  [the longest x1 37.3 us: per_device(): lax.all_gather(to_low(norm_gains), ('dp', 'seq'), axis=1, tiled=True)]
    psum x1 -> x0, blocking collectives: 43.7 us -> none  [per_device(): grad_norm = jnp.sqrt(lax.psum(local_squares, ('dp', 'seq', 'mp')))]
  transfers between devices with their start and end apart: 21 -> 86, of which waited for: 12 -> 32; matrix products, arithmetic and copies ran while one was open for 16% -> 39% of each run, Pallas kernels for 0% -> 0%
where the time goes in v1:
time: 639 us; the launch traced here: 630 us
  waiting for transfers between devices  175 us (27%)
  starting transfers between devices  161 us (25%)
  local copies, waits for them, and re-layouts  154 us (24%)
  other arithmetic  67 us (10%)
  matrix products  62.9 us (10%)
  between operations  10.3 us (2%)
    ppermute x51, waiting for transfers between devices, swapped(): return lax.ppermute(value, axis, [(i, i ^ by) for i in range(count)])  117 us
    ppermute x51, starting transfers between devices, swapped(): return lax.ppermute(value, axis, [(i, i ^ by) for i in range(count)])  78.3 us
    ppermute x27, starting transfers between devices, rotated(): lax.ppermute(value, axis, [(i, (i + by) % count) for i in range(count)])  59.5 us
    dynamic_update_slice x41, local copies, waits for them, and re-layouts, put(): return lax.dynamic_update_slice(buffer, piece, starts)  41.2 us
    ppermute x27, waiting for transfers between devices, rotated(): lax.ppermute(value, axis, [(i, (i + by) % count) for i in range(count)])  40 us
    ppermute x8, starting transfers between devices, shifted(): lax.ppermute(value, axis, [(i, i + by) for i in range(count) if 0 <= i +...  23 us
    dot_general x7, matrix products, mm(): return jnp.dot(a, b, preferred_element_type=f32)  18.5 us
    ppermute x8, waiting for transfers between devices, shifted(): lax.ppermute(value, axis, [(i, i + by) for i in range(count) if 0 <= i +...  18.1 us
  transfers between devices with their start and end apart: 86, of which 32 were waited for; matrix products, arithmetic and copies ran while one was open for 39% of the time, Pallas kernels for 0%

profile of v1, /device:TPU:0, one launch (start us, length us, event | category | flops | bytes accessed | tf_op | source)
XLA Modules:
  0.0 630.3 jit_solution(13147797519286757181)
XLA Ops:
  1.3 4.9 collective-permute-start.10
  6.2 3.4 collective-permute-start.9
  10.9 2.7 collective-permute-start.21
  39.0 3.4 collective-permute-start.13
  43.9 5.4 collective-permute-done.11
  49.3 3.9 collective-permute-start.2
  53.9 4.6 collective-permute-done.12
  58.4 4.9 collective-permute-start.31
  66.2 12.2 %collective-permute-start.29 = (bf16[56,1792]{1,0:T(8,128)(2,1)}, bf16[56,1792]{1,0:T(8,128)(2,1)S(1)}, u32[]{:S(2)}, u32[]{:S(2)}) collective-permute-start(bf16[56,1792]{1,0:T(8,128)(2,1)} %get-tuple-element.166), channel_id=1, source_target_pairs={{0,8},{8,16},{16,24},{24,0},{1,9},{9,17},{17,25},{25,1},{2,10},{10... | collective-permute-start | bytes 602120 | tf_op jit(solution)/shard_map/ppermute | solution.py:41
  79.8 3.8 collective-permute-start.37
  88.1 7.5 %collective-permute-start.36 = (bf16[56,1792]{1,0:T(8,128)(2,1)S(1)}, bf16[56,1792]{1,0:T(8,128)(2,1)S(1)}, u32[]{:S(2)}, u32[]{:S(2)}) collective-permute-start(bf16[56,1792]{1,0:T(8,128)(2,1)S(1)} %copy-done.56), channel_id=1, source_target_pairs={{0,8},{8,16},{16,24},{24,0},{1,9},{9,17},{17,25},{25,1},{2,10},{10... | collective-permute-start | bytes 602120 | tf_op jit(solution)/shard_map/ppermute | solution.py:41
  96.3 3.3 collective-permute-start.19
  115.3 2.9 collective-permute-done.24
  118.2 2.5 collective-permute-start.4
  122.4 16.4 %collective-permute-done.25 = bf16[4,56,512]{2,1,0:T(8,128)(2,1)S(1)} collective-permute-done((bf16[4,56,512]{2,1,0:T(8,128)(2,1)S(1)}, bf16[4,56,512]{2,1,0:T(8,128)(2,1)S(1)}, u32[]{:S(2)}, u32[]{:S(2)}) %collective-permute-start.25) | collective-permute-done | bytes 229408 | tf_op jit(solution)/shard_map/ppermute | solution.py:46
  138.9 14.9 %collective-permute-done.26 = bf16[4,56,512]{2,1,0:T(8,128)(2,1)S(1)} collective-permute-done((bf16[4,56,512]{2,1,0:T(8,128)(2,1)S(1)}, bf16[4,56,512]{2,1,0:T(8,128)(2,1)S(1)}, u32[]{:S(2)}, u32[]{:S(2)}) %collective-permute-start.26) | collective-permute-done | bytes 229408 | tf_op jit(solution)/shard_map/ppermute | solution.py:46
  153.8 2.5 collective-permute-start.40
  156.4 3.4 convolution_convert_fusion
  161.5 4.3 reshape.559
  165.8 4.1 copy.307
  170.0 4.3 reshape.558
  174.3 4.1 copy.308
  194.6 22.0 %collective-permute-done.32 = bf16[4,56,1792]{2,1,0:T(8,128)(2,1)S(1)} collective-permute-done((bf16[4,56,1792]{2,1,0:T(8,128)(2,1)}, bf16[4,56,1792]{2,1,0:T(8,128)(2,1)S(1)}, u32[]{:S(2)}, u32[]{:S(2)}) %collective-permute-start.32) | collective-permute-done | bytes 802848 | tf_op jit(solution)/shard_map/ppermute | solution.py:46
  217.7 5.1 collective-permute-done.5
  228.6 2.8 fusion.4
  245.3 3.3 collective-permute-start.8
  248.6 3.5 collective-permute-start.7
  264.6 6.8 %collective-permute-done.8 = bf16[256,1024]{1,0:T(8,128)(2,1)S(1)} collective-permute-done((bf16[256,1024]{1,0:T(8,128)(2,1)S(1)}, bf16[256,1024]{1,0:T(8,128)(2,1)S(1)}, u32[]{:S(2)}, u32[]{:S(2)}) %collective-permute-start.8) | collective-permute-done | bytes 524320 | tf_op jit(solution)/shard_map/ppermute | solution.py:36
  271.3 2.5 collective-permute-start.35
  279.8 2.5 fusion
  317.6 3.1 fusion.164
  320.7 3.2 fusion.170
  323.9 3.7 fusion.16
  330.5 3.3 fusion.186
  337.2 13.9 %collective-permute-done.65 = bf16[4,2,56,896]{3,2,1,0:T(8,128)(2,1)S(1)} collective-permute-done((bf16[4,2,56,896]{3,2,1,0:T(8,128)(2,1)S(1)}, bf16[4,2,56,896]{3,2,1,0:T(8,128)(2,1)S(1)}, u32[]{:S(2)}, u32[]{:S(2)}) %collective-permute-start.65) | collective-permute-done | bytes 802848 | tf_op jit(solution)/shard_map/ppermute | solution.py:46
  352.2 3.1 collective-permute-done.63
  356.4 11.1 %collective-permute-done.72 = bf16[4,2,56,896]{3,2,1,0:T(8,128)(2,1)S(1)} collective-permute-done((bf16[4,2,56,896]{3,2,1,0:T(8,128)(2,1)S(1)}, bf16[4,2,56,896]{3,2,1,0:T(8,128)(2,1)S(1)}, u32[]{:S(2)}, u32[]{:S(2)}) %collective-permute-start.72) | collective-permute-done | bytes 802848 | tf_op jit(solution)/shard_map/ppermute | solution.py:46
  368.8 3.7 collective-permute-done.70
  377.7 2.7 convolution_convert_fusion.12
  390.3 3.2 fusion.19
  409.9 8.7 %pad_maximum_fusion.2 = bf16[896,2048]{0,1:T(8,128)(2,1)} fusion(bf16[896,512]{0,1:T(8,128)(2,1)S(1)} %copy-done.24, bf16[896,512]{0,1:T(8,128)(2,1)S(1)} %convolution_convert_fusion.8, bf16[896,512]{0,1:T(8,128)(2,1)S(1)} %convolution_convert_fusion.9, bf16[896,512]{0,1:T(8,128)(2,1)S(1)} %convolution_convert_fusion.6), kind=kLoop, calls=%fused_computation.11 | loop fusion | flops 14680064 | bytes 7340032 | tf_op jit(solution)/shard_map/concatenate | solution.py:333
  418.6 6.3 %copy.335 = bf16[896,2048]{1,0:T(8,128)(2,1)} copy(bf16[896,2048]{0,1:T(8,128)(2,1)} %pad_maximum_fusion.2) | data formatting | bytes 7340032 | tf_op jit(solution)/shard_map/concatenate | solution.py:333
  424.9 2.8 fusion.178
  432.7 2.4 collective-permute-start.67
  440.1 2.4 collective-permute-done.67
  447.4 11.1 %collective-permute-done.68 = bf16[56,1792]{1,0:T(8,128)(2,1)S(1)} collective-permute-done((bf16[56,1792]{1,0:T(8,128)(2,1)S(1)}, bf16[56,1792]{1,0:T(8,128)(2,1)S(1)}, u32[]{:S(2)}, u32[]{:S(2)}) %collective-permute-start.68) | collective-permute-done | bytes 200736 | tf_op jit(solution)/shard_map/ppermute | solution.py:41
  468.5 5.9 multiply_reduce_fusion
  487.0 7.6 %collective-permute-done.57 = bf16[4,56,1024]{2,1,0:T(8,128)(2,1)S(1)} collective-permute-done((bf16[4,56,1024]{2,1,0:T(8,128)(2,1)S(1)}, bf16[4,56,1024]{2,1,0:T(8,128)(2,1)S(1)}, u32[]{:S(2)}, u32[]{:S(2)}) %collective-permute-start.57) | collective-permute-done | bytes 458784 | tf_op jit(solution)/shard_map/ppermute | solution.py:46
  496.2 3.5 collective-permute-done.46
  501.7 7.8 %collective-permute-done.47 = bf16[256,1024]{0,1:T(8,128)(2,1)S(1)} collective-permute-done((bf16[256,1024]{0,1:T(8,128)(2,1)S(1)}, bf16[256,1024]{0,1:T(8,128)(2,1)S(1)}, u32[]{:S(2)}, u32[]{:S(2)}) %collective-permute-start.47) | collective-permute-done | bytes 524320 | tf_op jit(solution)/shard_map/ppermute | solution.py:36
  510.0 2.9 fusion.2
  515.1 3.2 collective-permute-start.62
  518.4 2.6 multiply_reduce_fusion.10
  521.3 11.9 %collective-permute-start.49 = (bf16[4,2,56,1024]{3,2,0,1:T(8,128)(2,1)S(1)}, bf16[4,2,56,1024]{3,2,0,1:T(8,128)(2,1)S(1)}, u32[]{:S(2)}, u32[]{:S(2)}) collective-permute-start(bf16[4,2,56,1024]{3,2,0,1:T(8,128)(2,1)S(1)} %bitcast.742), channel_id=1, source_target_pairs={{0,2},{2,0},{4,6},{6,4},{1,3},{3,1},{5,7},{7,5},{8,10},{10,8},{12,... | collective-permute-start | bytes 2752520 | tf_op jit(solution)/shard_map/ppermute | solution.py:46
  535.0 11.9 %collective-permute-start.77 = (f32[3,896]{1,0:T(4,128)S(1)}, f32[3,896]{1,0:T(4,128)S(1)}, u32[]{:S(2)}, u32[]{:S(2)}) collective-permute-start(f32[3,896]{1,0:T(4,128)S(1)} %pad_maximum_fusion.31), channel_id=1, source_target_pairs={{0,2},{2,0},{4,6},{6,4},{1,3},{3,1},{5,7},{7,5},{8,10},{10,8},{12,... | collective-permute-start | bytes 32264 | tf_op jit(solution)/shard_map/ppermute | solution.py:46
  547.3 5.9 collective-permute-start.52
  559.9 2.5 collective-permute-done.79
  562.3 3.0 collective-permute-start.80
  565.4 2.4 collective-permute-done.50
  569.5 3.3 collective-permute-start.55
  575.8 3.8 collective-permute-done.53
  580.4 10.1 %collective-permute-done.54 = bf16[56,2048]{1,0:T(8,128)(2,1)} collective-permute-done((bf16[56,2048]{1,0:T(8,128)(2,1)}, bf16[56,2048]{1,0:T(8,128)(2,1)}, u32[]{:S(2)}, u32[]{:S(2)}) %collective-permute-start.54) | collective-permute-done | bytes 229408 | tf_op jit(solution)/shard_map/ppermute | solution.py:41
  601.2 2.4 collective-permute-start.83
  611.1 3.2 collective-permute-done.85
  (551 shorter events, 273.3 us)
Async XLA Ops:
  1.3 36.8 %collective-permute-start.10 = (s32[1,256]{1,0:T(1,128)S(1)}, s32[1,256]{1,0:T(1,128)S(1)}, u32[]{:S(2)}, u32[]{:S(2)}) collective-permute-start(s32[1,256]{1,0:T(1,128)S(1)} %broadcast_add_fusion), channel_id=1, source_target_pairs={{0,4},{2,6},{1,5},{3,7},{8,12},{10,14},{9,13},{11,15},{16,20},{18,... | collective-permute-start | bytes 3080 | tf_op jit(solution)/shard_map/ppermute | solution.py:36
  6.2 32.0 %collective-permute-start.9 = (s32[1,256]{1,0:T(1,128)S(1)}, s32[1,256]{1,0:T(1,128)S(1)}, u32[]{:S(2)}, u32[]{:S(2)}) collective-permute-start(s32[1,256]{1,0:T(1,128)S(1)} %broadcast_add_fusion), channel_id=1, source_target_pairs={{0,2},{2,4},{4,6},{1,3},{3,5},{5,7},{8,10},{10,12},{12,14},{9,11},... | collective-permute-start | bytes 3080 | tf_op jit(solution)/shard_map/ppermute | solution.py:36
  10.9 31.4 %collective-permute-start.21 = (bf16[56,1024]{1,0:T(8,128)(2,1)S(1)}, bf16[56,1024]{1,0:T(8,128)(2,1)S(1)}, u32[]{:S(2)}, u32[]{:S(2)}) collective-permute-start(bf16[56,1024]{1,0:T(8,128)(2,1)S(1)} %pad_maximum_fusion.30), channel_id=1, source_target_pairs={{0,16},{8,24},{16,0},{24,8},{1,17},{9,25},{17,1},{25,9},{2,18},{10... | collective-permute-start | bytes 344072 | tf_op jit(solution)/shard_map/ppermute | solution.py:41
  13.6 25.4 %collective-permute-start.20 = (bf16[56,1024]{1,0:T(8,128)(2,1)S(1)}, bf16[56,1024]{1,0:T(8,128)(2,1)S(1)}, u32[]{:S(2)}, u32[]{:S(2)}) collective-permute-start(bf16[56,1024]{1,0:T(8,128)(2,1)S(1)} %pad_maximum_fusion.30), channel_id=1, source_target_pairs={{0,8},{8,16},{16,24},{24,0},{1,9},{9,17},{17,25},{25,1},{2,10},{10... | collective-permute-start | bytes 344072 | tf_op jit(solution)/shard_map/ppermute | solution.py:41
  17.3 15.4 %collective-permute-start.27 = (s32[3]{0:T(128)S(1)}, s32[3]{0:T(128)S(1)}, u32[]{:S(2)}, u32[]{:S(2)}) collective-permute-start(s32[3]{0:T(128)S(1)} %pad_add_fusion.3), channel_id=1, source_target_pairs={{0,2},{2,4},{4,6},{1,3},{3,5},{5,7},{8,10},{10,12},{12,14},{9,11},... | collective-permute-start | bytes 44 | tf_op jit(solution)/shard_map/ppermute | solution.py:36
  38.2 20.3 %collective-permute-start.12 = (bf16[56,1536]{1,0:T(8,128)(2,1)S(1)}, bf16[56,1536]{1,0:T(8,128)(2,1)S(1)}, u32[]{:S(2)}, u32[]{:S(2)}) collective-permute-start(bf16[56,1536]{1,0:T(8,128)(2,1)S(1)} %pad_maximum_fusion.27), channel_id=1, source_target_pairs={{0,16},{8,24},{16,0},{24,8},{1,17},{9,25},{17,1},{25,9},{2,18},{10... | collective-permute-start | bytes 516104 | tf_op jit(solution)/shard_map/ppermute | solution.py:41
  39.0 25.0 %collective-permute-start.13 = (bf16[56,1536]{1,0:T(8,128)(2,1)S(1)}, bf16[56,1536]{1,0:T(8,128)(2,1)S(1)}, u32[]{:S(2)}, u32[]{:S(2)}) collective-permute-start(bf16[56,1536]{1,0:T(8,128)(2,1)S(1)} %pad_maximum_fusion.27), channel_id=1, source_target_pairs={{0,24},{8,0},{16,8},{24,16},{1,25},{9,1},{17,9},{25,17},{2,26},{10... | collective-permute-start | bytes 516104 | tf_op jit(solution)/shard_map/ppermute | solution.py:41
  42.4 36.7 %collective-permute-start.1 = (bf16[56,1664]{1,0:T(8,128)(2,1)}, bf16[56,1664]{1,0:T(8,128)(2,1)S(1)}, u32[]{:S(2)}, u32[]{:S(2)}) collective-permute-start(bf16[56,1664]{1,0:T(8,128)(2,1)} %fusion.94), channel_id=1, source_target_pairs={{0,16},{8,24},{16,0},{24,8},{1,17},{9,25},{17,1},{25,9},{2,18},{10... | collective-permute-start | bytes 559112 | tf_op jit(solution)/shard_map/ppermute | solution.py:41
  43.6 22.6 %collective-permute-start = (bf16[56,1664]{1,0:T(8,128)(2,1)}, bf16[56,1664]{1,0:T(8,128)(2,1)S(1)}, u32[]{:S(2)}, u32[]{:S(2)}) collective-permute-start(bf16[56,1664]{1,0:T(8,128)(2,1)} %fusion.94), channel_id=1, source_target_pairs={{0,8},{8,16},{16,24},{24,0},{1,9},{9,17},{17,25},{25,1},{2,10},{10... | collective-permute-start | bytes 559112 | tf_op jit(solution)/shard_map/ppermute | solution.py:41
  49.3 30.5 %collective-permute-start.2 = (bf16[56,1664]{1,0:T(8,128)(2,1)}, bf16[56,1664]{1,0:T(8,128)(2,1)S(1)}, u32[]{:S(2)}, u32[]{:S(2)}) collective-permute-start(bf16[56,1664]{1,0:T(8,128)(2,1)} %fusion.94), channel_id=1, source_target_pairs={{0,24},{8,0},{16,8},{24,16},{1,25},{9,1},{17,9},{25,17},{2,26},{10... | collective-permute-start | bytes 559112 | tf_op jit(solution)/shard_map/ppermute | solution.py:41
  58.4 41.9 %collective-permute-start.31 = (bf16[56,1792]{1,0:T(8,128)(2,1)}, bf16[56,1792]{1,0:T(8,128)(2,1)S(1)}, u32[]{:S(2)}, u32[]{:S(2)}) collective-permute-start(bf16[56,1792]{1,0:T(8,128)(2,1)} %get-tuple-element.166), channel_id=1, source_target_pairs={{0,24},{8,0},{16,8},{24,16},{1,25},{9,1},{17,9},{25,17},{2,26},{10... | collective-permute-start | bytes 602120 | tf_op jit(solution)/shard_map/ppermute | solution.py:41
  64.1 32.2 %collective-permute-start.30 = (bf16[56,1792]{1,0:T(8,128)(2,1)}, bf16[56,1792]{1,0:T(8,128)(2,1)S(1)}, u32[]{:S(2)}, u32[]{:S(2)}) collective-permute-start(bf16[56,1792]{1,0:T(8,128)(2,1)} %get-tuple-element.166), channel_id=1, source_target_pairs={{0,16},{8,24},{16,0},{24,8},{1,17},{9,25},{17,1},{25,9},{2,18},{10... | collective-permute-start | bytes 602120 | tf_op jit(solution)/shard_map/ppermute | solution.py:41
  66.2 22.0 %collective-permute-start.29 = (bf16[56,1792]{1,0:T(8,128)(2,1)}, bf16[56,1792]{1,0:T(8,128)(2,1)S(1)}, u32[]{:S(2)}, u32[]{:S(2)}) collective-permute-start(bf16[56,1792]{1,0:T(8,128)(2,1)} %get-tuple-element.166), channel_id=1, source_target_pairs={{0,8},{8,16},{16,24},{24,0},{1,9},{9,17},{17,25},{25,1},{2,10},{10... | collective-permute-start | bytes 602120 | tf_op jit(solution)/shard_map/ppermute | solution.py:41
  79.0 29.4 %collective-permute-start.38 = (bf16[56,1792]{1,0:T(8,128)(2,1)S(1)}, bf16[56,1792]{1,0:T(8,128)(2,1)S(1)}, u32[]{:S(2)}, u32[]{:S(2)}) collective-permute-start(bf16[56,1792]{1,0:T(8,128)(2,1)S(1)} %copy-done.56), channel_id=1, source_target_pairs={{0,24},{8,0},{16,8},{24,16},{1,25},{9,1},{17,9},{25,17},{2,26},{10... | collective-permute-start | bytes 602120 | tf_op jit(solution)/shard_map/ppermute | solution.py:41
  79.8 26.0 %collective-permute-start.37 = (bf16[56,1792]{1,0:T(8,128)(2,1)S(1)}, bf16[56,1792]{1,0:T(8,128)(2,1)S(1)}, u32[]{:S(2)}, u32[]{:S(2)}) collective-permute-start(bf16[56,1792]{1,0:T(8,128)(2,1)S(1)} %copy-done.56), channel_id=1, source_target_pairs={{0,16},{8,24},{16,0},{24,8},{1,17},{9,25},{17,1},{25,9},{2,18},{10... | collective-permute-start | bytes 602120 | tf_op jit(solution)/shard_map/ppermute | solution.py:41
  88.1 16.9 %collective-permute-start.36 = (bf16[56,1792]{1,0:T(8,128)(2,1)S(1)}, bf16[56,1792]{1,0:T(8,128)(2,1)S(1)}, u32[]{:S(2)}, u32[]{:S(2)}) collective-permute-start(bf16[56,1792]{1,0:T(8,128)(2,1)S(1)} %copy-done.56), channel_id=1, source_target_pairs={{0,8},{8,16},{16,24},{24,0},{1,9},{9,17},{17,25},{25,1},{2,10},{10... | collective-permute-start | bytes 602120 | tf_op jit(solution)/shard_map/ppermute | solution.py:41
  96.3 57.5 %collective-permute-start.19 = (bf16[256,896]{1,0:T(8,128)(2,1)S(1)}, bf16[256,896]{1,0:T(8,128)(2,1)S(1)}, u32[]{:S(2)}, u32[]{:S(2)}) collective-permute-start(bf16[256,896]{1,0:T(8,128)(2,1)S(1)} %bitcast.747), channel_id=1, source_target_pairs={{0,2},{2,4},{4,6},{1,3},{3,5},{5,7},{8,10},{10,12},{12,14},{9,11},... | collective-permute-start | bytes 1376264 | tf_op jit(solution)/shard_map/ppermute | solution.py:36
  100.3 17.9 %collective-permute-start.24 = (bf16[4,56,1024]{2,1,0:T(8,128)(2,1)S(1)}, bf16[4,56,1024]{2,1,0:T(8,128)(2,1)S(1)}, u32[]{:S(2)}, u32[]{:S(2)}) collective-permute-start(bf16[4,56,1024]{2,1,0:T(8,128)(2,1)S(1)} %bitcast_dynamic-update-slice_fusion.39), channel_id=1, source_target_pairs={{0,4},{2,6},{4,0},{6,2},{1,5},{3,7},{5,1},{7,3},{8,12},{10,14},{12... | collective-permute-start | bytes 1376264 | tf_op jit(solution)/shard_map/ppermute | solution.py:46
  105.0 15.7 %collective-permute-start.23 = (bf16[4,56,1024]{2,1,0:T(8,128)(2,1)S(1)}, bf16[4,56,1024]{2,1,0:T(8,128)(2,1)S(1)}, u32[]{:S(2)}, u32[]{:S(2)}) collective-permute-start(bf16[4,56,1024]{2,1,0:T(8,128)(2,1)S(1)} %bitcast_dynamic-update-slice_fusion.39), channel_id=1, source_target_pairs={{0,2},{2,0},{4,6},{6,4},{1,3},{3,1},{5,7},{7,5},{8,10},{10,8},{12,... | collective-permute-start | bytes 1376264 | tf_op jit(solution)/shard_map/ppermute | solution.py:46
  105.7 72.7 %collective-permute-start.15 = (bf16[4,56,1536]{2,1,0:T(8,128)(2,1)}, bf16[4,56,1536]{2,1,0:T(8,128)(2,1)}, u32[]{:S(2)}, u32[]{:S(2)}) collective-permute-start(bf16[4,56,1536]{2,1,0:T(8,128)(2,1)} %bitcast_dynamic-update-slice_fusion.35), channel_id=1, source_target_pairs={{0,4},{2,6},{4,0},{6,2},{1,5},{3,7},{5,1},{7,3},{8,12},{10,14},{12... | collective-permute-start | bytes 2064392 | tf_op jit(solution)/shard_map/ppermute | solution.py:46
  108.5 73.8 %collective-permute-start.14 = (bf16[4,56,1536]{2,1,0:T(8,128)(2,1)}, bf16[4,56,1536]{2,1,0:T(8,128)(2,1)}, u32[]{:S(2)}, u32[]{:S(2)}) collective-permute-start(bf16[4,56,1536]{2,1,0:T(8,128)(2,1)} %bitcast_dynamic-update-slice_fusion.35), channel_id=1, source_target_pairs={{0,2},{2,0},{4,6},{6,4},{1,3},{3,1},{5,7},{7,5},{8,10},{10,8},{12,... | collective-permute-start | bytes 2064392 | tf_op jit(solution)/shard_map/ppermute | solution.py:46
  118.2 68.1 %collective-permute-start.4 = (bf16[4,56,1664]{2,1,0:T(8,128)(2,1)}, bf16[4,56,1664]{2,1,0:T(8,128)(2,1)}, u32[]{:S(2)}, u32[]{:S(2)}) collective-permute-start(bf16[4,56,1664]{2,1,0:T(8,128)(2,1)} %bitcast_dynamic-update-slice_fusion.31), channel_id=1, source_target_pairs={{0,4},{2,6},{4,0},{6,2},{1,5},{3,7},{5,1},{7,3},{8,12},{10,14},{12... | collective-permute-start | bytes 2236424 | tf_op jit(solution)/shard_map/ppermute | solution.py:46
  120.7 18.1 %collective-permute-start.25 = (bf16[4,56,512]{2,1,0:T(8,128)(2,1)S(1)}, bf16[4,56,512]{2,1,0:T(8,128)(2,1)S(1)}, u32[]{:S(2)}, u32[]{:S(2)}) collective-permute-start(bf16[4,56,512]{2,1,0:T(8,128)(2,1)S(1)} %slice.408), channel_id=1, source_target_pairs={{0,2},{2,0},{4,6},{6,4},{1,3},{3,1},{5,7},{7,5},{8,10},{10,8},{12,... | collective-permute-start | bytes 688136 | tf_op jit(solution)/shard_map/ppermute | solution.py:46
  153.8 33.7 %collective-permute-start.3 = (bf16[4,56,1664]{2,1,0:T(8,128)(2,1)}, bf16[4,56,1664]{2,1,0:T(8,128)(2,1)}, u32[]{:S(2)}, u32[]{:S(2)}) collective-permute-start(bf16[4,56,1664]{2,1,0:T(8,128)(2,1)} %bitcast_dynamic-update-slice_fusion.31), channel_id=1, source_target_pairs={{0,2},{2,0},{4,6},{6,4},{1,3},{3,1},{5,7},{7,5},{8,10},{10,8},{12,... | collective-permute-start | bytes 2236424 | tf_op jit(solution)/shard_map/ppermute | solution.py:46
  153.8 91.4 %collective-permute-start.40 = (bf16[4,56,1792]{2,1,0:T(8,128)(2,1)}, bf16[4,56,1792]{2,1,0:T(8,128)(2,1)}, u32[]{:S(2)}, u32[]{:S(2)}) collective-permute-start(bf16[4,56,1792]{2,1,0:T(8,128)(2,1)} %bitcast_dynamic-update-slice_fusion.25), channel_id=1, source_target_pairs={{0,4},{2,6},{4,0},{6,2},{1,5},{3,7},{5,1},{7,3},{8,12},{10,14},{12... | collective-permute-start | bytes 2408456 | tf_op jit(solution)/shard_map/ppermute | solution.py:46
  178.4 80.2 %collective-permute-start.39 = (bf16[4,56,1792]{2,1,0:T(8,128)(2,1)}, bf16[4,56,1792]{2,1,0:T(8,128)(2,1)}, u32[]{:S(2)}, u32[]{:S(2)}) collective-permute-start(bf16[4,56,1792]{2,1,0:T(8,128)(2,1)} %bitcast_dynamic-update-slice_fusion.25), channel_id=1, source_target_pairs={{0,2},{2,0},{4,6},{6,4},{1,3},{3,1},{5,7},{7,5},{8,10},{10,8},{12,... | collective-permute-start | bytes 2408456 | tf_op jit(solution)/shard_map/ppermute | solution.py:46
  182.2 66.4 %collective-permute-start.33 = (bf16[4,56,1792]{2,1,0:T(8,128)(2,1)}, bf16[4,56,1792]{2,1,0:T(8,128)(2,1)}, u32[]{:S(2)}, u32[]{:S(2)}) collective-permute-start(bf16[4,56,1792]{2,1,0:T(8,128)(2,1)} %bitcast_dynamic-update-slice_fusion.28), channel_id=1, source_target_pairs={{0,4},{2,6},{4,0},{6,2},{1,5},{3,7},{5,1},{7,3},{8,12},{10,14},{12... | collective-permute-start | bytes 2408456 | tf_op jit(solution)/shard_map/ppermute | solution.py:46
  186.3 30.3 %collective-permute-start.32 = (bf16[4,56,1792]{2,1,0:T(8,128)(2,1)}, bf16[4,56,1792]{2,1,0:T(8,128)(2,1)S(1)}, u32[]{:S(2)}, u32[]{:S(2)}) collective-permute-start(bf16[4,56,1792]{2,1,0:T(8,128)(2,1)} %bitcast_dynamic-update-slice_fusion.28), channel_id=1, source_target_pairs={{0,2},{2,0},{4,6},{6,4},{1,3},{3,1},{5,7},{7,5},{8,10},{10,8},{12,... | collective-permute-start | bytes 2408456 | tf_op jit(solution)/shard_map/ppermute | solution.py:46
  187.4 35.4 %collective-permute-start.5 = (bf16[4,56,768]{2,1,0:T(8,128)(2,1)S(1)}, bf16[4,56,768]{2,1,0:T(8,128)(2,1)S(1)}, u32[]{:S(2)}, u32[]{:S(2)}) collective-permute-start(bf16[4,56,768]{2,1,0:T(8,128)(2,1)S(1)} %slice.391), channel_id=1, source_target_pairs={{0,2},{2,0},{4,6},{6,4},{1,3},{3,1},{5,7},{7,5},{8,10},{10,8},{12,... | collective-permute-start | bytes 1032200 | tf_op jit(solution)/shard_map/ppermute | solution.py:46
  222.8 37.7 %collective-permute-start.16 = (bf16[4,56,768]{2,1,0:T(8,128)(2,1)}, bf16[4,56,768]{2,1,0:T(8,128)(2,1)}, u32[]{:S(2)}, u32[]{:S(2)}) collective-permute-start(bf16[4,56,768]{2,1,0:T(8,128)(2,1)} %slice.405), channel_id=1, source_target_pairs={{0,2},{2,0},{4,6},{6,4},{1,3},{3,1},{5,7},{7,5},{8,10},{10,8},{12,... | collective-permute-start | bytes 1032200 | tf_op jit(solution)/shard_map/ppermute | solution.py:46
  225.4 36.0 %collective-permute-start.17 = (bf16[4,56,768]{2,1,0:T(8,128)(2,1)}, bf16[4,56,768]{2,1,0:T(8,128)(2,1)}, u32[]{:S(2)}, u32[]{:S(2)}) collective-permute-start(bf16[4,56,768]{2,1,0:T(8,128)(2,1)} %slice.406), channel_id=1, source_target_pairs={{0,4},{2,6},{4,0},{6,2},{1,5},{3,7},{5,1},{7,3},{8,12},{10,14},{12... | collective-permute-start | bytes 1032200 | tf_op jit(solution)/shard_map/ppermute | solution.py:46
  245.3 26.1 %collective-permute-start.8 = (bf16[256,1024]{1,0:T(8,128)(2,1)S(1)}, bf16[256,1024]{1,0:T(8,128)(2,1)S(1)}, u32[]{:S(2)}, u32[]{:S(2)}) collective-permute-start(bf16[256,1024]{1,0:T(8,128)(2,1)S(1)} %pad_maximum_fusion.16), channel_id=1, source_target_pairs={{0,4},{2,6},{1,5},{3,7},{8,12},{10,14},{9,13},{11,15},{16,20},{18,... | collective-permute-start | bytes 1572872 | tf_op jit(solution)/shard_map/ppermute | solution.py:36
  248.6 25.2 %collective-permute-start.7 = (bf16[256,1024]{1,0:T(8,128)(2,1)S(1)}, bf16[256,1024]{1,0:T(8,128)(2,1)S(1)}, u32[]{:S(2)}, u32[]{:S(2)}) collective-permute-start(bf16[256,1024]{1,0:T(8,128)(2,1)S(1)} %pad_maximum_fusion.16), channel_id=1, source_target_pairs={{0,2},{2,4},{4,6},{1,3},{3,5},{5,7},{8,10},{10,12},{12,14},{9,11},... | collective-permute-start | bytes 1572872 | tf_op jit(solution)/shard_map/ppermute | solution.py:36
  258.7 55.0 %collective-permute-start.41 = (bf16[4,56,896]{2,1,0:T(8,128)(2,1)}, bf16[4,56,896]{2,1,0:T(8,128)(2,1)}, u32[]{:S(2)}, u32[]{:S(2)}) collective-permute-start(bf16[4,56,896]{2,1,0:T(8,128)(2,1)} %slice.420), channel_id=1, source_target_pairs={{0,2},{2,0},{4,6},{6,4},{1,3},{3,1},{5,7},{7,5},{8,10},{10,8},{12,... | collective-permute-start | bytes 1204232 | tf_op jit(solution)/shard_map/ppermute | solution.py:46
  260.4 55.1 %collective-permute-start.42 = (bf16[4,56,896]{2,1,0:T(8,128)(2,1)}, bf16[4,56,896]{2,1,0:T(8,128)(2,1)}, u32[]{:S(2)}, u32[]{:S(2)}) collective-permute-start(bf16[4,56,896]{2,1,0:T(8,128)(2,1)} %slice.421), channel_id=1, source_target_pairs={{0,4},{2,6},{4,0},{6,2},{1,5},{3,7},{5,1},{7,3},{8,12},{10,14},{12... | collective-permute-start | bytes 1204232 | tf_op jit(solution)/shard_map/ppermute | solution.py:46
  261.5 48.6 %collective-permute-start.34 = (bf16[4,56,896]{2,1,0:T(8,128)(2,1)}, bf16[4,56,896]{2,1,0:T(8,128)(2,1)}, u32[]{:S(2)}, u32[]{:S(2)}) collective-permute-start(bf16[4,56,896]{2,1,0:T(8,128)(2,1)} %slice.418), channel_id=1, source_target_pairs={{0,2},{2,0},{4,6},{6,4},{1,3},{3,1},{5,7},{7,5},{8,10},{10,8},{12,... | collective-permute-start | bytes 1204232 | tf_op jit(solution)/shard_map/ppermute | solution.py:46
  271.3 40.6 %collective-permute-start.35 = (bf16[4,56,896]{2,1,0:T(8,128)(2,1)}, bf16[4,56,896]{2,1,0:T(8,128)(2,1)}, u32[]{:S(2)}, u32[]{:S(2)}) collective-permute-start(bf16[4,56,896]{2,1,0:T(8,128)(2,1)} %slice.419), channel_id=1, source_target_pairs={{0,4},{2,6},{4,0},{6,2},{1,5},{3,7},{5,1},{7,3},{8,12},{10,14},{12... | collective-permute-start | bytes 1204232 | tf_op jit(solution)/shard_map/ppermute | solution.py:46
  330.4 20.8 %collective-permute-start.65 = (bf16[4,2,56,896]{3,2,1,0:T(8,128)(2,1)S(1)}, bf16[4,2,56,896]{3,2,1,0:T(8,128)(2,1)S(1)}, u32[]{:S(2)}, u32[]{:S(2)}) collective-permute-start(bf16[4,2,56,896]{3,2,1,0:T(8,128)(2,1)S(1)} %dynamic-slice_bitcast_fusion.4), channel_id=1, source_target_pairs={{0,4},{2,6},{4,0},{6,2},{1,5},{3,7},{5,1},{7,3},{8,12},{10,14},{12... | collective-permute-start | bytes 2408456 | tf_op jit(solution)/shard_map/ppermute | solution.py:46
  333.7 39.9 %collective-permute-start.44 = (f32[256,896]{1,0:T(8,128)S(1)}, f32[256,896]{1,0:T(8,128)S(1)}, u32[]{:S(2)}, u32[]{:S(2)}) collective-permute-start(f32[256,896]{1,0:T(8,128)S(1)} %fusion.186), channel_id=1, source_target_pairs={{0,1},{1,0},{2,3},{3,2},{4,5},{5,4},{6,7},{7,6},{8,9},{9,8},{10,11... | collective-permute-start | bytes 2752520 | tf_op jit(solution)/shard_map/ppermute | solution.py:46
  333.8 42.7 %collective-permute-start.43 = (f32[256,896]{1,0:T(8,128)S(1)}, f32[256,896]{1,0:T(8,128)S(1)}, u32[]{:S(2)}, u32[]{:S(2)}) collective-permute-start(f32[256,896]{1,0:T(8,128)S(1)} %fusion.170), channel_id=1, source_target_pairs={{0,1},{1,0},{2,3},{3,2},{4,5},{5,4},{6,7},{7,6},{8,9},{9,8},{10,11... | collective-permute-start | bytes 2752520 | tf_op jit(solution)/shard_map/ppermute | solution.py:46
  334.5 20.8 %collective-permute-start.63 = (bf16[4,2,56,896]{3,2,0,1:T(8,128)(2,1)S(1)}, bf16[4,2,56,896]{3,2,0,1:T(8,128)(2,1)S(1)}, u32[]{:S(2)}, u32[]{:S(2)}) collective-permute-start(bf16[4,2,56,896]{3,2,0,1:T(8,128)(2,1)S(1)} %bitcast.744), channel_id=1, source_target_pairs={{0,2},{2,0},{4,6},{6,4},{1,3},{3,1},{5,7},{7,5},{8,10},{10,8},{12,... | collective-permute-start | bytes 2408456 | tf_op jit(solution)/shard_map/ppermute | solution.py:46
  335.2 32.3 %collective-permute-start.72 = (bf16[4,2,56,896]{3,2,1,0:T(8,128)(2,1)S(1)}, bf16[4,2,56,896]{3,2,1,0:T(8,128)(2,1)S(1)}, u32[]{:S(2)}, u32[]{:S(2)}) collective-permute-start(bf16[4,2,56,896]{3,2,1,0:T(8,128)(2,1)S(1)} %dynamic-slice_bitcast_fusion.3), channel_id=1, source_target_pairs={{0,4},{2,6},{4,0},{6,2},{1,5},{3,7},{5,1},{7,3},{8,12},{10,14},{12... | collective-permute-start | bytes 2408456 | tf_op jit(solution)/shard_map/ppermute | solution.py:46
  351.2 21.3 %collective-permute-start.70 = (bf16[4,2,56,896]{3,2,0,1:T(8,128)(2,1)S(1)}, bf16[4,2,56,896]{3,2,0,1:T(8,128)(2,1)S(1)}, u32[]{:S(2)}, u32[]{:S(2)}) collective-permute-start(bf16[4,2,56,896]{3,2,0,1:T(8,128)(2,1)S(1)} %bitcast.743), channel_id=1, source_target_pairs={{0,2},{2,0},{4,6},{6,4},{1,3},{3,1},{5,7},{7,5},{8,10},{10,8},{12,... | collective-permute-start | bytes 2408456 | tf_op jit(solution)/shard_map/ppermute | solution.py:46
  355.3 74.2 %collective-permute-start.66 = (bf16[4,56,896]{2,1,0:T(8,128)(2,1)}, bf16[4,56,896]{2,1,0:T(8,128)(2,1)}, u32[]{:S(2)}, u32[]{:S(2)}) collective-permute-start(bf16[4,56,896]{2,1,0:T(8,128)(2,1)} %fusion.68), channel_id=1, source_target_pairs={{0,2},{2,0},{4,6},{6,4},{1,3},{3,1},{5,7},{7,5},{8,10},{10,8},{12,... | collective-permute-start | bytes 1204232 | tf_op jit(solution)/shard_map/ppermute | solution.py:46
  367.5 63.8 %collective-permute-start.64 = (bf16[4,56,896]{2,1,0:T(8,128)(2,1)}, bf16[4,56,896]{2,1,0:T(8,128)(2,1)}, u32[]{:S(2)}, u32[]{:S(2)}) collective-permute-start(bf16[4,56,896]{2,1,0:T(8,128)(2,1)} %fusion.67), channel_id=1, source_target_pairs={{0,4},{2,6},{4,0},{6,2},{1,5},{3,7},{5,1},{7,3},{8,12},{10,14},{12... | collective-permute-start | bytes 1204232 | tf_op jit(solution)/shard_map/ppermute | solution.py:46
  372.5 62.6 %collective-permute-start.73 = (bf16[4,56,896]{2,1,0:T(8,128)(2,1)}, bf16[4,56,896]{2,1,0:T(8,128)(2,1)}, u32[]{:S(2)}, u32[]{:S(2)}) collective-permute-start(bf16[4,56,896]{2,1,0:T(8,128)(2,1)} %fusion.70), channel_id=1, source_target_pairs={{0,2},{2,0},{4,6},{6,4},{1,3},{3,1},{5,7},{7,5},{8,10},{10,8},{12,... | collective-permute-start | bytes 1204232 | tf_op jit(solution)/shard_map/ppermute | solution.py:46
  373.6 64.0 %collective-permute-start.71 = (bf16[4,56,896]{2,1,0:T(8,128)(2,1)}, bf16[4,56,896]{2,1,0:T(8,128)(2,1)}, u32[]{:S(2)}, u32[]{:S(2)}) collective-permute-start(bf16[4,56,896]{2,1,0:T(8,128)(2,1)} %fusion.69), channel_id=1, source_target_pairs={{0,4},{2,6},{4,0},{6,2},{1,5},{3,7},{5,1},{7,3},{8,12},{10,14},{12... | collective-permute-start | bytes 1204232 | tf_op jit(solution)/shard_map/ppermute | solution.py:46
  428.5 33.8 %collective-permute-start.58 = (bf16[4,2,56,1024]{3,2,1,0:T(8,128)(2,1)S(1)}, bf16[4,2,56,1024]{3,2,1,0:T(8,128)(2,1)S(1)}, u32[]{:S(2)}, u32[]{:S(2)}) collective-permute-start(bf16[4,2,56,1024]{3,2,1,0:T(8,128)(2,1)S(1)} %dynamic-slice_bitcast_fusion), channel_id=1, source_target_pairs={{0,4},{2,6},{4,0},{6,2},{1,5},{3,7},{5,1},{7,3},{8,12},{10,14},{12... | collective-permute-start | bytes 2752520 | tf_op jit(solution)/shard_map/ppermute | solution.py:46
  429.5 30.4 %collective-permute-start.45 = (f32[256,896]{1,0:T(8,128)S(1)}, f32[256,896]{1,0:T(8,128)S(1)}, u32[]{:S(2)}, u32[]{:S(2)}) collective-permute-start(f32[256,896]{1,0:T(8,128)S(1)} %fusion.41), channel_id=1, source_target_pairs={{0,1},{1,0},{2,3},{3,2},{4,5},{5,4},{6,7},{7,6},{8,9},{9,8},{10,11... | collective-permute-start | bytes 2752520 | tf_op jit(solution)/shard_map/ppermute | solution.py:46
  437.6 20.8 %collective-permute-start.68 = (bf16[56,1792]{1,0:T(8,128)(2,1)S(1)}, bf16[56,1792]{1,0:T(8,128)(2,1)S(1)}, u32[]{:S(2)}, u32[]{:S(2)}) collective-permute-start(bf16[56,1792]{1,0:T(8,128)(2,1)S(1)} %get-tuple-element.165), channel_id=1, source_target_pairs={{0,16},{8,24},{16,0},{24,8},{1,17},{9,25},{17,1},{25,9},{2,18},{10... | collective-permute-start | bytes 602120 | tf_op jit(solution)/shard_map/ppermute | solution.py:41
  442.4 38.0 %collective-permute-start.56 = (bf16[4,2,56,1024]{3,2,1,0:T(8,128)(2,1)}, bf16[4,2,56,1024]{3,2,1,0:T(8,128)(2,1)}, u32[]{:S(2)}, u32[]{:S(2)}) collective-permute-start(bf16[4,2,56,1024]{3,2,1,0:T(8,128)(2,1)} %dynamic-slice_bitcast_fusion.1), channel_id=1, source_target_pairs={{0,2},{2,0},{4,6},{6,4},{1,3},{3,1},{5,7},{7,5},{8,10},{10,8},{12,... | collective-permute-start | bytes 2752520 | tf_op jit(solution)/shard_map/ppermute | solution.py:46
  445.6 69.5 %collective-permute-start.74 = (bf16[56,1792]{1,0:T(8,128)(2,1)}, bf16[56,1792]{1,0:T(8,128)(2,1)}, u32[]{:S(2)}, u32[]{:S(2)}) collective-permute-start(bf16[56,1792]{1,0:T(8,128)(2,1)} %get-tuple-element.160), channel_id=1, source_target_pairs={{0,8},{8,16},{16,24},{24,0},{1,9},{9,17},{17,25},{25,1},{2,10},{10... | collective-permute-start | bytes 602120 | tf_op jit(solution)/shard_map/ppermute | solution.py:41
  458.5 59.9 %collective-permute-start.76 = (bf16[56,1792]{1,0:T(8,128)(2,1)}, bf16[56,1792]{1,0:T(8,128)(2,1)}, u32[]{:S(2)}, u32[]{:S(2)}) collective-permute-start(bf16[56,1792]{1,0:T(8,128)(2,1)} %get-tuple-element.161), channel_id=1, source_target_pairs={{0,24},{8,0},{16,8},{24,16},{1,25},{9,1},{17,9},{25,17},{2,26},{10... | collective-permute-start | bytes 602120 | tf_op jit(solution)/shard_map/ppermute | solution.py:41
  459.9 58.4 %collective-permute-start.75 = (bf16[56,1792]{1,0:T(8,128)(2,1)}, bf16[56,1792]{1,0:T(8,128)(2,1)}, u32[]{:S(2)}, u32[]{:S(2)}) collective-permute-start(bf16[56,1792]{1,0:T(8,128)(2,1)} %get-tuple-element.162), channel_id=1, source_target_pairs={{0,16},{8,24},{16,0},{24,8},{1,17},{9,25},{17,1},{25,9},{2,18},{10... | collective-permute-start | bytes 602120 | tf_op jit(solution)/shard_map/ppermute | solution.py:41
  464.7 19.7 %collective-permute-start.59 = (bf16[4,56,1024]{2,1,0:T(8,128)(2,1)}, bf16[4,56,1024]{2,1,0:T(8,128)(2,1)}, u32[]{:S(2)}, u32[]{:S(2)}) collective-permute-start(bf16[4,56,1024]{2,1,0:T(8,128)(2,1)} %fusion.52), channel_id=1, source_target_pairs={{0,2},{2,0},{4,6},{6,4},{1,3},{3,1},{5,7},{7,5},{8,10},{10,8},{12,... | collective-permute-start | bytes 1376264 | tf_op jit(solution)/shard_map/ppermute | solution.py:46
  499.7 21.5 %collective-permute-start.60 = (bf16[56,2048]{1,0:T(8,128)(2,1)S(1)}, bf16[56,2048]{1,0:T(8,128)(2,1)S(1)}, u32[]{:S(2)}, u32[]{:S(2)}) collective-permute-start(bf16[56,2048]{1,0:T(8,128)(2,1)S(1)} %get-tuple-element.152), channel_id=1, source_target_pairs={{0,8},{8,16},{16,24},{24,0},{1,9},{9,17},{17,25},{25,1},{2,10},{10... | collective-permute-start | bytes 688136 | tf_op jit(solution)/shard_map/ppermute | solution.py:41
  514.0 20.6 %collective-permute-start.48 = (f32[256,896]{1,0:T(8,128)S(1)}, f32[256,896]{1,0:T(8,128)S(1)}, u32[]{:S(2)}, u32[]{:S(2)}) collective-permute-start(f32[256,896]{1,0:T(8,128)S(1)} %fusion.2), channel_id=1, source_target_pairs={{0,1},{1,0},{2,3},{3,2},{4,5},{5,4},{6,7},{7,6},{8,9},{9,8},{10,11... | collective-permute-start | bytes 2752520 | tf_op jit(solution)/shard_map/ppermute | solution.py:46
  515.1 18.0 %collective-permute-start.62 = (bf16[56,2048]{1,0:T(8,128)(2,1)S(1)}, bf16[56,2048]{1,0:T(8,128)(2,1)S(1)}, u32[]{:S(2)}, u32[]{:S(2)}) collective-permute-start(bf16[56,2048]{1,0:T(8,128)(2,1)S(1)} %get-tuple-element.153), channel_id=1, source_target_pairs={{0,24},{8,0},{16,8},{24,16},{1,25},{9,1},{17,9},{25,17},{2,26},{10... | collective-permute-start | bytes 688136 | tf_op jit(solution)/shard_map/ppermute | solution.py:41
  518.4 15.5 %collective-permute-start.61 = (bf16[56,2048]{1,0:T(8,128)(2,1)S(1)}, bf16[56,2048]{1,0:T(8,128)(2,1)S(1)}, u32[]{:S(2)}, u32[]{:S(2)}) collective-permute-start(bf16[56,2048]{1,0:T(8,128)(2,1)S(1)} %get-tuple-element.154), channel_id=1, source_target_pairs={{0,16},{8,24},{16,0},{24,8},{1,17},{9,25},{17,1},{25,9},{2,18},{10... | collective-permute-start | bytes 688136 | tf_op jit(solution)/shard_map/ppermute | solution.py:41
  518.4 28.5 %collective-permute-start.51 = (bf16[4,2,56,1024]{3,2,1,0:T(8,128)(2,1)S(1)}, bf16[4,2,56,1024]{3,2,1,0:T(8,128)(2,1)S(1)}, u32[]{:S(2)}, u32[]{:S(2)}) collective-permute-start(bf16[4,2,56,1024]{3,2,1,0:T(8,128)(2,1)S(1)} %dynamic-slice_bitcast_fusion.2), channel_id=1, source_target_pairs={{0,4},{2,6},{4,0},{6,2},{1,5},{3,7},{5,1},{7,3},{8,12},{10,14},{12... | collective-permute-start | bytes 2752520 | tf_op jit(solution)/shard_map/ppermute | solution.py:46
  521.3 33.0 %collective-permute-start.49 = (bf16[4,2,56,1024]{3,2,0,1:T(8,128)(2,1)S(1)}, bf16[4,2,56,1024]{3,2,0,1:T(8,128)(2,1)S(1)}, u32[]{:S(2)}, u32[]{:S(2)}) collective-permute-start(bf16[4,2,56,1024]{3,2,0,1:T(8,128)(2,1)S(1)} %bitcast.742), channel_id=1, source_target_pairs={{0,2},{2,0},{4,6},{6,4},{1,3},{3,1},{5,7},{7,5},{8,10},{10,8},{12,... | collective-permute-start | bytes 2752520 | tf_op jit(solution)/shard_map/ppermute | solution.py:46
  535.0 19.6 %collective-permute-start.77 = (f32[3,896]{1,0:T(4,128)S(1)}, f32[3,896]{1,0:T(4,128)S(1)}, u32[]{:S(2)}, u32[]{:S(2)}) collective-permute-start(f32[3,896]{1,0:T(4,128)S(1)} %pad_maximum_fusion.31), channel_id=1, source_target_pairs={{0,2},{2,0},{4,6},{6,4},{1,3},{3,1},{5,7},{7,5},{8,10},{10,8},{12,... | collective-permute-start | bytes 32264 | tf_op jit(solution)/shard_map/ppermute | solution.py:46
  547.3 18.0 %collective-permute-start.52 = (bf16[4,56,1024]{2,1,0:T(8,128)(2,1)S(1)}, bf16[4,56,1024]{2,1,0:T(8,128)(2,1)S(1)}, u32[]{:S(2)}, u32[]{:S(2)}) collective-permute-start(bf16[4,56,1024]{2,1,0:T(8,128)(2,1)S(1)} %fusion.50), channel_id=1, source_target_pairs={{0,2},{2,0},{4,6},{6,4},{1,3},{3,1},{5,7},{7,5},{8,10},{10,8},{12,... | collective-permute-start | bytes 1376264 | tf_op jit(solution)/shard_map/ppermute | solution.py:46
  572.8 17.7 %collective-permute-start.54 = (bf16[56,2048]{1,0:T(8,128)(2,1)}, bf16[56,2048]{1,0:T(8,128)(2,1)}, u32[]{:S(2)}, u32[]{:S(2)}) collective-permute-start(bf16[56,2048]{1,0:T(8,128)(2,1)} %get-tuple-element.157), channel_id=1, source_target_pairs={{0,16},{8,24},{16,0},{24,8},{1,17},{9,25},{17,1},{25,9},{2,18},{10... | collective-permute-start | bytes 688136 | tf_op jit(solution)/shard_map/ppermute | solution.py:41
  (104 other events, 1250.4 us)

commit v2 on v1

v2 whole, which is shorter than its diff:
```python
import jax
import jax.numpy as jnp
from jax import lax
from jax.experimental import pallas as pl
from jax.experimental.pallas import tpu as pltpu
from jax.sharding import PartitionSpec as P

HEAD_DIM = 64
PAIR = 128
BLOCK = 64
NEIGHBOURS = 2
NEIGH_LEN = 128
KEYS = NEIGHBOURS * NEIGH_LEN
STEP = 10
DOC_MAX = 512
CHUNK = 256

norm_eps = 1e-05
rope_base = 10000.0
beta_one = 0.9
beta_two = 0.95
adam_eps = 1e-08
weight_decay = 0.1
learn_rate = 0.1
gain_rate = 0.5
clip_limit = 1.0
masked_fill = -1e30
score_scale = HEAD_DIM ** (-0.5)
gelu_c = 0.7978845608028654
gelu_k = 0.044715

f32 = jnp.float32
bf16 = jnp.bfloat16


def to_low(array_in):
    return array_in.astype(bf16)


def shifted(value, axis, by):
    count = lax.axis_size(axis)
    return lax.ppermute(value, axis, [(i, i + by) for i in range(count) if 0 <= i + by < count])


def rotated(value, axis, by):
    count = lax.axis_size(axis)
    return lax.ppermute(value, axis, [(i, (i + by) % count) for i in range(count)])


def swapped(value, axis, by):
    count = lax.axis_size(axis)
    return lax.ppermute(value, axis, [(i, i ^ by) for i in range(count)])


def butterfly(value, axes):
    for axis in axes:
        step = 1
        while step < lax.axis_size(axis):
            value = value + swapped(value, axis, step)
            step *= 2
    return value


def core_sum(partial_out):
    return partial_out + swapped(partial_out, "mp", 1)


def small_mesh():
    return lax.axis_size("dp") == 4 and lax.axis_size("seq") == 4


def put(buffer, piece, starts):
    return lax.dynamic_update_slice(buffer, piece, starts)


def gather_rows(block):
    if not small_mesh():
        return lax.all_gather(block, ("dp", "seq"), axis=0, tiled=True)
    rows, cols = block.shape
    half = cols // 256 * 128
    z = lax.axis_index("dp")
    s = lax.axis_index("seq")
    pieces = [block] + [rotated(block, "dp", k) for k in (1, 2, 3)]
    column = jnp.zeros((4, rows, cols), block.dtype)
    for k, piece in enumerate(pieces):
        column = put(column, piece[None], ((z - k) % 4, 0, 0))
    from_x = swapped(column, "seq", 1)
    from_y = swapped(column, "seq", 2)
    diag_a = swapped(from_y[..., :half], "seq", 1)
    diag_b = swapped(from_x[..., half:], "seq", 2)
    out = jnp.zeros((4, 4, rows, cols), block.dtype)
    out = put(out, column[:, None], (0, s, 0, 0))
    out = put(out, from_x[:, None], (0, s ^ 1, 0, 0))
    out = put(out, from_y[:, None], (0, s ^ 2, 0, 0))
    out = put(out, diag_a[:, None], (0, s ^ 3, 0, 0))
    out = put(out, diag_b[:, None], (0, s ^ 3, 0, half))
    return out.reshape(16 * rows, cols)


def take(array_in, index, axis):
    return lax.dynamic_index_in_dim(array_in, index, axis, keepdims=False)


def z_sum(column):
    z = lax.axis_index("dp")
    low = to_low(column)
    total = take(column, z, 0).astype(f32)
    for k in (1, 2, 3):
        total = total + rotated(take(low, (z + k) % 4, 0), "dp", k).astype(f32)
    return total


def scatter_rows(left, right):
    if not small_mesh():
        low = jnp.concatenate(left + right, axis=1)
        return lax.psum_scatter(low, ("dp", "seq"), scatter_dimension=0, tiled=True).astype(f32)
    rows = left[0].shape[0] // 16
    s = lax.axis_index("seq")
    x, y = s % 2, s // 2

    def pick(parts, index, axis):
        return jnp.concatenate(
            [take(p.reshape(4, 2, 2, rows, p.shape[1]), index, axis) for p in parts], axis=-1
        )

    got_a = swapped(pick(left, 1 - x, 2), "seq", 1)
    got_b = swapped(pick(right, 1 - y, 1), "seq", 2)
    sum_a = pick(left, x, 2).astype(f32) + got_a.astype(f32)
    sum_b = pick(right, y, 1).astype(f32) + got_b.astype(f32)
    got_a = swapped(to_low(take(sum_a, 1 - y, 1)), "seq", 2)
    got_b = swapped(to_low(take(sum_b, 1 - x, 1)), "seq", 1)
    sum_a = take(sum_a, y, 1) + got_a.astype(f32)
    sum_b = take(sum_b, x, 1) + got_b.astype(f32)
    return z_sum(jnp.concatenate([sum_a, sum_b], axis=-1))


def scatter_feed(parts):
    if not small_mesh():
        low = jnp.concatenate(parts, axis=1)
        return lax.psum_scatter(low, ("dp", "seq"), scatter_dimension=0, tiled=True).astype(f32)
    rows = parts[0].shape[0] // 16
    sums = [
        lax.psum_scatter(
            p.reshape(4, 4, rows, p.shape[1]), "seq", scatter_dimension=1, tiled=True
        )[:, 0]
        for p in parts
    ]
    return z_sum(jnp.concatenate(sums, axis=-1))


def adam_step(weight, gradient, first_old, second_old, factor, step_rate, decay_coef):
    clipped = gradient * factor
    first_new = beta_one * first_old + (1.0 - beta_one) * clipped
    second_new = beta_two * second_old + (1.0 - beta_two) * clipped * clipped
    first_hat = first_new / (1.0 - beta_one**STEP)
    second_hat = second_new / (1.0 - beta_two**STEP)
    weight_new = weight - step_rate * (
        first_hat / (jnp.sqrt(second_hat) + adam_eps) + decay_coef * weight
    )
    return (weight_new, first_new, second_new)


def call(kernel, grid, ins, outs, args, scratch=(), prefetch=0):
    specs = [
        i if isinstance(i, pl.BlockSpec) else pl.BlockSpec(i[0], i[1]) for i in ins
    ]
    return pl.pallas_call(
        kernel,
        out_shape=[jax.ShapeDtypeStruct(o[2], o[3]) for o in outs],
        grid_spec=pltpu.PrefetchScalarGridSpec(
            num_scalar_prefetch=prefetch,
            grid=grid,
            in_specs=specs,
            out_specs=[pl.BlockSpec(o[0], o[1]) for o in outs],
            scratch_shapes=list(scratch),
        ),
        compiler_params=pltpu.CompilerParams(
            dimension_semantics=("arbitrary",) * len(grid), vmem_limit_bytes=56 << 20
        ),
    )(*args)


def dot(a, b):
    return jnp.dot(a, b, preferred_element_type=f32)


def dot_t(a, b):
    return lax.dot_general(a, b, (((1,), (1,)), ((), ())), preferred_element_type=f32)


def t_dot(a, b):
    return lax.dot_general(a, b, (((0,), (0,)), ((), ())), preferred_element_type=f32)


def rms_factor(z):
    return lax.rsqrt(jnp.mean(z * z, axis=-1, keepdims=True) + norm_eps)


def rms_back(z, gain, grad):
    factor = rms_factor(z)
    scaled = grad * gain
    inner = jnp.mean(scaled * z, axis=-1, keepdims=True)
    return factor * scaled - z * (factor * factor * factor * inner), grad * z * factor


def lane_in_head(shape):
    return lax.broadcasted_iota(jnp.int32, shape, 1)


def rope(z, cos, sin, sign):
    lane = lane_in_head(z.shape)
    lead = lane % HEAD_DIM < HEAD_DIM // 2
    partner = jnp.where(lead, -pltpu.roll(z, PAIR - 32, 1), pltpu.roll(z, 32, 1))
    return z * cos + partner * (sin * sign)


def split_heads(z):
    first = lane_in_head(z.shape) < HEAD_DIM
    zero = jnp.zeros_like(z)
    return jnp.where(first, z, zero), jnp.where(first, zero, z)


def join_heads(a, b):
    return jnp.where(lane_in_head(a.shape) < HEAD_DIM, a, b)


def qkv_kernel(x_ref, g_ref, w_ref, cos_ref, sin_ref, n_ref, q_ref, k_ref, v_ref):
    x = x_ref[...].astype(f32)
    width = q_ref.shape[1]
    normed = to_low(x * rms_factor(x) * g_ref[...])
    n_ref[...] = normed
    cos, sin = cos_ref[...], sin_ref[...]

    def turned(raw):
        return jnp.concatenate(
            [
                to_low(rope(raw[:, c : c + PAIR], cos, sin, 1.0))
                for c in range(0, width, PAIR)
            ],
            axis=1,
        )

    k_ref[...] = turned(dot(normed, w_ref[:, width : 2 * width]))
    v_ref[...] = to_low(dot(normed, w_ref[:, 2 * width : 3 * width]))

    @pl.when(pl.program_id(0) == pl.num_programs(0) - 1)
    def _():
        q_ref[...] = turned(dot(normed, w_ref[:, :width]))


def qkv_call(x_ext, gain, w, cos, sin, span, width):
    rows, model = x_ext.shape
    steps = rows // span
    row = lambda i: (i, 0)
    fix = lambda i: (0, 0)
    return call(
        qkv_kernel,
        (steps,),
        [
            ((span, model), row),
            ((1, model), fix),
            ((model, 3 * width), fix),
            ((span, PAIR), row),
            ((span, PAIR), row),
        ],
        [
            ((span, model), row, (rows, model), bf16),
            ((span, width), fix, (span, width), bf16),
            ((span, width), row, (rows, width), bf16),
            ((span, width), row, (rows, width), bf16),
        ],
        (x_ext, gain, w, cos, sin),
    )


def self_bias(segq_ref, segk_ref, bias_ref):
    keys, span = bias_ref.shape
    key_pos = lax.broadcasted_iota(jnp.int32, (keys, span), 0) - (keys - span)
    query_pos = lax.broadcasted_iota(jnp.int32, (keys, span), 1)
    ok = jnp.logical_and(key_pos <= query_pos, segk_ref[...] == segq_ref[...])
    bias_ref[...] = jnp.where(ok, 0.0, masked_fill)


def self_kernel(q_ref, k_ref, v_ref, segq_ref, segk_ref, w_ref, o_ref, lse_ref, part_ref, bias_ref):
    @pl.when(pl.program_id(0) == 0)
    def _():
        self_bias(segq_ref, segk_ref, bias_ref)
        part_ref[...] = jnp.zeros_like(part_ref)

    k, v, bias = k_ref[...], v_ref[...], bias_ref[...]
    outs, lses = [], []
    for qh in split_heads(q_ref[...] * score_scale):
        s = dot_t(k, qh) + bias
        top = jnp.max(s, axis=0, keepdims=True)
        e = jnp.exp(s - top)
        total = jnp.sum(e, axis=0, keepdims=True)
        lses.append(top + jnp.log(total))
        outs.append(t_dot(to_low(e * (1.0 / total)), v))
    o = to_low(join_heads(outs[0], outs[1]))
    o_ref[...] = o
    lse_ref[0] = jnp.concatenate(lses, axis=0)
    part_ref[...] += dot_t(o, w_ref[...])


def self_call(q, k, v, segq, segk, w_att, at, model):
    span, width = q.shape
    keys = k.shape[0]
    pair = lambda p: (0, p)
    fix = lambda p: (0, 0)
    return call(
        self_kernel,
        (width // PAIR,),
        [
            ((span, PAIR), pair),
            ((keys, PAIR), pair),
            ((keys, PAIR), pair),
            ((1, span), fix),
            ((keys, 1), fix),
            ((model, PAIR), lambda p: (0, at + p)),
        ],
        [
            ((span, PAIR), pair, (span, width), bf16),
            ((1, 2, span), lambda p: (p, 0, 0), (width // PAIR, 2, span), f32),
            ((span, model), fix, (span, model), f32),
        ],
        (q, k, v, segq, segk, w_att),
        scratch=[pltpu.VMEM((keys, span), f32)],
    )


def block_bias(len_ref, block, rows):
    lane = lax.broadcasted_iota(jnp.int32, (rows, KEYS), 1)
    limit = jnp.where(lane < NEIGH_LEN, len_ref[block, 0], len_ref[block, 1])
    return jnp.where(lane % NEIGH_LEN < limit, 0.0, masked_fill)


def tile_bias(len_ref, tile, tiles):
    if tile:
        return block_bias(len_ref, tile, BLOCK)
    row = lax.broadcasted_iota(jnp.int32, (BLOCK, KEYS), 0)
    lead = jnp.where(row > 0, block_bias(len_ref, 0, BLOCK), masked_fill)
    last = jnp.where(row > 0, masked_fill, block_bias(len_ref, tiles, BLOCK))
    return jnp.concatenate([lead, last], axis=1)


def tile_keys(ref, tile, tiles):
    own = ref[tile * KEYS : (tile + 1) * KEYS, :]
    if tile:
        return own
    return jnp.concatenate([own, ref[tiles * KEYS : (tiles + 1) * KEYS, :]], axis=0)


def cross_kernel(
    len_ref, x_ref, pa_ref, pb_ref, g_ref, wq_ref, k_ref, v_ref, keep_ref, wo_ref,
    h_ref, n_ref, q_ref, o_ref, lse_ref, part_ref, acc_ref,
):
    span = x_ref.shape[0]
    tiles = span // BLOCK

    @pl.when(pl.program_id(0) == 0)
    def _():
        h = x_ref[...].astype(f32) + (pa_ref[...] + pb_ref[...])
        h_ref[...] = h
        n_ref[...] = to_low(h * rms_factor(h) * g_ref[...])
        part_ref[...] = jnp.zeros_like(part_ref)

    turned = pltpu.roll(to_low(dot(n_ref[...], wq_ref[...])).astype(f32), 1, 0)
    q = to_low(turned * score_scale)
    q_ref[...] = q
    for tile in range(tiles):
        rows = slice(tile * BLOCK, (tile + 1) * BLOCK)
        k, v = tile_keys(k_ref, tile, tiles), tile_keys(v_ref, tile, tiles)
        bias = tile_bias(len_ref, tile, tiles)
        outs, lses = [], []
        for qh in split_heads(q[rows]):
            s = dot_t(qh, k) + bias
            top = jnp.max(s, axis=1, keepdims=True)
            e = jnp.exp(s - top)
            total = jnp.sum(e, axis=1, keepdims=True)
            lses.append(top + jnp.log(total))
            outs.append(dot(to_low(e * (1.0 / total)), v))
        acc_ref[rows, :] = join_heads(outs[0], outs[1])
        lse_ref[rows, :] = join_heads(
            jnp.broadcast_to(lses[0], (BLOCK, PAIR)), jnp.broadcast_to(lses[1], (BLOCK, PAIR))
        )
    o = to_low(pltpu.roll(acc_ref[...] * keep_ref[...], span - 1, 0))
    o_ref[...] = o
    part_ref[...] += dot_t(o, wo_ref[...])


def cross_call(lens, x, pa, pb, gain, w_att, at_q, at_o, kv2, keep):
    span, model = x.shape
    keys, width = kv2.shape[0], kv2.shape[1] // 2
    pairs = width // PAIR
    pair = lambda p, *_: (0, p)
    fix = lambda p, *_: (0, 0)
    return call(
        cross_kernel,
        (pairs,),
        [
            ((span, model), fix),
            ((span, model), fix),
            ((span, model), fix),
            ((1, model), fix),
            ((model, PAIR), lambda p, *_: (0, at_q + p)),
            ((keys, PAIR), pair),
            ((keys, PAIR), lambda p, *_: (0, pairs + p)),
            ((span, 1), fix),
            ((model, PAIR), lambda p, *_: (0, at_o + p)),
        ],
        [
            ((span, model), fix, (span, model), f32),
            ((span, model), fix, (span, model), bf16),
            ((span, PAIR), pair, (span, width), bf16),
            ((span, PAIR), pair, (span, width), bf16),
            ((span, PAIR), pair, (span, width), f32),
            ((span, model), fix, (span, model), f32),
        ],
        (lens, x, pa, pb, gain, w_att, kv2, kv2, keep, w_att),
        scratch=[pltpu.VMEM((span, PAIR), f32)],
        prefetch=1,
    )


def feed_kernel(h1_ref, pa_ref, pb_ref, g_ref, cot_ref, up_ref, down_ref,
                h_ref, n_ref, act_ref, du_ref, y_ref, dn_ref):
    @pl.when(pl.program_id(0) == 0)
    def _():
        h = h1_ref[...] + (pa_ref[...] + pb_ref[...])
        h_ref[...] = h
        n_ref[...] = to_low(h * rms_factor(h) * g_ref[...])
        y_ref[...] = jnp.zeros_like(y_ref)
        dn_ref[...] = jnp.zeros_like(dn_ref)

    up, down = up_ref[...], down_ref[...]
    u = dot(n_ref[...], up)
    t = jnp.tanh(gelu_c * (u + gelu_k * (u * u * u)))
    act = to_low(0.5 * u * (1.0 + t))
    slope = 0.5 * (1.0 + t) + 0.5 * u * (1.0 - t * t) * (gelu_c * (1.0 + 3.0 * gelu_k * (u * u)))
    du = to_low(dot(cot_ref[...], down) * slope)
    act_ref[...] = act
    du_ref[...] = du
    y_ref[...] += dot_t(act, down)
    dn_ref[...] += dot_t(du, up)


def feed_call(h1, pa, pb, gain, cot, w_feed, hidden):
    span, model = h1.shape
    steps = hidden // CHUNK
    fix = lambda c: (0, 0)
    col = lambda c: (0, c)
    return call(
        feed_kernel,
        (steps,),
        [
            ((span, model), fix),
            ((span, model), fix),
            ((span, model), fix),
            ((1, model), fix),
            ((span, model), fix),
            ((model, CHUNK), col),
            ((model, CHUNK), lambda c: (0, steps + c)),
        ],
        [
            ((span, model), fix, (span, model), f32),
            ((span, model), fix, (span, model), bf16),
            ((span, CHUNK), col, (span, hidden), bf16),
            ((span, CHUNK), col, (span, hidden), bf16),
            ((span, model), fix, (span, model), f32),
            ((span, model), fix, (span, model), f32),
        ],
        (h1, pa, pb, gain, cot, w_feed, w_feed),
    )


def cross_back_kernel(
    len_ref, base_ref, h_ref, da_ref, db_ref, g_ref, wo_ref, q_ref, k_ref, v_ref, lse_ref,
    keep_ref, wq_ref,
    grad_ref, low_ref, gain_ref, dq_ref, dk_ref, dv_ref, dn_ref, acc_ref,
):
    span = h_ref.shape[0]
    tiles = span // BLOCK

    @pl.when(pl.program_id(0) == 0)
    def _():
        back, gains = rms_back(h_ref[...], g_ref[...], da_ref[...] + db_ref[...])
        grad = base_ref[...].astype(f32) + back
        grad_ref[...] = grad
        low_ref[...] = to_low(grad)
        gain_ref[...] = jnp.sum(gains, axis=0, keepdims=True)
        dn_ref[...] = jnp.zeros_like(dn_ref)

    do = to_low(dot(low_ref[...], wo_ref[...])).astype(f32)
    do = to_low(pltpu.roll(do, 1, 0) * keep_ref[...])
    q = q_ref[...]
    for tile in range(tiles):
        rows = slice(tile * BLOCK, (tile + 1) * BLOCK)
        k, v = tile_keys(k_ref, tile, tiles), tile_keys(v_ref, tile, tiles)
        bias = tile_bias(len_ref, tile, tiles)
        dqs, scores, probs = [], [], []
        qs, dos = split_heads(q[rows]), split_heads(do[rows])
        for h in range(2):
            p = jnp.exp(dot_t(qs[h], k) + bias - lse_ref[rows, h * HEAD_DIM : h * HEAD_DIM + 1])
            dp = dot_t(dos[h], v)
            ds = to_low(p * (dp - jnp.sum(p * dp, axis=1, keepdims=True)))
            dqs.append(dot(ds, k))
            scores.append(ds)
            probs.append(to_low(p))
        acc_ref[rows, :] = join_heads(dqs[0], dqs[1])
        dk = to_low(t_dot(scores[0], qs[0]) + t_dot(scores[1], qs[1]))
        dv = to_low(t_dot(probs[0], dos[0]) + t_dot(probs[1], dos[1]))
        own = slice(tile * KEYS, (tile + 1) * KEYS)
        dk_ref[own, :] = dk[:KEYS]
        dv_ref[own, :] = dv[:KEYS]
        if not tile:
            last = slice(tiles * KEYS, (tiles + 1) * KEYS)
            dk_ref[last, :] = dk[KEYS:]
            dv_ref[last, :] = dv[KEYS:]
    dq = to_low(pltpu.roll(acc_ref[...] * score_scale, span - 1, 0))
    dq_ref[...] = dq
    dn_ref[...] += dot_t(dq, wq_ref[...])


def cross_back_call(lens, base, h, da, db, gain, w_att, at_q, at_o, q, kv2, lse, keep):
    span, model = h.shape
    keys, width = kv2.shape[0], kv2.shape[1] // 2
    pairs = width // PAIR
    pair = lambda p, *_: (0, p)
    fix = lambda p, *_: (0, 0)
    return call(
        cross_back_kernel,
        (pairs,),
        [
            ((span, model), fix),
            ((span, model), fix),
            ((span, model), fix),
            ((span, model), fix),
            ((1, model), fix),
            ((model, PAIR), lambda p, *_: (0, at_o + p)),
            ((span, PAIR), pair),
            ((keys, PAIR), pair),
            ((keys, PAIR), lambda p, *_: (0, pairs + p)),
            ((span, PAIR), pair),
            ((span, 1), fix),
            ((model, PAIR), lambda p, *_: (0, at_q + p)),
        ],
        [
            ((span, model), fix, (span, model), f32),
            ((span, model), fix, (span, model), bf16),
            ((1, model), fix, (1, model), f32),
            ((span, PAIR), pair, (span, width), bf16),
            ((keys, PAIR), pair, (keys, width), bf16),
            ((keys, PAIR), pair, (keys, width), bf16),
            ((span, model), fix, (span, model), f32),
        ],
        (lens, base, h, da, db, gain, w_att, q, kv2, kv2, lse, keep, w_att),
        scratch=[pltpu.VMEM((span, PAIR), f32)],
        prefetch=1,
    )


def self_back_kernel(
    base_ref, h_ref, da_ref, db_ref, g_ref, w_ref, q_ref, k_ref, v_ref, lse_ref, segq_ref,
    segk_ref, cos_ref, sin_ref,
    grad_ref, low_ref, gain_ref, dq_ref, dk_ref, dv_ref, bias_ref,
):
    span = h_ref.shape[0]
    keys = k_ref.shape[0]

    @pl.when(pl.program_id(0) == 0)
    def _():
        back, gains = rms_back(h_ref[...], g_ref[...], da_ref[...] + db_ref[...])
        grad = base_ref[...] + back
        grad_ref[...] = grad
        low_ref[...] = to_low(grad)
        gain_ref[...] = jnp.sum(gains, axis=0, keepdims=True)
        self_bias(segq_ref, segk_ref, bias_ref)

    do = to_low(dot(low_ref[...], w_ref[...]))
    k, v, bias = k_ref[...], v_ref[...], bias_ref[...]
    qs, dos = split_heads(q_ref[...] * score_scale), split_heads(do)
    dqs, dk, dv = [], 0.0, 0.0
    for h in range(2):
        p = jnp.exp(dot_t(k, qs[h]) + bias - lse_ref[0, h : h + 1, :])
        dp = dot_t(v, dos[h])
        ds = to_low(p * (dp - jnp.sum(p * dp, axis=0, keepdims=True)))
        dqs.append(t_dot(ds, k))
        dk = dk + dot(ds, qs[h])
        dv = dv + dot(to_low(p), dos[h])
    cos, sin = cos_ref[...], sin_ref[...]
    dq = join_heads(dqs[0], dqs[1]) * score_scale
    dq_ref[...] = to_low(rope(dq, cos[keys - span :], sin[keys - span :], -1.0))
    dk_ref[...] = to_low(rope(dk, cos, sin, -1.0))
    dv_ref[...] = to_low(dv)


def self_back_call(base, h, da, db, gain, w_att, at, q, k, v, lse, segq, segk, cos, sin):
    span, model = h.shape
    keys, width = k.shape
    pair = lambda p: (0, p)
    fix = lambda p: (0, 0)
    return call(
        self_back_kernel,
        (width // PAIR,),
        [
            ((span, model), fix),
            ((span, model), fix),
            ((span, model), fix),
            ((span, model), fix),
            ((1, model), fix),
            ((model, PAIR), lambda p: (0, at + p)),
            ((span, PAIR), pair),
            ((keys, PAIR), pair),
            ((keys, PAIR), pair),
            ((1, 2, span), lambda p: (p, 0, 0)),
            ((1, span), fix),
            ((keys, 1), fix),
            ((keys, PAIR), fix),
            ((keys, PAIR), fix),
        ],
        [
            ((span, model), fix, (span, model), f32),
            ((span, model), fix, (span, model), bf16),
            ((1, model), fix, (1, model), f32),
            ((span, PAIR), pair, (span, width), bf16),
            ((keys, PAIR), pair, (keys, width), bf16),
            ((keys, PAIR), pair, (keys, width), bf16),
        ],
        (base, h, da, db, gain, w_att, q, k, v, lse, segq, segk, cos, sin),
        scratch=[pltpu.VMEM((keys, span), f32)],
    )


def inner_kernel(x_ref, dq_ref, dk_ref, dv_ref, w_ref, dn_ref, gain_ref):
    step = pl.program_id(0)
    last = pl.num_programs(0) - 1
    width = dk_ref.shape[1]

    @pl.when(step == 0)
    def _():
        gain_ref[...] = jnp.zeros_like(gain_ref)

    dn_ref[...] = dot_t(dk_ref[...], w_ref[:, width : 2 * width]) + dot_t(
        dv_ref[...], w_ref[:, 2 * width : 3 * width]
    )

    @pl.when(step == last)
    def _():
        dn_ref[...] += dot_t(dq_ref[...], w_ref[:, :width])

    x = x_ref[...].astype(f32)
    gain_ref[...] += jnp.sum(dn_ref[...] * x * rms_factor(x), axis=0, keepdims=True)


def inner_call(x_ext, dq, dk, dv, w):
    rows, model = x_ext.shape
    span, width = dq.shape
    row = lambda i: (i, 0)
    fix = lambda i: (0, 0)
    return call(
        inner_kernel,
        (rows // span,),
        [
            ((span, model), row),
            ((span, width), fix),
            ((span, width), row),
            ((span, width), row),
            ((model, 3 * width), fix),
        ],
        [
            ((span, model), row, (rows, model), f32),
            ((1, model), fix, (1, model), f32),
        ],
        (x_ext, dq, dk, dv, w),
    )


def adam_kernel(factor_ref, w_ref, g_ref, m_ref, v_ref, wo_ref, mo_ref, vo_ref):
    wo_ref[0], mo_ref[0], vo_ref[0] = adam_step(
        w_ref[0], g_ref[...], m_ref[0], v_ref[0], factor_ref[0], learn_rate, weight_decay
    )


def adam_call(factor, weights, grads, first, second, order):
    count, rows, width = weights.shape
    each = lambda j, *_: (j, 0, 0)
    block = ((1, rows, width), each)
    out = ((1, rows, width), each, weights.shape, f32)
    return call(
        adam_kernel,
        (count,),
        [block, ((rows, width), lambda j, *_: (0, order(j))), block, block],
        [out, out, out],
        (factor, weights, grads, first, second),
        prefetch=1,
    )


def rows_kernel(a_ref, w_ref, o_ref):
    o_ref[...] = to_low(dot(a_ref[...], w_ref[...]))


def rows_call(a, w, width):
    rows, model = a.shape
    return call(
        rows_kernel,
        (rows // KEYS,),
        [((KEYS, model), lambda i: (i, 0)), ((model, width), lambda i: (0, 0))],
        [((KEYS, width), lambda i: (i, 0), (rows, width), bf16)],
        (a, w),
    )[0]


def per_device(
    tokens,
    neighbours,
    neighbour_lengths,
    segment_ids,
    out_grad,
    self_weights,
    cross_weights,
    feed_weights,
    norm_gains,
    self_first,
    cross_first,
    feed_first,
    gains_first,
    self_second,
    cross_second,
    feed_second,
    gains_second,
):
    row_count, span, model = tokens.shape
    width = self_weights.shape[2]
    hidden = feed_weights.shape[2]
    shard_rows = self_weights.shape[1]
    pairs = width // PAIR
    blocks = span // BLOCK
    halo = min(-(-(DOC_MAX - 1) // span), lax.axis_size("seq") - 1)
    s_index = lax.axis_index("seq")
    core = lax.axis_index("mp")

    def columns(*parts):
        return jnp.concatenate([to_low(p) for p in parts], axis=1)

    gain_cols = jnp.zeros((shard_rows, 128), f32).at[:, :3].set(norm_gains.T)
    full_feed = lax.all_gather(
        columns(feed_weights[0], feed_weights[1]), ("dp", "seq"), axis=0, tiled=True
    )
    full_qkv = gather_rows(columns(self_weights[0], self_weights[1], self_weights[2], gain_cols))
    full_att = gather_rows(
        columns(cross_weights[1], cross_weights[2], self_weights[3], cross_weights[0], cross_weights[3])
    )
    at_so, at_cq, at_co = 2 * pairs, 3 * pairs, 4 * pairs
    gains = full_qkv[:, 3 * width : 3 * width + 3].T.astype(f32)

    x = tokens.reshape(span, model)
    flat = neighbours.reshape(-1, model)
    half = span // 2
    pad = KEYS // 2
    mine = lax.dynamic_slice_in_dim(x, core * half, half, 0)
    edge = lax.dynamic_slice_in_dim(flat, flat.shape[0] - KEYS + core * pad, pad, 0)
    got = shifted(jnp.concatenate([mine, edge], axis=0), "seq", 1)
    far = [shifted(mine, "seq", k) for k in range(2, halo + 1)]
    got = jnp.concatenate([got] + far, axis=0)
    other = swapped(got, "mp", 1)
    low_half = jnp.where(core == 0, got, other)
    high_half = jnp.where(core == 0, other, got)

    def whole(start, size):
        return [low_half[start : start + size], high_half[start : start + size]]

    pieces = []
    for k in range(halo, 1, -1):
        pieces += whole(half + pad + (k - 2) * half, half)
    x_ext = jnp.concatenate(pieces + whole(0, half) + [x], axis=0)
    flat_ext = jnp.concatenate(whole(half, pad) + [flat], axis=0)

    seg_here = segment_ids.reshape(1, span) + 1
    lengths = neighbour_lengths.reshape(blocks, NEIGHBOURS)
    ints = jnp.concatenate([seg_here[0], lengths[-1]])[None]
    ints_prev = [shifted(ints, "seq", k) for k in range(1, halo + 1)]
    seg_keys = jnp.concatenate([p[:, :span] for p in ints_prev[::-1]] + [seg_here], axis=1)
    seg_keys = seg_keys.reshape(-1, 1)
    lens = jnp.concatenate([ints_prev[0][:, span:], lengths], axis=0)
    before = jnp.concatenate([ints_prev[0][0, span - 1 : span], seg_here[0, : span - 1]])
    heads_of = jnp.repeat(before[::BLOCK], BLOCK)
    keep = (before == heads_of).at[0].set(True)
    valid_from = jnp.where(s_index == 0, BLOCK, 0)
    spot = jnp.arange(span)
    keep = jnp.where(jnp.logical_or(spot == 0, spot >= valid_from), keep, False)
    keep = keep.astype(f32).reshape(span, 1)

    frequency = rope_base ** (-(jnp.arange(PAIR) % (HEAD_DIM // 2)).astype(f32) / (HEAD_DIM // 2))
    places = (s_index - halo) * span + jnp.arange((halo + 1) * span)
    angles = places.astype(f32)[:, None] * frequency[None, :]
    cos, sin = jnp.cos(angles), jnp.sin(angles)

    n1, q, k, v = qkv_call(x_ext, gains[:1], full_qkv, cos, sin, span, width)
    attn, lse, part = self_call(q, k, v, seg_here, seg_keys, full_att, at_so, model)
    kv2 = rows_call(flat_ext, full_att, 2 * width)
    h1, n2, q2, cross, lse2, part2 = cross_call(
        lens, x, part, swapped(part, "mp", 1), gains[1:2], full_att, at_cq, at_co, kv2, keep
    )
    cot = out_grad.reshape(span, model)
    h2, n3, act, du, y, dn3 = feed_call(
        h1, part2, swapped(part2, "mp", 1), gains[2:3], cot, full_feed, hidden
    )
    out = to_low(h2 + core_sum(y)).reshape(row_count, span, model)
    feed_part = scatter_feed([to_low(t_dot(n3, du)), to_low(t_dot(cot, act))])
    g2, low2, dgain3, dq2, dk2, dv2, dn2 = cross_back_call(
        lens, cot, h2, dn3, swapped(dn3, "mp", 1), gains[2:3], full_att, at_cq, at_co,
        q2, kv2, lse2, keep,
    )
    cross_part = scatter_rows(
        [to_low(t_dot(n2, dq2)), to_low(t_dot(low2, cross))],
        [to_low(t_dot(flat_ext, dk2)), to_low(t_dot(flat_ext, dv2))],
    )
    g1, low1, dgain2, dq, dk, dv = self_back_call(
        g2, h1, dn2, swapped(dn2, "mp", 1), gains[1:2], full_att, at_so,
        q, k, v, lse, seg_here, seg_keys, cos, sin,
    )
    self_part = scatter_rows(
        [to_low(t_dot(n1[halo * span :], dq)), to_low(t_dot(low1, attn))],
        [to_low(t_dot(n1, dk)), to_low(t_dot(n1, dv))],
    )
    dn1, dgain1 = inner_call(x_ext, dq, dk, dv, full_qkv)
    own = dn1[halo * span :]
    for k_off in range(1, halo + 1):
        start = (halo - k_off) * span
        own = own + shifted(to_low(dn1[start : start + span]), "seq", -k_off).astype(f32)
    back, _ = rms_back(x.astype(f32), gains[:1], core_sum(own))
    in_grad = (g1 + back).reshape(row_count, span, model)

    gain_grads = butterfly(
        jnp.concatenate([dgain1, 0.5 * dgain2, 0.5 * dgain3], axis=0), ("mp", "seq", "dp")
    )
    shard = lax.axis_index("dp") * lax.axis_size("seq") + s_index
    gains_part = lax.dynamic_slice_in_dim(gain_grads, shard * shard_rows, shard_rows, axis=1)
    first_model = (core == 0).astype(f32)
    local_squares = (
        jnp.sum(self_part * self_part)
        + jnp.sum(cross_part * cross_part)
        + jnp.sum(feed_part * feed_part)
        + first_model * jnp.sum(gains_part * gains_part)
    )
    grad_norm = jnp.sqrt(butterfly(local_squares.reshape(1, 1), ("mp", "seq", "dp")).reshape(()))
    factor = jnp.minimum(1.0, clip_limit / (grad_norm + 1e-06))
    scalar = factor.reshape(1)
    mixed = lambda j: jnp.where(j == 0, 0, jnp.where(j == 3, 1, j + 1))
    plain = lambda j: j
    self_new, self_first_new, self_second_new = adam_call(
        scalar, self_weights, self_part, self_first, self_second, mixed
    )
    cross_new, cross_first_new, cross_second_new = adam_call(
        scalar, cross_weights, cross_part, cross_first, cross_second, mixed
    )
    feed_new, feed_first_new, feed_second_new = adam_call(
        scalar, feed_weights, feed_part, feed_first, feed_second, plain
    )
    gains_new, gains_first_new, gains_second_new = adam_step(
        norm_gains, gains_part, gains_first, gains_second, factor, gain_rate, 0.0
    )
    return (
        out,
        in_grad,
        grad_norm,
        self_new,
        cross_new,
        feed_new,
        gains_new,
        self_first_new,
        cross_first_new,
        feed_first_new,
        gains_first_new,
        self_second_new,
        cross_second_new,
        feed_second_new,
        gains_second_new,
    )


def solution(mesh):
    tok = P("dp", "seq", None)
    mat = P(None, ("dp", "seq"), "mp")
    vec = P(None, ("dp", "seq"))
    in_specs = (
        tok,
        P("dp", "seq", None, None, None),
        tok,
        P("dp", "seq"),
        tok,
    ) + (mat, mat, mat, vec) * 3
    out_specs = (tok, tok, P()) + (mat, mat, mat, vec) * 3
    return jax.shard_map(
        per_device, mesh=mesh, in_specs=in_specs, out_specs=out_specs, check_vma=False
    )
```

time: 639 us -> 516 us (0.81)
  local copies, waits for them, and re-layouts: 154 us -> 53.2 us
  Pallas kernels: 0 us -> 100 us
  starting transfers between devices: 161 us -> 103 us
  matrix products: 62.9 us -> 10.6 us
  other arithmetic: 67 us -> 40.2 us
  between operations: 10.3 us -> 21.8 us
  waiting for transfers between devices: 175 us -> 184 us
    pallas_call x0 -> x11, Pallas kernels: none -> 100 us  [call(): pl.pallas_call(kernel, out_shape=[jax.ShapeDtypeStruct(o[2], o[3]) for o...]
    dot_general x33 -> x10, matrix products: 62.9 us -> 10.6 us  [t_dot(): lax.dot_general(a, b, (((0,), (0,)), ((), ())), preferred_element_type=f32)]
    ppermute x27 -> x15, starting transfers between devices: 59.5 us -> 32 us  [rotated(): lax.ppermute(value, axis, [(i, (i + by) % count) for i in range(count)])]
    dynamic_update_slice x41 -> x17, local copies, waits for them, and re-layouts: 41.2 us -> 18.2 us  [put(): return lax.dynamic_update_slice(buffer, piece, starts)]
    ppermute x51 -> x33, starting transfers between devices: 78.3 us -> 56 us  [swapped(): return lax.ppermute(value, axis, [(i, i ^ by) for i in range(count)])]
    slice x24 -> x13, local copies, waits for them, and re-layouts: 28.3 us -> 8.16 us  [the longest x2 3.3 us: per_device(): n1, q, k, v = qkv_call(x_ext, gains[:1], full_qkv, cos, sin, span, width)]
    ppermute x27 -> x15, waiting for transfers between devices: 40 us -> 54.1 us  [rotated(): lax.ppermute(value, axis, [(i, (i + by) % count) for i in range(count)])]
    ppermute x51 -> x33, waiting for transfers between devices: 117 us -> 104 us  [swapped(): return lax.ppermute(value, axis, [(i, i ^ by) for i in range(count)])]
  transfers between devices with their start and end apart: 86 -> 57, of which waited for: 32 -> 24; matrix products, arithmetic and copies ran while one was open for 39% -> 17% of each run, Pallas kernels for 0% -> 15%
where the time goes in v2:
time: 516 us; the launch traced here: 513 us
  waiting for transfers between devices  184 us (36%)
  starting transfers between devices  103 us (20%)
  Pallas kernels  100 us (19%)
  local copies, waits for them, and re-layouts  53.2 us (10%)
  other arithmetic  40.2 us (8%)
  between operations  21.8 us (4%)
  matrix products  10.6 us (2%)
    ppermute x33, waiting for transfers between devices, swapped(): return lax.ppermute(value, axis, [(i, i ^ by) for i in range(count)])  104 us
    pallas_call x11, Pallas kernels, call(): pl.pallas_call(kernel, out_shape=[jax.ShapeDtypeStruct(o[2], o[3]) for o...  100 us
    ppermute x33, starting transfers between devices, swapped(): return lax.ppermute(value, axis, [(i, i ^ by) for i in range(count)])  56 us
    ppermute x15, waiting for transfers between devices, rotated(): lax.ppermute(value, axis, [(i, (i + by) % count) for i in range(count)])  54.1 us
    ppermute x15, starting transfers between devices, rotated(): lax.ppermute(value, axis, [(i, (i + by) % count) for i in range(count)])  32 us
    ppermute x6, waiting for transfers between devices, shifted(): lax.ppermute(value, axis, [(i, i + by) for i in range(count) if 0 <= i +...  25.5 us
    dynamic_update_slice x17, local copies, waits for them, and re-layouts, put(): return lax.dynamic_update_slice(buffer, piece, starts)  18.2 us
    ppermute x6, starting transfers between devices, shifted(): lax.ppermute(value, axis, [(i, i + by) for i in range(count) if 0 <= i +...  15.4 us
  transfers between devices with their start and end apart: 57, of which 24 were waited for; matrix products, arithmetic and copies ran while one was open for 17% of the time, Pallas kernels for 15%

profile of v2, /device:TPU:0, one launch (start us, length us, event | category | flops | bytes accessed | tf_op | source)
XLA Modules:
  0.0 513.5 jit_solution(7846189731927327922)
XLA Ops:
  12.6 3.0 collective-permute-start.12
  15.6 2.6 collective-permute-start.13
  18.4 3.4 collective-permute-start
  21.8 3.4 collective-permute-start.11
  34.1 2.5 multiply_sine_fusion
  36.6 1.8 pad_maximum_fusion.7
  38.4 3.6 collective-permute-start.14
  42.1 2.0 collective-permute-start.2
  45.6 6.1 %collective-permute-start.5 = (bf16[56,1664]{1,0:T(8,128)(2,1)S(1)}, bf16[56,1664]{1,0:T(8,128)(2,1)S(1)}, u32[]{:S(2)}, u32[]{:S(2)}) collective-permute-start(bf16[56,1664]{1,0:T(8,128)(2,1)S(1)} %fusion.34), channel_id=1, source_target_pairs={{0,16},{8,24},{16,0},{24,8},{1,17},{9,25},{17,1},{25,9},{2,18},{10... | collective-permute-start | bytes 559112 | tf_op jit(solution)/shard_map/ppermute | solution.py:47
  52.4 11.3 %collective-permute-done.5 = bf16[56,1664]{1,0:T(8,128)(2,1)S(1)} collective-permute-done((bf16[56,1664]{1,0:T(8,128)(2,1)S(1)}, bf16[56,1664]{1,0:T(8,128)(2,1)S(1)}, u32[]{:S(2)}, u32[]{:S(2)}) %collective-permute-start.5) | collective-permute-done | bytes 186400 | tf_op jit(solution)/shard_map/ppermute | solution.py:47
  66.0 10.4 %collective-permute-done.6 = bf16[56,1664]{1,0:T(8,128)(2,1)S(1)} collective-permute-done((bf16[56,1664]{1,0:T(8,128)(2,1)S(1)}, bf16[56,1664]{1,0:T(8,128)(2,1)S(1)}, u32[]{:S(2)}, u32[]{:S(2)}) %collective-permute-start.6) | collective-permute-done | bytes 186400 | tf_op jit(solution)/shard_map/ppermute | solution.py:47
  76.4 3.8 collective-permute-start.1
  82.3 1.8 collective-permute-start.7
  85.8 1.9 collective-permute-start.8
  91.1 2.0 collective-permute-start.15
  96.4 16.4 %collective-permute-done.8 = bf16[4,56,1664]{2,1,0:T(8,128)(2,1)S(1)} collective-permute-done((bf16[4,56,1664]{2,1,0:T(8,128)(2,1)}, bf16[4,56,1664]{2,1,0:T(8,128)(2,1)S(1)}, u32[]{:S(2)}, u32[]{:S(2)}) %collective-permute-start.8) | collective-permute-done | bytes 745504 | tf_op jit(solution)/shard_map/ppermute | solution.py:52
  113.0 3.1 collective-permute-done.7
  116.1 3.3 collective-permute-start.10
  121.4 39.4 %collective-permute-done.9 = bf16[4,56,768]{2,1,0:T(8,128)(2,1)S(1)} collective-permute-done((bf16[4,56,768]{2,1,0:T(8,128)(2,1)S(1)}, bf16[4,56,768]{2,1,0:T(8,128)(2,1)S(1)}, u32[]{:S(2)}, u32[]{:S(2)}) %collective-permute-start.9) | collective-permute-done | bytes 344096 | tf_op jit(solution)/shard_map/ppermute | solution.py:52
  162.5 1.8 copy.145.g_ref
  164.3 7.0 %shard_map.280 = (bf16[768,896]{1,0:T(8,128)(2,1)}, bf16[256,512]{1,0:T(8,128)(2,1)}, bf16[768,512]{1,0:T(8,128)(2,1)}, bf16[768,512]{1,0:T(8,128)(2,1)}) custom-call(bf16[768,896]{1,0:T(8,128)(2,1)} %copy-done.4, f32[1,896]{1,0:T(1,128)} %copy.145.g_ref, bf16[896,1664]{1,0:T(8,128)(2,1)} %bitcast.259, f32[768,128]{1,0:T(8,128)} %get-tuple-element.181.cos_ref, ...), custom_call_target="tpu_custom_call" | custom-call | tf_op jit(solution)/shard_map/pallas_call | solution.py:167
  173.9 1.8 collective-permute-start.18
  175.6 2.4 bitcast_dynamic-update-slice_fusion.1
  178.0 2.4 bitcast_dynamic-update-slice_fusion
  180.4 3.4 collective-permute-done.17
  186.1 10.3 %shard_map.281 = (bf16[256,512]{1,0:T(8,128)(2,1)}, f32[4,2,256]{2,1,0:T(2,128)}, f32[256,896]{1,0:T(8,128)}) custom-call(bf16[256,512]{1,0:T(8,128)(2,1)} %get-tuple-element.82.q_ref, bf16[768,512]{1,0:T(8,128)(2,1)} %get-tuple-element.83.k_ref, bf16[768,512]{1,0:T(8,128)(2,1)} %get-tuple-element.84.v_ref, s32[1,256]{1,0:T(1,128)} %copy-done.36, ...), custom_call_target="tpu_custom_call" | custom-call | tf_op jit(solution)/shard_map/pallas_call | solution.py:167
  202.2 7.0 %shard_map.282.k_ref.v_ref = bf16[1280,1024]{1,0:T(8,128)(2,1)} custom-call(bf16[1280,896]{1,0:T(8,128)(2,1)} %pad_maximum_fusion.a_ref, bf16[896,2560]{1,0:T(8,128)(2,1)} %bitcast.252), custom_call_target="tpu_custom_call" | custom-call | tf_op jit(solution)/shard_map/pallas_call | solution.py:167
  209.2 17.5 %shard_map.283 = (f32[256,896]{1,0:T(8,128)}, bf16[256,896]{1,0:T(8,128)(2,1)}, bf16[256,512]{1,0:T(8,128)(2,1)}, bf16[256,512]{1,0:T(8,128)(2,1)}, f32[256,512]{1,0:T(8,128)}, /*index=5*/f32[256,896]{1,0:T(8,128)}) custom-call(s32[5,2]{1,0:T(8,128)} %pad_add_fusion.len_ref, bf16[256,896]{1,0:T(8,128)(2,1)} %bitcast.263, ...), custom_call_target="tpu_custom_call" | custom-call | tf_op jit(solution)/shard_map/pallas_call | solution.py:167
  230.4 10.9 %shard_map.284 = (f32[256,896]{1,0:T(8,128)}, bf16[256,896]{1,0:T(8,128)(2,1)}, bf16[256,1792]{1,0:T(8,128)(2,1)}, bf16[256,1792]{1,0:T(8,128)(2,1)}, f32[256,896]{1,0:T(8,128)}, /*index=5*/f32[256,896]{1,0:T(8,128)}) custom-call(f32[256,896]{1,0:T(8,128)} %get-tuple-element.86.h1_ref.h_ref, f32[256,896]{1,0:T(8,128)} %get-tuple-element.87.pa_ref, ...), custom_call_target="tpu_custom_call" | custom-call | tf_op jit(solution)/shard_map/pallas_call | solution.py:167
  241.4 2.4 convolution_convert_fusion.1
  243.7 1.8 copy.174
  247.9 1.9 copy.175
  250.3 18.0 %shard_map.285 = (f32[256,896]{1,0:T(8,128)}, bf16[256,896]{1,0:T(8,128)(2,1)}, f32[1,896]{1,0:T(1,128)}, bf16[256,512]{1,0:T(8,128)(2,1)}, bf16[1280,512]{1,0:T...) custom-call(s32[5,2]{1,0:T(8,128)} %pad_add_fusion.len_ref, bf16[256,896]{1,0:T(8,128)(2,1)} %bitcast.265, ...), custom_call_target="tpu_custom_call" | custom-call | tf_op jit(solution)/shard_map/pallas_call | solution.py:167
  277.5 2.2 fusion.9
  280.6 12.1 %shard_map.286 = (f32[256,896]{1,0:T(8,128)}, bf16[256,896]{1,0:T(8,128)(2,1)}, f32[1,896]{1,0:T(1,128)}, bf16[256,512]{1,0:T(8,128)(2,1)}, bf16[768,512]{1,0:T(8,128)(2,1)}, /*index=5*/bf16[768,512]{1,0:T(8,128)(2,1)}) custom-call(f32[256,896]{1,0:T(8,128)} %get-tuple-element.93.base_ref, f32[256,896]{1,0:T(8,128)} %get-tuple-element.86.h1_ref.h_ref, ...), custom_call_target="tpu_custom_call" | custom-call | tf_op jit(solution)/shard_map/pallas_call | solution.py:167
  292.7 6.7 %shard_map.287 = (f32[768,896]{1,0:T(8,128)}, f32[1,896]{1,0:T(1,128)}) custom-call(bf16[768,896]{1,0:T(8,128)(2,1)} %copy-done.4, bf16[256,512]{1,0:T(8,128)(2,1)} %get-tuple-element.97.dq_ref, bf16[768,512]{1,0:T(8,128)(2,1)} %get-tuple-element.98.dk_ref, bf16[768,512]{1,0:T(8,128)(2,1)} %get-tuple-element.99.dv_ref, bf16[896,1664]{1,0:T(8,128)(2,1)} %bitcast.260), custom_call_target="tpu_custom_call" | custom-call | tf_op jit(solution)/shard_map/pallas_call | solution.py:167
  303.7 4.8 collective-permute-done.36
  317.9 15.6 %collective-permute-done.45 = f32[3,896]{1,0:T(4,128)S(1)} collective-permute-done((f32[3,896]{1,0:T(4,128)S(1)}, f32[3,896]{1,0:T(4,128)S(1)}, u32[]{:S(2)}, u32[]{:S(2)}) %collective-permute-start.45) | collective-permute-done | bytes 10784 | tf_op jit(solution)/shard_map/ppermute | solution.py:52
  334.7 2.5 collective-permute-done.46
  337.2 2.5 collective-permute-start.47
  341.4 3.8 collective-permute-start.48
  356.2 20.3 %collective-permute-done.24 = bf16[256,896]{1,0:T(8,128)(2,1)} collective-permute-done((bf16[256,896]{1,0:T(8,128)(2,1)}, bf16[256,896]{1,0:T(8,128)(2,1)}, u32[]{:S(2)}, u32[]{:S(2)}) %collective-permute-start.24) | collective-permute-done | bytes 458784 | tf_op jit(solution)/shard_map/ppermute | solution.py:42
  376.5 3.3 collective-permute-start.39
  379.8 5.1 collective-permute-done.25
  391.1 10.2 %collective-permute-start.30 = (bf16[4,56,1024]{2,1,0:T(8,128)(2,1)S(1)}, bf16[4,56,1024]{2,1,0:T(8,128)(2,1)S(1)}, u32[]{:S(2)}, u32[]{:S(2)}) collective-permute-start(bf16[4,56,1024]{2,1,0:T(8,128)(2,1)S(1)} %fusion.11), channel_id=1, source_target_pairs={{0,2},{2,0},{4,6},{6,4},{1,3},{3,1},{5,7},{7,5},{8,10},{10,8},{12,... | collective-permute-start | bytes 1376264 | tf_op jit(solution)/shard_map/ppermute | solution.py:52
  402.9 9.5 %collective-permute-done.30 = bf16[4,56,1024]{2,1,0:T(8,128)(2,1)S(1)} collective-permute-done((bf16[4,56,1024]{2,1,0:T(8,128)(2,1)S(1)}, bf16[4,56,1024]{2,1,0:T(8,128)(2,1)S(1)}, u32[]{:S(2)}, u32[]{:S(2)}) %collective-permute-start.30) | collective-permute-done | bytes 458784 | tf_op jit(solution)/shard_map/ppermute | solution.py:52
  413.6 2.0 collective-permute-start.31
  415.9 2.4 collective-permute-start.33
  419.6 2.5 fusion.30
  422.1 2.3 collective-permute-start.42
  424.4 1.8 collective-permute-start.43
  427.5 6.7 %collective-permute-done.32 = bf16[56,2048]{1,0:T(8,128)(2,1)} collective-permute-done((bf16[56,2048]{1,0:T(8,128)(2,1)}, bf16[56,2048]{1,0:T(8,128)(2,1)}, u32[]{:S(2)}, u32[]{:S(2)}) %collective-permute-start.32) | collective-permute-done | bytes 229408 | tf_op jit(solution)/shard_map/ppermute | solution.py:47
  434.2 2.7 multiply_reduce_fusion.2
  438.3 4.5 collective-permute-done.41
  442.8 21.0 %collective-permute-done.42 = bf16[56,3584]{1,0:T(8,128)(2,1)} collective-permute-done((bf16[56,3584]{1,0:T(8,128)(2,1)}, bf16[56,3584]{1,0:T(8,128)(2,1)}, u32[]{:S(2)}, u32[]{:S(2)}) %collective-permute-start.42) | collective-permute-done | bytes 401440 | tf_op jit(solution)/shard_map/ppermute | solution.py:47
  463.9 3.0 multiply_reduce_fusion
  469.4 2.9 collective-permute-start.50
  473.7 2.9 collective-permute-start.51
  477.9 10.4 %collective-permute-start.52 = (f32[1,1]{1,0:T(1,128)}, f32[1,1]{1,0:T(1,128)}, u32[]{:S(2)}, u32[]{:S(2)}) collective-permute-start(f32[1,1]{1,0:T(1,128)} %add.415), channel_id=1, source_target_pairs={{0,8},{8,0},{16,24},{24,16},{1,9},{9,1},{17,25},{25,17},{2,10},{10... | collective-permute-start | bytes 20 | tf_op jit(solution)/shard_map/ppermute | solution.py:52
  489.3 2.4 collective-permute-start.53
  491.6 2.2 collective-permute-done.53
  495.2 3.2 shard_map.290
  498.4 3.7 shard_map.289
  502.1 3.7 shard_map.288
  (317 shorter events, 102.4 us)
Async XLA Ops:
  7.2 222.3 %all-gather.2.cloned.1.call-start = ((), (), s32[]{:S(2)}) async-start(), calls=%async_computation.2 | async-start | bytes 6823936 | tf_op jit(solution)/shard_map/all_gather | solution.py:747
  12.6 69.8 %collective-permute-start.12 = (bf16[56,2560]{1,0:T(8,128)(2,1)}, bf16[56,2560]{1,0:T(8,128)(2,1)}, u32[]{:S(2)}, u32[]{:S(2)}) collective-permute-start(bf16[56,2560]{1,0:T(8,128)(2,1)} %fusion.35), channel_id=1, source_target_pairs={{0,8},{8,16},{16,24},{24,0},{1,9},{9,17},{17,25},{25,1},{2,10},{10... | collective-permute-start | bytes 860168 | tf_op jit(solution)/shard_map/ppermute | solution.py:47
  15.6 70.2 %collective-permute-start.13 = (bf16[56,2560]{1,0:T(8,128)(2,1)}, bf16[56,2560]{1,0:T(8,128)(2,1)}, u32[]{:S(2)}, u32[]{:S(2)}) collective-permute-start(bf16[56,2560]{1,0:T(8,128)(2,1)} %fusion.35), channel_id=1, source_target_pairs={{0,16},{8,24},{16,0},{24,8},{1,17},{9,25},{17,1},{25,9},{2,18},{10... | collective-permute-start | bytes 860168 | tf_op jit(solution)/shard_map/ppermute | solution.py:47
  18.4 20.0 %collective-permute-start = (s32[1,258]{1,0:T(1,128)S(1)}, s32[1,258]{1,0:T(1,128)S(1)}, u32[]{:S(2)}, u32[]{:S(2)}) collective-permute-start(s32[1,258]{1,0:T(1,128)S(1)} %broadcast_in_dim.81), channel_id=1, source_target_pairs={{0,2},{2,4},{4,6},{1,3},{3,5},{5,7},{8,10},{10,12},{12,14},{9,11},... | collective-permute-start | bytes 3104 | tf_op jit(solution)/shard_map/ppermute | solution.py:42
  21.8 20.3 %collective-permute-start.11 = (s32[1,258]{1,0:T(1,128)S(1)}, s32[1,258]{1,0:T(1,128)S(1)}, u32[]{:S(2)}, u32[]{:S(2)}) collective-permute-start(s32[1,258]{1,0:T(1,128)S(1)} %broadcast_in_dim.81), channel_id=1, source_target_pairs={{0,4},{2,6},{1,5},{3,7},{8,12},{10,14},{9,13},{11,15},{16,20},{18,... | collective-permute-start | bytes 3104 | tf_op jit(solution)/shard_map/ppermute | solution.py:42
  26.7 18.9 %collective-permute-start.4 = (bf16[56,1664]{1,0:T(8,128)(2,1)S(1)}, bf16[56,1664]{1,0:T(8,128)(2,1)S(1)}, u32[]{:S(2)}, u32[]{:S(2)}) collective-permute-start(bf16[56,1664]{1,0:T(8,128)(2,1)S(1)} %fusion.34), channel_id=1, source_target_pairs={{0,8},{8,16},{16,24},{24,0},{1,9},{9,17},{17,25},{25,1},{2,10},{10... | collective-permute-start | bytes 559112 | tf_op jit(solution)/shard_map/ppermute | solution.py:47
  27.9 391.7 %reduce-scatter.7.cloned.1.call-start = ((), (), s32[]{:S(2)}) async-start(), calls=%async_computation.3 | async-start | bytes 4014080
  38.4 51.0 %collective-permute-start.14 = (bf16[56,2560]{1,0:T(8,128)(2,1)}, bf16[56,2560]{1,0:T(8,128)(2,1)}, u32[]{:S(2)}, u32[]{:S(2)}) collective-permute-start(bf16[56,2560]{1,0:T(8,128)(2,1)} %fusion.35), channel_id=1, source_target_pairs={{0,24},{8,0},{16,8},{24,16},{1,25},{9,1},{17,9},{25,17},{2,26},{10... | collective-permute-start | bytes 860168 | tf_op jit(solution)/shard_map/ppermute | solution.py:47
  42.1 53.1 %collective-permute-start.2 = (bf16[128,896]{1,0:T(8,128)(2,1)}, bf16[128,896]{1,0:T(8,128)(2,1)}, u32[]{:S(2)}, u32[]{:S(2)}) collective-permute-start(bf16[128,896]{1,0:T(8,128)(2,1)} %dynamic-slice_bitcast_fusion.6), channel_id=1, source_target_pairs={{0,4},{2,6},{1,5},{3,7},{8,12},{10,14},{9,13},{11,15},{16,20},{18,... | collective-permute-start | bytes 688136 | tf_op jit(solution)/shard_map/ppermute | solution.py:42
  45.6 18.1 %collective-permute-start.5 = (bf16[56,1664]{1,0:T(8,128)(2,1)S(1)}, bf16[56,1664]{1,0:T(8,128)(2,1)S(1)}, u32[]{:S(2)}, u32[]{:S(2)}) collective-permute-start(bf16[56,1664]{1,0:T(8,128)(2,1)S(1)} %fusion.34), channel_id=1, source_target_pairs={{0,16},{8,24},{16,0},{24,8},{1,17},{9,25},{17,1},{25,9},{2,18},{10... | collective-permute-start | bytes 559112 | tf_op jit(solution)/shard_map/ppermute | solution.py:47
  63.7 12.8 %collective-permute-start.6 = (bf16[56,1664]{1,0:T(8,128)(2,1)S(1)}, bf16[56,1664]{1,0:T(8,128)(2,1)S(1)}, u32[]{:S(2)}, u32[]{:S(2)}) collective-permute-start(bf16[56,1664]{1,0:T(8,128)(2,1)S(1)} %fusion.34), channel_id=1, source_target_pairs={{0,24},{8,0},{16,8},{24,16},{1,25},{9,1},{17,9},{25,17},{2,26},{10... | collective-permute-start | bytes 559112 | tf_op jit(solution)/shard_map/ppermute | solution.py:47
  76.4 18.5 %collective-permute-start.1 = (bf16[256,896]{1,0:T(8,128)(2,1)}, bf16[256,896]{1,0:T(8,128)(2,1)S(1)}, u32[]{:S(2)}, u32[]{:S(2)}) collective-permute-start(bf16[256,896]{1,0:T(8,128)(2,1)} %pad_maximum_fusion.7), channel_id=1, source_target_pairs={{0,2},{2,4},{4,6},{1,3},{3,5},{5,7},{8,10},{10,12},{12,14},{9,11},... | collective-permute-start | bytes 1376264 | tf_op jit(solution)/shard_map/ppermute | solution.py:42
  82.3 33.8 %collective-permute-start.7 = (bf16[4,56,1664]{2,1,0:T(8,128)(2,1)}, bf16[4,56,1664]{2,1,0:T(8,128)(2,1)S(1)}, u32[]{:S(2)}, u32[]{:S(2)}) collective-permute-start(bf16[4,56,1664]{2,1,0:T(8,128)(2,1)} %bitcast_dynamic-update-slice_fusion.14), channel_id=1, source_target_pairs={{0,2},{2,0},{4,6},{6,4},{1,3},{3,1},{5,7},{7,5},{8,10},{10,8},{12,... | collective-permute-start | bytes 2236424 | tf_op jit(solution)/shard_map/ppermute | solution.py:52
  85.8 27.1 %collective-permute-start.8 = (bf16[4,56,1664]{2,1,0:T(8,128)(2,1)}, bf16[4,56,1664]{2,1,0:T(8,128)(2,1)S(1)}, u32[]{:S(2)}, u32[]{:S(2)}) collective-permute-start(bf16[4,56,1664]{2,1,0:T(8,128)(2,1)} %bitcast_dynamic-update-slice_fusion.14), channel_id=1, source_target_pairs={{0,4},{2,6},{4,0},{6,2},{1,5},{3,7},{5,1},{7,3},{8,12},{10,14},{12... | collective-permute-start | bytes 2236424 | tf_op jit(solution)/shard_map/ppermute | solution.py:52
  91.1 81.7 %collective-permute-start.15 = (bf16[4,56,2560]{2,1,0:T(8,128)(2,1)}, bf16[4,56,2560]{2,1,0:T(8,128)(2,1)}, u32[]{:S(2)}, u32[]{:S(2)}) collective-permute-start(bf16[4,56,2560]{2,1,0:T(8,128)(2,1)} %bitcast_dynamic-update-slice_fusion.10), channel_id=1, source_target_pairs={{0,2},{2,0},{4,6},{6,4},{1,3},{3,1},{5,7},{7,5},{8,10},{10,8},{12,... | collective-permute-start | bytes 3440648 | tf_op jit(solution)/shard_map/ppermute | solution.py:52
  94.9 76.4 %collective-permute-start.16 = (bf16[4,56,2560]{2,1,0:T(8,128)(2,1)}, bf16[4,56,2560]{2,1,0:T(8,128)(2,1)}, u32[]{:S(2)}, u32[]{:S(2)}) collective-permute-start(bf16[4,56,2560]{2,1,0:T(8,128)(2,1)} %bitcast_dynamic-update-slice_fusion.10), channel_id=1, source_target_pairs={{0,4},{2,6},{4,0},{6,2},{1,5},{3,7},{5,1},{7,3},{8,12},{10,14},{12... | collective-permute-start | bytes 3440648 | tf_op jit(solution)/shard_map/ppermute | solution.py:52
  96.4 23.3 %collective-permute-start.3 = (bf16[384,896]{1,0:T(8,128)(2,1)S(1)}, bf16[384,896]{1,0:T(8,128)(2,1)S(1)}, u32[]{:S(2)}, u32[]{:S(2)}) collective-permute-start(bf16[384,896]{1,0:T(8,128)(2,1)S(1)} %constant_dynamic-update-slice_fusion), channel_id=1, source_target_pairs={{0,1},{1,0},{2,3},{3,2},{4,5},{5,4},{6,7},{7,6},{8,9},{9,8},{10,11... | collective-permute-start | bytes 2064392 | tf_op jit(solution)/shard_map/ppermute | solution.py:52
  112.9 47.9 %collective-permute-start.9 = (bf16[4,56,768]{2,1,0:T(8,128)(2,1)S(1)}, bf16[4,56,768]{2,1,0:T(8,128)(2,1)S(1)}, u32[]{:S(2)}, u32[]{:S(2)}) collective-permute-start(bf16[4,56,768]{2,1,0:T(8,128)(2,1)S(1)} %slice.190), channel_id=1, source_target_pairs={{0,2},{2,0},{4,6},{6,4},{1,3},{3,1},{5,7},{7,5},{8,10},{10,8},{12,... | collective-permute-start | bytes 1032200 | tf_op jit(solution)/shard_map/ppermute | solution.py:52
  116.1 44.7 %collective-permute-start.10 = (bf16[4,56,896]{2,1,0:T(8,128)(2,1)S(1)}, bf16[4,56,896]{2,1,0:T(8,128)(2,1)S(1)}, u32[]{:S(2)}, u32[]{:S(2)}) collective-permute-start(bf16[4,56,896]{2,1,0:T(8,128)(2,1)S(1)} %slice.191), channel_id=1, source_target_pairs={{0,4},{2,6},{4,0},{6,2},{1,5},{3,7},{5,1},{7,3},{8,12},{10,14},{12... | collective-permute-start | bytes 1204232 | tf_op jit(solution)/shard_map/ppermute | solution.py:52
  121.4 39.5 %copy-start.4 = (bf16[768,896]{1,0:T(8,128)(2,1)}, bf16[768,896]{1,0:T(8,128)(2,1)S(1)}, u32[]{:S(2)}) copy-start(bf16[768,896]{1,0:T(8,128)(2,1)S(1)} %constant_dynamic-update-slice_fusion.2.x_ref) | copy-start | bytes 4128772
  172.4 11.5 %collective-permute-start.17 = (bf16[4,56,1280]{2,1,0:T(8,128)(2,1)S(1)}, bf16[4,56,1280]{2,1,0:T(8,128)(2,1)S(1)}, u32[]{:S(2)}, u32[]{:S(2)}) collective-permute-start(bf16[4,56,1280]{2,1,0:T(8,128)(2,1)S(1)} %slice.201), channel_id=1, source_target_pairs={{0,2},{2,0},{4,6},{6,4},{1,3},{3,1},{5,7},{7,5},{8,10},{10,8},{12,... | collective-permute-start | bytes 1720328 | tf_op jit(solution)/shard_map/ppermute | solution.py:52
  173.9 11.3 %collective-permute-start.18 = (bf16[4,56,1280]{2,1,0:T(8,128)(2,1)S(1)}, bf16[4,56,1280]{2,1,0:T(8,128)(2,1)S(1)}, u32[]{:S(2)}, u32[]{:S(2)}) collective-permute-start(bf16[4,56,1280]{2,1,0:T(8,128)(2,1)S(1)} %slice.202), channel_id=1, source_target_pairs={{0,4},{2,6},{4,0},{6,2},{1,5},{3,7},{5,1},{7,3},{8,12},{10,14},{12... | collective-permute-start | bytes 1720328 | tf_op jit(solution)/shard_map/ppermute | solution.py:52
  196.3 12.8 %collective-permute-start.19 = (f32[256,896]{1,0:T(8,128)}, f32[256,896]{1,0:T(8,128)}, u32[]{:S(2)}, u32[]{:S(2)}) collective-permute-start(f32[256,896]{1,0:T(8,128)} %get-tuple-element.85.pa_ref), channel_id=1, source_target_pairs={{0,1},{1,0},{2,3},{3,2},{4,5},{5,4},{6,7},{7,6},{8,9},{9,8},{10,11... | collective-permute-start | bytes 2752520 | tf_op jit(solution)/shard_map/ppermute | solution.py:52
  226.7 2.9 collective-permute-start.20
  245.6 174.0 %reduce-scatter.9.cloned.1.call-start = ((), (), s32[]{:S(2)}) async-start(), calls=%async_computation.4 | async-start | bytes 4014080
  245.7 4.6 collective-permute-start.22
  249.8 27.0 %collective-permute-start.21 = (f32[256,896]{1,0:T(8,128)S(1)}, f32[256,896]{1,0:T(8,128)}, u32[]{:S(2)}, u32[]{:S(2)}) collective-permute-start(f32[256,896]{1,0:T(8,128)S(1)} %copy-done.22), channel_id=1, source_target_pairs={{0,1},{1,0},{2,3},{3,2},{4,5},{5,4},{6,7},{7,6},{8,9},{9,8},{10,11... | collective-permute-start | bytes 2752520 | tf_op jit(solution)/shard_map/ppermute | solution.py:52
  268.2 11.4 %collective-permute-start.23 = (f32[256,896]{1,0:T(8,128)}, f32[256,896]{1,0:T(8,128)S(1)}, u32[]{:S(2)}, u32[]{:S(2)}) collective-permute-start(f32[256,896]{1,0:T(8,128)} %get-tuple-element.94.da_ref), channel_id=1, source_target_pairs={{0,1},{1,0},{2,3},{3,2},{4,5},{5,4},{6,7},{7,6},{8,9},{9,8},{10,11... | collective-permute-start | bytes 2752520 | tf_op jit(solution)/shard_map/ppermute | solution.py:52
  270.5 31.4 %collective-permute-start.34 = (bf16[4,2,56,1024]{3,2,0,1:T(8,128)(2,1)S(1)}, bf16[4,2,56,1024]{3,2,0,1:T(8,128)(2,1)S(1)}, u32[]{:S(2)}, u32[]{:S(2)}) collective-permute-start(bf16[4,2,56,1024]{3,2,0,1:T(8,128)(2,1)S(1)} %pad_maximum_fusion.5), channel_id=1, source_target_pairs={{0,2},{2,0},{4,6},{6,4},{1,3},{3,1},{5,7},{7,5},{8,10},{10,8},{12,... | collective-permute-start | bytes 2752520 | tf_op jit(solution)/shard_map/ppermute | solution.py:52
  276.4 32.1 %collective-permute-start.36 = (bf16[4,2,56,1024]{3,2,0,1:T(8,128)(2,1)}, bf16[4,2,56,1024]{3,2,0,1:T(8,128)(2,1)S(1)}, u32[]{:S(2)}, u32[]{:S(2)}) collective-permute-start(bf16[4,2,56,1024]{3,2,0,1:T(8,128)(2,1)} %pad_maximum_fusion.6), channel_id=1, source_target_pairs={{0,4},{2,6},{4,0},{6,2},{1,5},{3,7},{5,1},{7,3},{8,12},{10,14},{12... | collective-permute-start | bytes 2752520 | tf_op jit(solution)/shard_map/ppermute | solution.py:52
  300.1 13.8 %collective-permute-start.44 = (f32[3,896]{1,0:T(4,128)S(1)}, f32[3,896]{1,0:T(4,128)S(1)}, u32[]{:S(2)}, u32[]{:S(2)}) collective-permute-start(f32[3,896]{1,0:T(4,128)S(1)} %pad_maximum_fusion.9), channel_id=1, source_target_pairs={{0,1},{1,0},{2,3},{3,2},{4,5},{5,4},{6,7},{7,6},{8,9},{9,8},{10,11... | collective-permute-start | bytes 32264 | tf_op jit(solution)/shard_map/ppermute | solution.py:52
  303.1 47.8 %collective-permute-start.35 = (bf16[4,56,1024]{2,1,0:T(8,128)(2,1)}, bf16[4,56,1024]{2,1,0:T(8,128)(2,1)}, u32[]{:S(2)}, u32[]{:S(2)}) collective-permute-start(bf16[4,56,1024]{2,1,0:T(8,128)(2,1)} %fusion.12), channel_id=1, source_target_pairs={{0,4},{2,6},{4,0},{6,2},{1,5},{3,7},{5,1},{7,3},{8,12},{10,14},{12... | collective-permute-start | bytes 1376264 | tf_op jit(solution)/shard_map/ppermute | solution.py:52
  309.6 44.0 %collective-permute-start.37 = (bf16[4,56,1024]{2,1,0:T(8,128)(2,1)}, bf16[4,56,1024]{2,1,0:T(8,128)(2,1)}, u32[]{:S(2)}, u32[]{:S(2)}) collective-permute-start(bf16[4,56,1024]{2,1,0:T(8,128)(2,1)} %fusion.13), channel_id=1, source_target_pairs={{0,2},{2,0},{4,6},{6,4},{1,3},{3,1},{5,7},{7,5},{8,10},{10,8},{12,... | collective-permute-start | bytes 1376264 | tf_op jit(solution)/shard_map/ppermute | solution.py:52
  314.5 18.9 %collective-permute-start.45 = (f32[3,896]{1,0:T(4,128)S(1)}, f32[3,896]{1,0:T(4,128)S(1)}, u32[]{:S(2)}, u32[]{:S(2)}) collective-permute-start(f32[3,896]{1,0:T(4,128)S(1)} %fusion.49), channel_id=1, source_target_pairs={{0,2},{2,0},{4,6},{6,4},{1,3},{3,1},{5,7},{7,5},{8,10},{10,8},{12,... | collective-permute-start | bytes 32264 | tf_op jit(solution)/shard_map/ppermute | solution.py:52
  316.7 71.1 %collective-permute-start.27 = (bf16[4,2,56,1024]{3,2,0,1:T(8,128)(2,1)}, bf16[4,2,56,1024]{3,2,0,1:T(8,128)(2,1)}, u32[]{:S(2)}, u32[]{:S(2)}) collective-permute-start(bf16[4,2,56,1024]{3,2,0,1:T(8,128)(2,1)} %pad_maximum_fusion.3), channel_id=1, source_target_pairs={{0,2},{2,0},{4,6},{6,4},{1,3},{3,1},{5,7},{7,5},{8,10},{10,8},{12,... | collective-permute-start | bytes 2752520 | tf_op jit(solution)/shard_map/ppermute | solution.py:52
  333.4 3.8 collective-permute-start.46
  337.2 4.2 collective-permute-start.47
  341.4 6.2 %collective-permute-start.48 = (f32[3,896]{1,0:T(4,128)S(1)}, f32[3,896]{1,0:T(4,128)S(1)}, u32[]{:S(2)}, u32[]{:S(2)}) collective-permute-start(f32[3,896]{1,0:T(4,128)S(1)} %add.408), channel_id=1, source_target_pairs={{0,16},{8,24},{16,0},{24,8},{1,17},{9,25},{17,1},{25,9},{2,18},{10... | collective-permute-start | bytes 32264 | tf_op jit(solution)/shard_map/ppermute | solution.py:52
  347.2 42.3 %collective-permute-start.29 = (bf16[4,2,56,1024]{3,2,0,1:T(8,128)(2,1)}, bf16[4,2,56,1024]{3,2,0,1:T(8,128)(2,1)}, u32[]{:S(2)}, u32[]{:S(2)}) collective-permute-start(bf16[4,2,56,1024]{3,2,0,1:T(8,128)(2,1)} %pad_maximum_fusion.4), channel_id=1, source_target_pairs={{0,4},{2,6},{4,0},{6,2},{1,5},{3,7},{5,1},{7,3},{8,12},{10,14},{12... | collective-permute-start | bytes 2752520 | tf_op jit(solution)/shard_map/ppermute | solution.py:52
  347.6 28.9 %collective-permute-start.24 = (bf16[256,896]{1,0:T(8,128)(2,1)}, bf16[256,896]{1,0:T(8,128)(2,1)}, u32[]{:S(2)}, u32[]{:S(2)}) collective-permute-start(bf16[256,896]{1,0:T(8,128)(2,1)} %get-tuple-element.141), channel_id=1, source_target_pairs={{2,0},{4,2},{6,4},{3,1},{5,3},{7,5},{10,8},{12,10},{14,12},{11,9},... | collective-permute-start | bytes 1376264 | tf_op jit(solution)/shard_map/ppermute | solution.py:42
  350.9 34.0 %collective-permute-start.25 = (bf16[256,896]{1,0:T(8,128)(2,1)}, bf16[256,896]{1,0:T(8,128)(2,1)S(1)}, u32[]{:S(2)}, u32[]{:S(2)}) collective-permute-start(bf16[256,896]{1,0:T(8,128)(2,1)} %get-tuple-element.142), channel_id=1, source_target_pairs={{4,0},{6,2},{5,1},{7,3},{12,8},{14,10},{13,9},{15,11},{20,16},{22,... | collective-permute-start | bytes 1376264 | tf_op jit(solution)/shard_map/ppermute | solution.py:42
  355.0 36.1 %collective-permute-start.38 = (bf16[56,2048]{1,0:T(8,128)(2,1)S(1)}, bf16[56,2048]{1,0:T(8,128)(2,1)S(1)}, u32[]{:S(2)}, u32[]{:S(2)}) collective-permute-start(bf16[56,2048]{1,0:T(8,128)(2,1)S(1)} %get-tuple-element.145), channel_id=1, source_target_pairs={{0,8},{8,16},{16,24},{24,0},{1,9},{9,17},{17,25},{25,1},{2,10},{10... | collective-permute-start | bytes 688136 | tf_op jit(solution)/shard_map/ppermute | solution.py:47
  376.5 24.7 %collective-permute-start.39 = (bf16[56,2048]{1,0:T(8,128)(2,1)S(1)}, bf16[56,2048]{1,0:T(8,128)(2,1)S(1)}, u32[]{:S(2)}, u32[]{:S(2)}) collective-permute-start(bf16[56,2048]{1,0:T(8,128)(2,1)S(1)} %get-tuple-element.147), channel_id=1, source_target_pairs={{0,16},{8,24},{16,0},{24,8},{1,17},{9,25},{17,1},{25,9},{2,18},{10... | collective-permute-start | bytes 688136 | tf_op jit(solution)/shard_map/ppermute | solution.py:47
  384.9 16.4 %collective-permute-start.40 = (bf16[56,2048]{1,0:T(8,128)(2,1)S(1)}, bf16[56,2048]{1,0:T(8,128)(2,1)S(1)}, u32[]{:S(2)}, u32[]{:S(2)}) collective-permute-start(bf16[56,2048]{1,0:T(8,128)(2,1)S(1)} %get-tuple-element.146), channel_id=1, source_target_pairs={{0,24},{8,0},{16,8},{24,16},{1,25},{9,1},{17,9},{25,17},{2,26},{10... | collective-permute-start | bytes 688136 | tf_op jit(solution)/shard_map/ppermute | solution.py:47
  387.8 30.4 %collective-permute-start.26 = (f32[256,896]{1,0:T(8,128)S(1)}, f32[256,896]{1,0:T(8,128)S(1)}, u32[]{:S(2)}, u32[]{:S(2)}) collective-permute-start(f32[256,896]{1,0:T(8,128)S(1)} %convert_add_fusion.4), channel_id=1, source_target_pairs={{0,1},{1,0},{2,3},{3,2},{4,5},{5,4},{6,7},{7,6},{8,9},{9,8},{10,11... | collective-permute-start | bytes 2752520 | tf_op jit(solution)/shard_map/ppermute | solution.py:52
  389.5 13.3 %collective-permute-start.28 = (bf16[4,56,1024]{2,1,0:T(8,128)(2,1)S(1)}, bf16[4,56,1024]{2,1,0:T(8,128)(2,1)S(1)}, u32[]{:S(2)}, u32[]{:S(2)}) collective-permute-start(bf16[4,56,1024]{2,1,0:T(8,128)(2,1)S(1)} %fusion.10), channel_id=1, source_target_pairs={{0,4},{2,6},{4,0},{6,2},{1,5},{3,7},{5,1},{7,3},{8,12},{10,14},{12... | collective-permute-start | bytes 1376264 | tf_op jit(solution)/shard_map/ppermute | solution.py:52
  391.1 21.3 %collective-permute-start.30 = (bf16[4,56,1024]{2,1,0:T(8,128)(2,1)S(1)}, bf16[4,56,1024]{2,1,0:T(8,128)(2,1)S(1)}, u32[]{:S(2)}, u32[]{:S(2)}) collective-permute-start(bf16[4,56,1024]{2,1,0:T(8,128)(2,1)S(1)} %fusion.11), channel_id=1, source_target_pairs={{0,2},{2,0},{4,6},{6,4},{1,3},{3,1},{5,7},{7,5},{8,10},{10,8},{12,... | collective-permute-start | bytes 1376264 | tf_op jit(solution)/shard_map/ppermute | solution.py:52
  413.6 10.8 %collective-permute-start.31 = (bf16[56,2048]{1,0:T(8,128)(2,1)}, bf16[56,2048]{1,0:T(8,128)(2,1)S(1)}, u32[]{:S(2)}, u32[]{:S(2)}) collective-permute-start(bf16[56,2048]{1,0:T(8,128)(2,1)} %get-tuple-element.156), channel_id=1, source_target_pairs={{0,8},{8,16},{16,24},{24,0},{1,9},{9,17},{17,25},{25,1},{2,10},{10... | collective-permute-start | bytes 688136 | tf_op jit(solution)/shard_map/ppermute | solution.py:47
  415.6 18.6 %collective-permute-start.32 = (bf16[56,2048]{1,0:T(8,128)(2,1)}, bf16[56,2048]{1,0:T(8,128)(2,1)}, u32[]{:S(2)}, u32[]{:S(2)}) collective-permute-start(bf16[56,2048]{1,0:T(8,128)(2,1)} %get-tuple-element.158), channel_id=1, source_target_pairs={{0,16},{8,24},{16,0},{24,8},{1,17},{9,25},{17,1},{25,9},{2,18},{10... | collective-permute-start | bytes 688136 | tf_op jit(solution)/shard_map/ppermute | solution.py:47
  415.9 18.3 %collective-permute-start.33 = (bf16[56,2048]{1,0:T(8,128)(2,1)}, bf16[56,2048]{1,0:T(8,128)(2,1)}, u32[]{:S(2)}, u32[]{:S(2)}) collective-permute-start(bf16[56,2048]{1,0:T(8,128)(2,1)} %get-tuple-element.157), channel_id=1, source_target_pairs={{0,24},{8,0},{16,8},{24,16},{1,25},{9,1},{17,9},{25,17},{2,26},{10... | collective-permute-start | bytes 688136 | tf_op jit(solution)/shard_map/ppermute | solution.py:47
  422.1 20.7 %collective-permute-start.41 = (bf16[56,3584]{1,0:T(8,128)(2,1)}, bf16[56,3584]{1,0:T(8,128)(2,1)}, u32[]{:S(2)}, u32[]{:S(2)}) collective-permute-start(bf16[56,3584]{1,0:T(8,128)(2,1)} %get-tuple-element.138), channel_id=1, source_target_pairs={{0,8},{8,16},{16,24},{24,0},{1,9},{9,17},{17,25},{25,1},{2,10},{10... | collective-permute-start | bytes 1204232 | tf_op jit(solution)/shard_map/ppermute | solution.py:47
  422.1 41.7 %collective-permute-start.42 = (bf16[56,3584]{1,0:T(8,128)(2,1)}, bf16[56,3584]{1,0:T(8,128)(2,1)}, u32[]{:S(2)}, u32[]{:S(2)}) collective-permute-start(bf16[56,3584]{1,0:T(8,128)(2,1)} %get-tuple-element.139), channel_id=1, source_target_pairs={{0,16},{8,24},{16,0},{24,8},{1,17},{9,25},{17,1},{25,9},{2,18},{10... | collective-permute-start | bytes 1204232 | tf_op jit(solution)/shard_map/ppermute | solution.py:47
  424.4 39.4 %collective-permute-start.43 = (bf16[56,3584]{1,0:T(8,128)(2,1)}, bf16[56,3584]{1,0:T(8,128)(2,1)}, u32[]{:S(2)}, u32[]{:S(2)}) collective-permute-start(bf16[56,3584]{1,0:T(8,128)(2,1)} %get-tuple-element.140), channel_id=1, source_target_pairs={{0,24},{8,0},{16,8},{24,16},{1,25},{9,1},{17,9},{25,17},{2,26},{10... | collective-permute-start | bytes 1204232 | tf_op jit(solution)/shard_map/ppermute | solution.py:47
  427.5 36.4 %copy-start.13 = (bf16[4,1,56,1792]{3,2,0,1:T(8,128)(2,1)S(1)}, bf16[4,1,56,1792]{3,2,0,1:T(8,128)(2,1)}, u32[]{:S(2)}) copy-start(bf16[4,1,56,1792]{3,2,0,1:T(8,128)(2,1)} %reduce-scatter.7.cloned.1.call-done) | copy-start | bytes 2408452
  427.5 36.4 %copy-start.14 = (bf16[4,1,56,1792]{3,2,0,1:T(8,128)(2,1)S(1)}, bf16[4,1,56,1792]{3,2,0,1:T(8,128)(2,1)}, u32[]{:S(2)}) copy-start(bf16[4,1,56,1792]{3,2,0,1:T(8,128)(2,1)} %reduce-scatter.9.cloned.1.call-done) | copy-start | bytes 2408452
  436.9 57.6 %copy-start.39 = (f32[3,56]{1,0:T(4,128)S(1)}, f32[3,56]{1,0:T(4,128)}, u32[]{:S(2)}) copy-start(f32[3,56]{1,0:T(4,128)} %get-tuple-element.131) | copy-start | bytes 2020
  436.9 57.6 %copy-start.41 = (f32[3,56]{1,0:T(4,128)S(1)}, f32[3,56]{1,0:T(4,128)}, u32[]{:S(2)}) copy-start(f32[3,56]{1,0:T(4,128)} %param.29) | copy-start | bytes 2020
  436.9 57.6 %copy-start.44 = (f32[3,56]{1,0:T(4,128)S(1)}, f32[3,56]{1,0:T(4,128)}, u32[]{:S(2)}) copy-start(f32[3,56]{1,0:T(4,128)} %param.33) | copy-start | bytes 2020
  436.9 57.6 %copy-start.45 = (f32[3,56]{1,0:T(4,128)S(1)}, f32[3,56]{1,0:T(4,128)}, u32[]{:S(2)}) copy-start(f32[3,56]{1,0:T(4,128)} %param.37) | copy-start | bytes 2020
  467.5 1.3 collective-permute-start.49
  469.4 3.7 collective-permute-start.50
  473.7 3.7 collective-permute-start.51
  477.9 10.8 %collective-permute-start.52 = (f32[1,1]{1,0:T(1,128)}, f32[1,1]{1,0:T(1,128)}, u32[]{:S(2)}, u32[]{:S(2)}) collective-permute-start(f32[1,1]{1,0:T(1,128)} %add.415), channel_id=1, source_target_pairs={{0,8},{8,0},{16,24},{24,16},{1,9},{9,1},{17,25},{25,17},{2,10},{10... | collective-permute-start | bytes 20 | tf_op jit(solution)/shard_map/ppermute | solution.py:52
  489.3 4.6 collective-permute-start.53
  (43 other events, 314.4 us)
Sparse Core Ops, SparseCore 0:
  28.0 137.0 all-gather.1
  245.7 54.4 reduce-scatter.6
  303.3 69.2 reduce-scatter.8

commit v3 on v2

v3 whole, which is shorter than its diff:
```python
import jax
import jax.numpy as jnp
from jax import lax
from jax.experimental import pallas as pl
from jax.experimental.pallas import tpu as pltpu
from jax.sharding import PartitionSpec as P

HEAD_DIM = 64
PAIR = 128
BLOCK = 64
NEIGHBOURS = 2
NEIGH_LEN = 128
KEYS = NEIGHBOURS * NEIGH_LEN
STEP = 10
DOC_MAX = 512
CHUNK = 256
TOKENS = 512

norm_eps = 1e-05
rope_base = 10000.0
beta_one = 0.9
beta_two = 0.95
adam_eps = 1e-08
weight_decay = 0.1
learn_rate = 0.1
gain_rate = 0.5
clip_limit = 1.0
masked_fill = -1e30
score_scale = HEAD_DIM ** (-0.5)
gelu_c = 0.7978845608028654
gelu_k = 0.044715

f32 = jnp.float32
bf16 = jnp.bfloat16


def to_low(array_in):
    return array_in.astype(bf16)


def shifted(value, axis, by):
    count = lax.axis_size(axis)
    return lax.ppermute(value, axis, [(i, i + by) for i in range(count) if 0 <= i + by < count])


def rotated(value, axis, by):
    count = lax.axis_size(axis)
    return lax.ppermute(value, axis, [(i, (i + by) % count) for i in range(count)])


def swapped(value, axis, by):
    count = lax.axis_size(axis)
    return lax.ppermute(value, axis, [(i, i ^ by) for i in range(count)])


def butterfly(value, axes):
    for axis in axes:
        step = 1
        while step < lax.axis_size(axis):
            value = value + swapped(value, axis, step)
            step *= 2
    return value


def sum_everywhere(value):
    axes = ("dp", "seq", "mp")
    if not small_mesh():
        return butterfly(value, axes)
    count = lax.axis_size("dp") * lax.axis_size("seq") * lax.axis_size("mp")
    spread = jnp.broadcast_to(value, (count, 8, PAIR))
    return jnp.sum(lax.all_to_all(spread, axes, 0, 0, tiled=True)[:, :1, :1], axis=0)


def core_sum(partial_out):
    return partial_out + swapped(partial_out, "mp", 1)


def small_mesh():
    return lax.axis_size("dp") == 4 and lax.axis_size("seq") == 4


def put(buffer, piece, starts):
    return lax.dynamic_update_slice(buffer, piece, starts)


def meet(*values):
    return lax.optimization_barrier(values)


def token_of(array_in):
    return array_in[:8, :PAIR]


ORDER = (0, 2, 1, 3)


def own_order(model, s):
    rows = model // 16
    spot = jnp.arange(model)
    near, z, inner = spot // (4 * rows), spot // rows % 4, spot % rows
    flip = (near % 2) * 2 + near // 2
    source = (z * 4 + (s ^ flip)) * rows + inner
    return (spot[:, None] == source[None, :]).astype(bf16)


def plane_sum(pieces):
    return (pieces[0] + pieces[1].astype(f32)) + (pieces[2].astype(f32) + pieces[3].astype(f32))


def take(array_in, index, axis):
    return lax.dynamic_index_in_dim(array_in, index, axis, keepdims=False)


def wide_for_dp(block):
    rows, cols = block.shape
    return jnp.broadcast_to(block[None], (4, rows, cols)).reshape(4 * rows, cols)


def exchanged(array_in, axis):
    return lax.all_to_all(array_in, axis, 0, 0, tiled=True)


def from_seq(column):
    return [swapped(column, "seq", k) for k in ORDER[1:]]


def weight(pieces, start):
    return [(p, start) for p in pieces]


def reduce_first(sent):
    return swapped(sent[0], "seq", 1), swapped(sent[1], "seq", 2)


def reduce_second(kept, got):
    keep_a, keep_b, sent_a, sent_b = half_sum_call(kept, got)
    return (keep_a, keep_b), (swapped(sent_a, "seq", 2), swapped(sent_b, "seq", 1))


def last_sum(kept, got):
    return jnp.concatenate(
        [to_low(k.astype(f32) + g.astype(f32)) for k, g in zip(kept, got)], axis=1
    )


def reduce_last(got):
    rows, cols = got.shape
    return jnp.sum(got.reshape(4, rows // 4, cols).astype(f32), axis=0)


def reduce_plain(grads):
    return lax.psum_scatter(
        jnp.concatenate(grads, axis=1), ("dp", "seq"), scatter_dimension=0, tiled=True
    ).astype(f32)


def halves(left, right):
    if not small_mesh():
        return None, [jnp.concatenate([to_low(t_dot(a, b)) for a, b in left + right], axis=1)]

    def products(pairs, pick):
        parts = [to_low(t_dot(pick(a), b)) for a, b in pairs]
        return parts[0] if len(parts) == 1 else jnp.concatenate(parts, axis=1)

    def second(a, first):
        quarter = a.shape[1] // 4
        return jnp.concatenate(
            [
                a[:, first * quarter : (first + 1) * quarter],
                a[:, (first + 2) * quarter : (first + 3) * quarter],
            ],
            axis=1,
        )

    mid = left[0][0].shape[1] // 2
    sent = (products(left, lambda a: a[:, mid:]), products(right, lambda a: second(a, 1)))
    kept = (products(left, lambda a: a[:, :mid]), products(right, lambda a: second(a, 0)))
    return sent, kept


def adam_step(weight, gradient, first_old, second_old, factor, step_rate, decay_coef):
    clipped = gradient * factor
    first_new = beta_one * first_old + (1.0 - beta_one) * clipped
    second_new = beta_two * second_old + (1.0 - beta_two) * clipped * clipped
    first_hat = first_new / (1.0 - beta_one**STEP)
    second_hat = second_new / (1.0 - beta_two**STEP)
    weight_new = weight - step_rate * (
        first_hat / (jnp.sqrt(second_hat) + adam_eps) + decay_coef * weight
    )
    return (weight_new, first_new, second_new)


def call(kernel, grid, ins, outs, args, scratch=(), prefetch=0):
    specs, flat, counts = [], list(args[:prefetch]), [1] * prefetch
    for (shape, index), arg in zip(ins, args[prefetch:]):
        if not isinstance(arg, list):
            specs.append(pl.BlockSpec(shape, index))
            flat.append(arg)
            counts.append(1)
            continue
        for array_in, start in arg:
            place = lambda *ids, at=start // shape, f=index: (0, f(ids[0]) + at)
            specs.append(pl.BlockSpec((array_in.shape[0], shape), place))
            flat.append(array_in)
        counts.append(-len(arg))

    def body(*refs):
        refs, grouped = list(refs), []
        for count in counts:
            grouped.append(refs.pop(0) if count > 0 else [refs.pop(0) for _ in range(-count)])
        kernel(*grouped, *refs)

    return pl.pallas_call(
        body,
        out_shape=[jax.ShapeDtypeStruct(o[2], o[3]) for o in outs],
        grid_spec=pltpu.PrefetchScalarGridSpec(
            num_scalar_prefetch=prefetch,
            grid=grid,
            in_specs=specs,
            out_specs=[pl.BlockSpec(o[0], o[1]) for o in outs],
            scratch_shapes=list(scratch),
        ),
        compiler_params=pltpu.CompilerParams(
            dimension_semantics=("arbitrary",) * len(grid), vmem_limit_bytes=56 << 20
        ),
        name=kernel.__name__,
    )(*flat)


def whole_weight(refs):
    pieces = [r[...] for r in refs]
    return pieces[0] if len(pieces) == 1 else jnp.concatenate(pieces, axis=0)


first_block = lambda i: 0
each_block = lambda i: i


def dot(a, b):
    return jnp.dot(a, b, preferred_element_type=f32)


def dot_t(a, b):
    return lax.dot_general(a, b, (((1,), (1,)), ((), ())), preferred_element_type=f32)


def t_dot(a, b):
    return lax.dot_general(a, b, (((0,), (0,)), ((), ())), preferred_element_type=f32)


def rms_factor(z):
    return lax.rsqrt(jnp.mean(z * z, axis=-1, keepdims=True) + norm_eps)


def rms_back(z, gain, grad):
    factor = rms_factor(z)
    scaled = grad * gain
    inner = jnp.mean(scaled * z, axis=-1, keepdims=True)
    return factor * scaled - z * (factor * factor * factor * inner), grad * z * factor


def lane_in_head(shape):
    return lax.broadcasted_iota(jnp.int32, shape, 1)


def rope(z, cos, sin, sign):
    lane = lane_in_head(z.shape)
    lead = lane % HEAD_DIM < HEAD_DIM // 2
    partner = jnp.where(lead, -pltpu.roll(z, PAIR - 32, 1), pltpu.roll(z, 32, 1))
    return z * cos + partner * (sin * sign)


def split_heads(z):
    first = lane_in_head(z.shape) < HEAD_DIM
    zero = jnp.zeros_like(z)
    return jnp.where(first, z, zero), jnp.where(first, zero, z)


def join_heads(a, b):
    return jnp.where(lane_in_head(a.shape) < HEAD_DIM, a, b)


def qkv_kernel(x_ref, g_ref, wq, wk, wv, cos_ref, sin_ref, n_ref, q_ref, k_ref, v_ref):
    rows, span = n_ref.shape[0], q_ref.shape[0]

    @pl.when(pl.program_id(0) == 0)
    def _():
        x = x_ref[...].astype(f32)
        n_ref[...] = to_low(x * rms_factor(x) * g_ref[...])

    normed, cos, sin = n_ref[...], cos_ref[...], sin_ref[...]

    def turned(raw, cos, sin):
        return jnp.concatenate(
            [
                to_low(rope(raw[:, c : c + PAIR], cos, sin, 1.0))
                for c in range(0, raw.shape[1], PAIR)
            ],
            axis=1,
        )

    k_ref[...] = turned(dot(normed, whole_weight(wk)), cos, sin)
    v_ref[...] = to_low(dot(normed, whole_weight(wv)))
    own = rows - span
    q_ref[...] = turned(dot(normed[own:], whole_weight(wq)), cos[own:], sin[own:])


def qkv_call(x_ext, gain, wq, wk, wv, cos, sin, span, width):
    rows, model = x_ext.shape
    fix = lambda i: (0, 0)
    col = lambda i: (0, i)
    return call(
        qkv_kernel,
        (width // CHUNK,),
        [
            ((rows, model), fix),
            ((1, model), fix),
            (CHUNK, each_block),
            (CHUNK, each_block),
            (CHUNK, each_block),
            ((rows, PAIR), fix),
            ((rows, PAIR), fix),
        ],
        [
            ((rows, model), fix, (rows, model), bf16),
            ((span, CHUNK), col, (span, width), bf16),
            ((rows, CHUNK), col, (rows, width), bf16),
            ((rows, CHUNK), col, (rows, width), bf16),
        ],
        (x_ext, gain, wq, wk, wv, cos, sin),
    )


def self_bias(segq_ref, segk_ref, bias_ref):
    keys, span = bias_ref.shape
    key_pos = lax.broadcasted_iota(jnp.int32, (keys, span), 0) - (keys - span)
    query_pos = lax.broadcasted_iota(jnp.int32, (keys, span), 1)
    ok = jnp.logical_and(key_pos <= query_pos, segk_ref[...] == segq_ref[...])
    bias_ref[...] = jnp.where(ok, 0.0, masked_fill)


def self_kernel(q_ref, k_ref, v_ref, segq_ref, segk_ref, wo, o_ref, lse_ref, part_ref, bias_ref):
    @pl.when(pl.program_id(0) == 0)
    def _():
        self_bias(segq_ref, segk_ref, bias_ref)
        part_ref[...] = jnp.zeros_like(part_ref)

    k, v, bias = k_ref[...], v_ref[...], bias_ref[...]
    outs, lses = [], []
    for qh in split_heads(q_ref[...] * score_scale):
        s = dot_t(k, qh) + bias
        top = jnp.max(s, axis=0, keepdims=True)
        e = jnp.exp(s - top)
        total = jnp.sum(e, axis=0, keepdims=True)
        lses.append(top + jnp.log(total))
        outs.append(t_dot(to_low(e * (1.0 / total)), v))
    o = to_low(join_heads(outs[0], outs[1]))
    o_ref[...] = o
    lse_ref[0] = jnp.concatenate(lses, axis=0)
    part_ref[...] += dot_t(o, whole_weight(wo))


def self_call(q, k, v, segq, segk, wo, model):
    span, width = q.shape
    keys = k.shape[0]
    pair = lambda p: (0, p)
    fix = lambda p: (0, 0)
    return call(
        self_kernel,
        (width // PAIR,),
        [
            ((span, PAIR), pair),
            ((keys, PAIR), pair),
            ((keys, PAIR), pair),
            ((1, span), fix),
            ((keys, 1), fix),
            (PAIR, each_block),
        ],
        [
            ((span, PAIR), pair, (span, width), bf16),
            ((1, 2, span), lambda p: (p, 0, 0), (width // PAIR, 2, span), f32),
            ((span, model), fix, (span, model), f32),
        ],
        (q, k, v, segq, segk, wo),
        scratch=[pltpu.VMEM((keys, span), f32)],
    )


def block_bias(len_ref, block):
    key = lax.broadcasted_iota(jnp.int32, (KEYS, PAIR), 0)
    limit = jnp.where(key < NEIGH_LEN, len_ref[block, 0], len_ref[block, 1])
    return jnp.where(key % NEIGH_LEN < limit, 0.0, masked_fill)


def tile_bias(len_ref, tile, tiles):
    if tile:
        return block_bias(len_ref, tile)
    first = lax.broadcasted_iota(jnp.int32, (KEYS, PAIR), 1) % BLOCK == 0
    lead = jnp.where(first, masked_fill, block_bias(len_ref, 0))
    last = jnp.where(first, block_bias(len_ref, tiles), masked_fill)
    return jnp.concatenate([lead, last], axis=0)


def stack_heads(z):
    return jnp.concatenate(split_heads(z), axis=0)


def merge_heads(z):
    return join_heads(z[:BLOCK], z[BLOCK:])


def tile_keys(ref, tile, tiles):
    own = ref[tile * KEYS : (tile + 1) * KEYS, :]
    if tile:
        return own
    return jnp.concatenate([own, ref[tiles * KEYS : (tiles + 1) * KEYS, :]], axis=0)


def cross_kernel(
    len_ref, x_ref, pa_ref, pb_ref, g_ref, wq, k_ref, v_ref, keep_ref, wo,
    h_ref, n_ref, q_ref, o_ref, lse_ref, part_ref, acc_ref,
):
    span = x_ref.shape[0]
    tiles = span // BLOCK

    @pl.when(pl.program_id(0) == 0)
    def _():
        h = x_ref[...].astype(f32) + (pa_ref[...] + pb_ref[...])
        h_ref[...] = h
        n_ref[...] = to_low(h * rms_factor(h) * g_ref[...])
        part_ref[...] = jnp.zeros_like(part_ref)

    turned = pltpu.roll(to_low(dot(n_ref[...], whole_weight(wq))).astype(f32), 1, 0)
    q = to_low(turned * score_scale)
    q_ref[...] = q
    for tile in range(tiles):
        rows = slice(tile * BLOCK, (tile + 1) * BLOCK)
        k, v = tile_keys(k_ref, tile, tiles), tile_keys(v_ref, tile, tiles)
        sc = dot_t(k, stack_heads(q[rows])) + tile_bias(len_ref, tile, tiles)
        top = jnp.max(sc, axis=0, keepdims=True)
        e = jnp.exp(sc - top)
        total = jnp.sum(e, axis=0, keepdims=True)
        lse_ref[0, tile : tile + 1, :] = top + jnp.log(total)
        acc_ref[rows, :] = merge_heads(t_dot(to_low(e * (1.0 / total)), v))
    o = to_low(pltpu.roll(acc_ref[...] * keep_ref[...], span - 1, 0))
    o_ref[...] = o
    part_ref[...] += dot_t(o, whole_weight(wo))


def cross_call(lens, x, pa, pb, gain, wq, wo, kv2, keep):
    span, model = x.shape
    keys, width = kv2.shape[0], kv2.shape[1] // 2
    pairs = width // PAIR
    pair = lambda p, *_: (0, p)
    fix = lambda p, *_: (0, 0)
    return call(
        cross_kernel,
        (pairs,),
        [
            ((span, model), fix),
            ((span, model), fix),
            ((span, model), fix),
            ((1, model), fix),
            (PAIR, each_block),
            ((keys, PAIR), pair),
            ((keys, PAIR), lambda p, *_: (0, pairs + p)),
            ((span, 1), fix),
            (PAIR, each_block),
        ],
        [
            ((span, model), fix, (span, model), f32),
            ((span, model), fix, (span, model), bf16),
            ((span, PAIR), pair, (span, width), bf16),
            ((span, PAIR), pair, (span, width), bf16),
            ((1, span // BLOCK, PAIR), lambda p, *_: (p, 0, 0), (pairs, span // BLOCK, PAIR), f32),
            ((span, model), fix, (span, model), f32),
        ],
        (lens, x, pa, pb, gain, wq, kv2, kv2, keep, wo),
        scratch=[pltpu.VMEM((span, PAIR), f32)],
        prefetch=1,
    )


def gelu_and_slope(u):
    t = jnp.tanh(gelu_c * (u + gelu_k * (u * u * u)))
    slope = 0.5 * (1.0 + t) + 0.5 * u * (1.0 - t * t) * (gelu_c * (1.0 + 3.0 * gelu_k * (u * u)))
    return to_low(0.5 * u * (1.0 + t)), slope


def norm_kernel(h1_ref, pa_ref, pb_ref, g_ref, turn_ref, h_ref, n_ref):
    h = h1_ref[...] + (pa_ref[...] + pb_ref[...])
    h_ref[...] = h
    n_ref[...] = to_low(dot_t(to_low(h * rms_factor(h) * g_ref[...]), turn_ref[...]))


def norm_call(h1, pa, pb, gain, turn):
    span, model = h1.shape
    row = lambda i: (i, 0)
    fix = lambda i: (0, 0)
    rows = span
    return call(
        norm_kernel,
        (1,),
        [((rows, model), row)] * 3 + [((1, model), fix), ((model, model), fix)],
        [
            ((rows, model), row, (span, model), f32),
            ((rows, model), row, (span, model), bf16),
        ],
        (h1, pa, pb, gain, turn),
    )


def feed_kernel(n_ref, cot_ref, up_ref, down_ref, act_ref, du_ref, ya_ref, yb_ref, da_ref, db_ref):
    up, down = up_ref[...], down_ref[...]
    act, slope = gelu_and_slope(dot(n_ref[...], up))
    du = to_low(dot(cot_ref[...], down) * slope)
    act_ref[...] = act
    du_ref[...] = du
    y, dn = dot_t(act, down), dot_t(du, up)
    step = pl.program_id(0)
    half = pl.num_programs(0) // 2

    @pl.when(step < half)
    def _():
        ya_ref[...] = to_low(y)
        da_ref[...] = dn

    @pl.when(step >= half)
    def _():
        yb_ref[...] = to_low(y)
        db_ref[...] = dn


def feed_call(n, cot, w_feed):
    rows, model = n.shape
    hidden = w_feed.shape[1] // 2
    half = rows // TOKENS // 2
    row = lambda i: (i, 0)
    lead = lambda i: (jnp.minimum(i, half - 1), 0)
    tail = lambda i: (jnp.maximum(i - half, 0), 0)
    block = (TOKENS, model)
    part = (rows // 2, model)
    return call(
        feed_kernel,
        (rows // TOKENS,),
        [
            (block, row),
            (block, row),
            ((model, hidden), lambda i: (0, 0)),
            ((model, hidden), lambda i: (0, 1)),
        ],
        [
            ((TOKENS, hidden), row, (rows, hidden), bf16),
            ((TOKENS, hidden), row, (rows, hidden), bf16),
            (block, lead, part, bf16),
            (block, tail, part, bf16),
            (block, lead, part, f32),
            (block, tail, part, f32),
        ],
        (n, cot, w_feed, w_feed),
    )


def cross_back_kernel(
    len_ref, core_ref, base_ref, h_ref, da_ref, db_ref, turn_ref, g_ref, wo, q_ref, k_ref, v_ref, lse_ref,
    keep_ref, wq,
    grad_ref, low_ref, gain_ref, dq_ref, dk_ref, dv_ref, dn_ref, acc_ref,
):
    span = h_ref.shape[0]
    tiles = span // BLOCK

    @pl.when(pl.program_id(0) == 0)
    def _():
        first, other = da_ref[...], db_ref[...]
        given = jnp.where(
            core_ref[0] == 0,
            jnp.concatenate([first, other], axis=0),
            jnp.concatenate([other, first], axis=0),
        )
        high = to_low(given)
        low = to_low(given - high.astype(f32))
        turn = turn_ref[...]
        back, gains = rms_back(h_ref[...], g_ref[...], dot(high, turn) + dot(low, turn))
        grad = base_ref[...].astype(f32) + back
        grad_ref[...] = grad
        low_ref[...] = to_low(grad)
        gain_ref[...] = jnp.sum(gains, axis=0, keepdims=True)
        dn_ref[...] = jnp.zeros_like(dn_ref)

    do = to_low(dot(low_ref[...], whole_weight(wo))).astype(f32)
    do = to_low(pltpu.roll(do, 1, 0) * keep_ref[...])
    q = q_ref[...]
    for tile in range(tiles):
        rows = slice(tile * BLOCK, (tile + 1) * BLOCK)
        k, v = tile_keys(k_ref, tile, tiles), tile_keys(v_ref, tile, tiles)
        qs, dos = stack_heads(q[rows]), stack_heads(do[rows])
        p = jnp.exp(dot_t(k, qs) + tile_bias(len_ref, tile, tiles) - lse_ref[0, tile : tile + 1, :])
        dp = dot_t(v, dos)
        ds = to_low(p * (dp - jnp.sum(p * dp, axis=0, keepdims=True)))
        acc_ref[rows, :] = merge_heads(t_dot(ds, k))
        dk = to_low(dot(ds, qs))
        dv = to_low(dot(to_low(p), dos))
        own = slice(tile * KEYS, (tile + 1) * KEYS)
        dk_ref[own, :] = dk[:KEYS]
        dv_ref[own, :] = dv[:KEYS]
        if not tile:
            last = slice(tiles * KEYS, (tiles + 1) * KEYS)
            dk_ref[last, :] = dk[KEYS:]
            dv_ref[last, :] = dv[KEYS:]
    dq = to_low(pltpu.roll(acc_ref[...] * score_scale, span - 1, 0))
    dq_ref[...] = dq
    dn_ref[...] += dot_t(dq, whole_weight(wq))


def cross_back_call(lens, core, base, h, da, db, turn, gain, wq, wo, q, kv2, lse, keep):
    span, model = h.shape
    keys, width = kv2.shape[0], kv2.shape[1] // 2
    pairs = width // PAIR
    pair = lambda p, *_: (0, p)
    fix = lambda p, *_: (0, 0)
    return call(
        cross_back_kernel,
        (pairs,),
        [
            ((span, model), fix),
            ((span, model), fix),
            ((span // 2, model), fix),
            ((span // 2, model), fix),
            ((model, model), fix),
            ((1, model), fix),
            (PAIR, each_block),
            ((span, PAIR), pair),
            ((keys, PAIR), pair),
            ((keys, PAIR), lambda p, *_: (0, pairs + p)),
            ((1, span // BLOCK, PAIR), lambda p, *_: (p, 0, 0)),
            ((span, 1), fix),
            (PAIR, each_block),
        ],
        [
            ((span, model), fix, (span, model), f32),
            ((span, model), fix, (span, model), bf16),
            ((1, model), fix, (1, model), f32),
            ((span, PAIR), pair, (span, width), bf16),
            ((keys, PAIR), pair, (keys, width), bf16),
            ((keys, PAIR), pair, (keys, width), bf16),
            ((span, model), fix, (span, model), f32),
        ],
        (lens, core, base, h, da, db, turn, gain, wo, q, kv2, kv2, lse, keep, wq),
        scratch=[pltpu.VMEM((span, PAIR), f32)],
        prefetch=2,
    )


def self_back_kernel(
    base_ref, h_ref, da_ref, db_ref, g_ref, wo, q_ref, k_ref, v_ref, lse_ref, segq_ref,
    segk_ref, cos_ref, sin_ref,
    grad_ref, low_ref, gain_ref, dq_ref, dk_ref, dv_ref, bias_ref,
):
    span = h_ref.shape[0]
    keys = k_ref.shape[0]

    @pl.when(pl.program_id(0) == 0)
    def _():
        back, gains = rms_back(h_ref[...], g_ref[...], da_ref[...] + db_ref[...])
        grad = base_ref[...] + back
        grad_ref[...] = grad
        low_ref[...] = to_low(grad)
        gain_ref[...] = jnp.sum(gains, axis=0, keepdims=True)
        self_bias(segq_ref, segk_ref, bias_ref)

    do = to_low(dot(low_ref[...], whole_weight(wo)))
    k, v, bias = k_ref[...], v_ref[...], bias_ref[...]
    qs, dos = split_heads(q_ref[...] * score_scale), split_heads(do)
    dqs, dk, dv = [], 0.0, 0.0
    for h in range(2):
        p = jnp.exp(dot_t(k, qs[h]) + bias - lse_ref[0, h : h + 1, :])
        dp = dot_t(v, dos[h])
        ds = to_low(p * (dp - jnp.sum(p * dp, axis=0, keepdims=True)))
        dqs.append(t_dot(ds, k))
        dk = dk + dot(ds, qs[h])
        dv = dv + dot(to_low(p), dos[h])
    cos, sin = cos_ref[...], sin_ref[...]
    dq = join_heads(dqs[0], dqs[1]) * score_scale
    dq_ref[...] = to_low(rope(dq, cos[keys - span :], sin[keys - span :], -1.0))
    dk_ref[...] = to_low(rope(dk, cos, sin, -1.0))
    dv_ref[...] = to_low(dv)


def self_back_call(base, h, da, db, gain, wo, q, k, v, lse, segq, segk, cos, sin):
    span, model = h.shape
    keys, width = k.shape
    pair = lambda p: (0, p)
    fix = lambda p: (0, 0)
    return call(
        self_back_kernel,
        (width // PAIR,),
        [
            ((span, model), fix),
            ((span, model), fix),
            ((span, model), fix),
            ((span, model), fix),
            ((1, model), fix),
            (PAIR, each_block),
            ((span, PAIR), pair),
            ((keys, PAIR), pair),
            ((keys, PAIR), pair),
            ((1, 2, span), lambda p: (p, 0, 0)),
            ((1, span), fix),
            ((keys, 1), fix),
            ((keys, PAIR), fix),
            ((keys, PAIR), fix),
        ],
        [
            ((span, model), fix, (span, model), f32),
            ((span, model), fix, (span, model), bf16),
            ((1, model), fix, (1, model), f32),
            ((span, PAIR), pair, (span, width), bf16),
            ((keys, PAIR), pair, (keys, width), bf16),
            ((keys, PAIR), pair, (keys, width), bf16),
        ],
        (base, h, da, db, gain, wo, q, k, v, lse, segq, segk, cos, sin),
        scratch=[pltpu.VMEM((keys, span), f32)],
    )


def inner_kernel(x_ref, dq_ref, dk_ref, dv_ref, wq, wk, wv, dn_ref, gain_ref):
    step = pl.program_id(0)
    rows, span = x_ref.shape[0], dq_ref.shape[0]
    own = rows - span
    dn = dot_t(dk_ref[...], whole_weight(wk)) + dot_t(dv_ref[...], whole_weight(wv))
    dn_own = dot_t(dq_ref[...], whole_weight(wq))

    @pl.when(step == 0)
    def _():
        dn_ref[...] = dn
        dn_ref[own:, :] += dn_own

    @pl.when(step > 0)
    def _():
        dn_ref[...] += dn
        dn_ref[own:, :] += dn_own

    @pl.when(step == pl.num_programs(0) - 1)
    def _():
        x = x_ref[...].astype(f32)
        gain_ref[...] = jnp.sum(dn_ref[...] * x * rms_factor(x), axis=0, keepdims=True)


def inner_call(x_ext, dq, dk, dv, wq, wk, wv):
    rows, model = x_ext.shape
    span, width = dq.shape
    fix = lambda i: (0, 0)
    col = lambda i: (0, i)
    return call(
        inner_kernel,
        (width // CHUNK,),
        [
            ((rows, model), fix),
            ((span, CHUNK), col),
            ((rows, CHUNK), col),
            ((rows, CHUNK), col),
            (CHUNK, each_block),
            (CHUNK, each_block),
            (CHUNK, each_block),
        ],
        [
            ((rows, model), fix, (rows, model), f32),
            ((1, model), fix, (1, model), f32),
        ],
        (x_ext, dq, dk, dv, wq, wk, wv),
    )


def adam_call(factor, weights, grads, first, second, order):
    count, rows, width = weights.shape

    def adam_kernel(factor_ref, w_ref, g_ref, m_ref, v_ref, wo_ref, mo_ref, vo_ref):
        for j, at in enumerate(order):
            wo_ref[j], mo_ref[j], vo_ref[j] = adam_step(
                w_ref[j],
                g_ref[:, at * width : (at + 1) * width],
                m_ref[j],
                v_ref[j],
                factor_ref[0],
                learn_rate,
                weight_decay,
            )

    block = (weights.shape, lambda i, *_: (0, 0, 0))
    return call(
        adam_kernel,
        (1,),
        [block, (grads.shape, lambda i, *_: (0, 0)), block, block],
        [block + (weights.shape, f32)] * 3,
        (factor, weights, grads, first, second),
        prefetch=1,
    )


def half_sum_kernel(ka, ga, kb, gb, keep_a, keep_b, sent_a, sent_b):
    step = pl.program_id(0)
    sum_a = to_low(ka[...].astype(f32) + ga[...].astype(f32))
    sum_b = to_low(kb[...].astype(f32) + gb[...].astype(f32))

    @pl.when(step == 0)
    def _():
        sent_a[...] = sum_a
        sent_b[...] = sum_b

    @pl.when(step == 1)
    def _():
        keep_a[...] = sum_a
        keep_b[...] = sum_b


def half_sum_call(kept, got):
    rows, (wide_a, wide_b) = kept[0].shape[0] // 2, (k.shape[1] for k in kept)
    turn = lambda i: (1 - i, 0)
    fix = lambda i: (0, 0)
    a, b = (rows, wide_a), (rows, wide_b)
    return call(
        half_sum_kernel,
        (2,),
        [(a, turn), (a, turn), (b, turn), (b, turn)],
        [(a, fix, a, bf16), (b, fix, b, bf16), (a, fix, a, bf16), (b, fix, b, bf16)],
        (kept[0], got[0], kept[1], got[1]),
    )


def rows_kernel(a_ref, w, o_ref):
    o_ref[...] = to_low(dot(a_ref[...], whole_weight(w)))


def rows_call(a, w, width):
    rows, model = a.shape
    block = CHUNK if width % CHUNK == 0 else width // 7 if width % 7 == 0 else width
    return call(
        rows_kernel,
        (width // block,),
        [((rows, model), lambda i: (0, 0)), (block, each_block)],
        [((rows, block), lambda i: (0, i), (rows, width), bf16)],
        (a, w),
    )[0]


def turn_call(a, turn):
    rows, model = a.shape
    return call(
        turn_kernel,
        (rows // KEYS,),
        [((KEYS, model), lambda i: (i, 0)), ((model, model), lambda i: (0, 0))],
        [((KEYS, model), lambda i: (i, 0), (rows, model), bf16)],
        (a, turn),
    )[0]


def turn_kernel(a_ref, t_ref, o_ref):
    o_ref[...] = to_low(dot(a_ref[...], t_ref[...]))


def per_device(
    tokens,
    neighbours,
    neighbour_lengths,
    segment_ids,
    out_grad,
    self_weights,
    cross_weights,
    feed_weights,
    norm_gains,
    self_first,
    cross_first,
    feed_first,
    gains_first,
    self_second,
    cross_second,
    feed_second,
    gains_second,
):
    row_count, span, model = tokens.shape
    width = self_weights.shape[2]
    hidden = feed_weights.shape[2]
    shard_rows = self_weights.shape[1]
    pairs = width // PAIR
    blocks = span // BLOCK
    halo = min(-(-(DOC_MAX - 1) // span), lax.axis_size("seq") - 1)
    s_index = lax.axis_index("seq")
    core = lax.axis_index("mp")

    def columns(*parts):
        return jnp.concatenate([to_low(p) for p in parts], axis=1)

    gain_cols = jnp.zeros((shard_rows, PAIR), f32).at[:, :3].set(norm_gains.T)
    block_q = columns(self_weights[0], self_weights[1], self_weights[2], gain_cols)
    small = small_mesh()
    x_own, cot = tokens.reshape(span, model), out_grad.reshape(span, model)
    flat_own = neighbours.reshape(-1, model)
    half, pad = span // 2, KEYS // 2
    seg_here = segment_ids.reshape(1, span) + 1
    lengths = neighbour_lengths.reshape(blocks, NEIGHBOURS)
    ints = jnp.concatenate([seg_here[0], lengths[-1]]).astype(bf16)
    ints = jnp.zeros((8, model), bf16).at[0, : span + NEIGHBOURS].set(ints)
    mine = lax.dynamic_slice_in_dim(x_own, core * half, half, 0)
    edge = lax.dynamic_slice_in_dim(flat_own, flat_own.shape[0] - KEYS + core * pad, pad, 0)
    frequency = rope_base ** (-(jnp.arange(PAIR) % (HEAD_DIM // 2)).astype(f32) / (HEAD_DIM // 2))
    places = (s_index - halo) * span + jnp.arange((halo + 1) * span)
    angles = places.astype(f32)[:, None] * frequency[None, :]

    plane = lax.axis_size("seq")
    groups = hidden // PAIR
    wide = -(-groups // plane) * PAIR
    spans = [(groups + plane - 1 - k) // plane * PAIR for k in range(plane)]
    firsts = [sum(spans[:k]) for k in range(plane)]

    def share_of(matrix, k):
        return jnp.pad(
            matrix[:, firsts[k] : firsts[k] + spans[k]], ((0, 0), (0, wide - spans[k]))
        )

    near = shifted(jnp.concatenate([mine, edge, ints], axis=0), "seq", 1)
    far = [shifted(jnp.concatenate([mine, ints], axis=0), "seq", k) for k in range(2, halo + 1)]
    low_f = to_low(feed_weights)
    block_f = jnp.concatenate(
        [
            jnp.concatenate([share_of(low_f[0], k), share_of(low_f[1], k)], axis=1)
            for k in range(plane)
        ],
        axis=0,
    )
    block_c = columns(
        cross_weights[1], cross_weights[2], self_weights[3], cross_weights[0], cross_weights[3]
    )
    if small:
        col_q = exchanged(wide_for_dp(block_q), "dp")
        spots = [s_index ^ k for k in range(plane)]
        shares = block_f.reshape(plane, shard_rows, 2 * wide)
        shares = [take(shares, spot, 0) for spot in spots]
        shares = shares[:1] + [swapped(shares[k], "seq", k) for k in range(1, plane)]
        col_q, near, block_c, angles, s_index, *rest = meet(
            col_q, near, block_c, angles, s_index, *shares, *far
        )
        shares, far = rest[:plane], rest[plane:]
        xy_q = from_seq(col_q)
    cos, sin = jnp.cos(angles), jnp.sin(angles)
    if small:
        turn = own_order(model, s_index)
        col_c = lax.all_gather(block_c, "dp", axis=0, tiled=True)
        cot_turned = turn_call(cot, turn)
    else:
        turn = jnp.eye(model, dtype=bf16)
        cot_turned = cot
    got = jnp.concatenate([near[: half + pad]] + [f[:half] for f in far], axis=0)
    other = swapped(got, "mp", 1)
    low_half = jnp.where(core == 0, got, other)
    high_half = jnp.where(core == 0, other, got)

    def whole(start, size):
        return [low_half[start : start + size], high_half[start : start + size]]

    pieces = []
    for k in range(halo, 1, -1):
        pieces += whole(half + pad + (k - 2) * half, half)
    x_ext = jnp.concatenate(pieces + whole(0, half) + [x_own], axis=0)
    flat_ext = jnp.concatenate(whole(half, pad) + [flat_own], axis=0)
    ints_prev = [near[half + pad]] + [f[half] for f in far]
    ints_prev = [p[None, : span + NEIGHBOURS].astype(jnp.int32) for p in ints_prev]
    seg_keys = jnp.concatenate([p[:, :span] for p in ints_prev[::-1]] + [seg_here], axis=1)
    seg_keys = seg_keys.reshape(-1, 1)
    lens = jnp.concatenate([ints_prev[0][:, span:], lengths], axis=0)
    before = jnp.concatenate([ints_prev[0][0, span - 1 : span], seg_here[0, : span - 1]])
    heads_of = jnp.repeat(before[::BLOCK], BLOCK)
    spot = jnp.arange(span)
    starts = jnp.where(s_index == 0, BLOCK, 0)
    keep = jnp.logical_or(spot == 0, jnp.logical_and(before == heads_of, spot >= starts))
    keep = keep.astype(f32).reshape(span, 1)

    if small:
        w_feed = jnp.broadcast_to(shares[0], (plane, shard_rows, 2 * wide))
        for spot, piece in zip(spots[1:], shares[1:]):
            w_feed = put(w_feed, piece[None], (spot, 0, 0))
        w_feed = w_feed.reshape(plane * shard_rows, 2 * wide)
        x_ext = turn_call(x_ext, turn)
        w_feed = lax.all_gather(w_feed, "dp", axis=0, tiled=True)
        col_c, turn, cot_turned, cos, sin, x_ext, flat_ext, cot, *xy_q = meet(
            col_c, turn, cot_turned, cos, sin, x_ext, flat_ext, cot, *xy_q
        )
        lead = 3 * width
        lead_c = from_seq(col_c[:, :lead])
        flat_ext = turn_call(flat_ext, turn)
        q_pieces = [col_q] + xy_q
        s_q, s_k, s_v = (weight(q_pieces, j * width) for j in range(3))
        gain_rows = jnp.concatenate(
            [p[:, 3 * width : 3 * width + PAIR] for p in q_pieces], axis=0
        )
    else:
        full_q, full_c = (
            lax.all_gather(b, ("dp", "seq"), axis=0, tiled=True) for b in (block_q, block_c)
        )
        w_feed = lax.all_to_all(block_f, "seq", 0, 0, tiled=True)
        w_feed = lax.all_gather(w_feed, "dp", axis=0, tiled=True)
        s_q, s_k, s_v = ([(full_q, j * width)] for j in range(3))
        gain_rows = full_q[:, 3 * width :]
        c_kv, s_o, c_q, c_o = ([(full_c, j * width)] for j in (0, 2, 3, 4))
    gains = gain_rows[:, :3].T.astype(f32)
    x = x_ext[halo * span :]
    n1, q, k, v = qkv_call(x_ext, gains[:1], s_q, s_k, s_v, cos, sin, span, width)
    if small:
        rest_c = col_c[:, lead:]
        q, flat_ext, seg_keys, lens, keep, cot, rest_c, *lead_c = meet(
            q, flat_ext, seg_keys, lens, keep, cot, rest_c, *lead_c
        )
        tail_c = from_seq(rest_c)
        c_kv, s_o = (weight([col_c] + lead_c, j * width) for j in (0, 2))
    def over_plane(rows):
        own = lax.dynamic_slice_in_dim(rows, core * half, half, 0)
        return [own] + [swapped(own, "seq", k) for k in range(1, plane)]

    def with_other(pieces):
        got = jnp.concatenate(pieces, axis=0)
        return jnp.concatenate([got, swapped(got, "mp", 1)], axis=0)

    def back_to_owner(own, other):
        total = own.astype(f32) + swapped(other, "mp", 1).astype(f32)
        sent = to_low(total)
        return [total[:half]] + [
            swapped(sent[k * half : (k + 1) * half], "seq", k) for k in range(1, plane)
        ]

    def f_assembled(got):
        got = got.reshape(plane, shard_rows, 2 * wide)
        return jnp.concatenate(
            [got[k, :, at : at + spans[k]] for at in (0, wide) for k in range(plane)], axis=1
        ).astype(f32)

    cot_rows = over_plane(cot)
    attn, lse, part = self_call(q, k, v, seg_here, seg_keys, s_o, model)
    kv2 = rows_call(flat_ext, c_kv, 2 * width)
    if small:
        part, kv2, *rest = meet(part, kv2, *tail_c, *cot_rows)
        tail_c, cot_rows = rest[:3], rest[3:]
        c_q, c_o = (weight([rest_c] + tail_c, j * width) for j in (0, 1))
    cot_rows = with_other(cot_rows)
    other = swapped(part, "mp", 1)
    if small:
        other, cot_rows = meet(other, cot_rows)
    h1, n2, q2, cross, lse2, part2 = cross_call(
        lens, x, part, other, gains[1:2], c_q, c_o, kv2, keep
    )
    other = swapped(part2, "mp", 1)
    h2, n3 = norm_call(h1, part2, other, gains[2:3], turn)

    n_rows = with_other(over_plane(n3))
    act, du, y_own, y_other, dn_own, dn_other = feed_call(n_rows, cot_rows, w_feed)
    dn3 = plane_sum(back_to_owner(dn_own, dn_other))
    dn3_other = swapped(dn3, "mp", 1)
    g2, low2, dgain3, dq2, dk2, dv2, dn2 = cross_back_call(
        lens, core.reshape(1), cot_turned, h2, dn3, dn3_other, turn, gains[2:3], c_q, c_o,
        q2, kv2, lse2, keep,
    )
    other = swapped(dn2, "mp", 1)
    cross_sent, cross_kept = halves(
        [(n2, dq2), (low2, cross)], [(flat_ext, dk2), (flat_ext, dv2)]
    )
    if small:
        *cross_sent, other, du, act = meet(*cross_sent, other, du, act)
        cross_got = reduce_first(cross_sent)
    g1, low1, dgain2, dq, dk, dv = self_back_call(
        g2, h1, dn2, other, gains[1:2], s_o, q, k, v, lse, seg_here, seg_keys, cos, sin
    )
    if small:
        *cross_got, low1, dq, dk, dv = meet(*cross_got, low1, dq, dk, dv)
        cross_kept, cross_got = reduce_second(cross_kept, cross_got)
    dn1, dgain1 = inner_call(x_ext, dq, dk, dv, s_q, s_k, s_v)
    dgain1 = core_sum(dgain1)
    dgains = jnp.concatenate(
        [dgain1, dgain2, dgain3, jnp.zeros((PAIR - 3, model), f32)], axis=0
    )
    self_sent, self_kept = halves(
        [(n1[halo * span :], dq), (low1, attn)],
        [(n1, dk), (n1, dv), (to_low(dgains), jnp.eye(PAIR, dtype=bf16))],
    )
    if small:
        sent_a, sent_b, got_a, got_b = meet(*self_sent, *cross_got)
        du, act, _ = meet(du, act, token_of(sent_a))
        self_got = reduce_first((sent_a, sent_b))
        cross_part = lax.psum_scatter(
            last_sum(cross_kept, (got_a, got_b)), "dp", scatter_dimension=0, tiled=True
        ).astype(f32)
        feed_grads = jnp.concatenate(
            [to_low(t_dot(n_rows, du)), to_low(t_dot(cot_rows, act))], axis=1
        )
        feed_low = lax.psum_scatter(feed_grads, "dp", scatter_dimension=0, tiled=True)
        *self_got, _ = meet(*self_got, token_of(feed_grads))
        self_kept, self_got = reduce_second(self_kept, self_got)
        got_a, got_b, dn1, y_own, y_other = meet(*self_got, dn1, y_own, y_other)
        self_got = exchanged(last_sum(self_kept, (got_a, got_b)), "dp")
    y_sums = back_to_owner(y_own, y_other)
    own = dn1[halo * span :]
    if halo:
        view = dn1[: halo * span].reshape(halo, 2, half, model)
        summed = to_low(take(view, core, 1) + swapped(take(view, 1 - core, 1), "mp", 1))
        if small:
            summed = to_low(dot_t(summed.reshape(-1, model), turn)).reshape(halo, half, model)
    back_parts = [shifted(summed[halo - k], "seq", -k) for k in range(1, halo + 1)]
    if small:
        squares = jnp.sum(cross_part * cross_part) + jnp.sum(jnp.square(feed_low.astype(f32)))
        self_part = reduce_last(self_got)
    else:
        feed_grads = jnp.concatenate(
            [to_low(t_dot(n_rows, du)), to_low(t_dot(cot_rows, act))], axis=1
        )
        feed_low = lax.psum_scatter(feed_grads, "dp", scatter_dimension=0, tiled=True)
        feed_part = f_assembled(exchanged(feed_low, "seq"))
        cross_part, self_part = reduce_plain(cross_kept), reduce_plain(self_kept)
        squares = jnp.sum(feed_part * feed_part) + jnp.sum(cross_part * cross_part)
    gains_part = self_part[:, 4 * width : 4 * width + 3].T
    first_model = (core == 0).astype(f32)
    local_squares = (
        jnp.sum(jnp.square(self_part[:, : 4 * width]))
        + squares
        + first_model * jnp.sum(gains_part * gains_part)
    )
    local_squares = local_squares.reshape(1, 1)
    if small:
        shares = [take(feed_low.reshape(plane, shard_rows, 2 * wide), spot, 0) for spot in spots]
        local_squares, *rest = meet(local_squares, *y_sums, *back_parts, *shares)
        y_sums, back_parts, shares = rest[:plane], rest[plane:-plane], rest[-plane:]
        shares = shares[:1] + [swapped(shares[k], "seq", k) for k in range(1, plane)]
        feed_got = jnp.zeros((plane, shard_rows, 2 * wide), bf16)
        for spot, piece in zip(spots, shares):
            feed_got = put(feed_got, piece[None], (spot, 0, 0))
        feed_part = f_assembled(feed_got)
    grad_norm = jnp.sqrt(sum_everywhere(local_squares).reshape(()))
    factor = jnp.minimum(1.0, clip_limit / (grad_norm + 1e-06))
    scalar = factor.reshape(1)
    mixed_order, plain = (0, 2, 3, 1), (0, 1)
    y_half = plane_sum(y_sums)
    y_other = swapped(y_half, "mp", 1)
    y_all = jnp.concatenate(
        [jnp.where(core == 0, y_half, y_other), jnp.where(core == 0, y_other, y_half)], axis=0
    )
    if halo:
        back = sum(p.astype(f32) for p in back_parts)
        if small:
            back = dot(to_low(back), turn)
        own = own + put(jnp.zeros_like(own), back, (core * half, 0))
    back, _ = rms_back(x.astype(f32), gains[:1], core_sum(own))
    in_grad = g1 + back

    def in_model_order(rows):
        high = to_low(lax.reduce_precision(rows, 8, 7))
        rest = rows - high.astype(f32)
        mid = to_low(lax.reduce_precision(rest, 8, 7))
        low = to_low(rest - mid.astype(f32))
        return dot_t(high, turn) + (dot_t(mid, turn) + dot_t(low, turn))

    if small:
        in_grad = in_model_order(in_grad)
        result = to_low(in_model_order(h2) + y_all)
    else:
        result = to_low(h2 + y_all)
    in_grad = in_grad.reshape(row_count, span, model)
    out = result.reshape(row_count, span, model)
    self_new, self_first_new, self_second_new = adam_call(
        scalar, self_weights, self_part, self_first, self_second, mixed_order
    )
    cross_new, cross_first_new, cross_second_new = adam_call(
        scalar, cross_weights, cross_part, cross_first, cross_second, mixed_order
    )
    feed_new, feed_first_new, feed_second_new = adam_call(
        scalar, feed_weights, feed_part, feed_first, feed_second, plain
    )
    gains_new, gains_first_new, gains_second_new = adam_step(
        norm_gains, gains_part, gains_first, gains_second, factor, gain_rate, 0.0
    )
    return (
        out,
        in_grad,
        grad_norm,
        self_new,
        cross_new,
        feed_new,
        gains_new,
        self_first_new,
        cross_first_new,
        feed_first_new,
        gains_first_new,
        self_second_new,
        cross_second_new,
        feed_second_new,
        gains_second_new,
    )


def solution(mesh):
    tok = P("dp", "seq", None)
    mat = P(None, ("dp", "seq"), "mp")
    vec = P(None, ("dp", "seq"))
    in_specs = (
        tok,
        P("dp", "seq", None, None, None),
        tok,
        P("dp", "seq"),
        tok,
    ) + (mat, mat, mat, vec) * 3
    out_specs = (tok, tok, P()) + (mat, mat, mat, vec) * 3
    return jax.shard_map(
        per_device, mesh=mesh, in_specs=in_specs, out_specs=out_specs, check_vma=False
    )
```

time: 516 us -> 469 us (0.909)
  waiting for transfers between devices: 184 us -> 104 us
  starting transfers between devices: 103 us -> 73.2 us
  matrix products: 10.6 us -> 29.5 us
  local copies, waits for them, and re-layouts: 53.2 us -> 68.4 us
  other arithmetic: 40.2 us -> 55.2 us
  Pallas kernels: 100 us -> 113 us
    ppermute x15 -> x0, waiting for transfers between devices: 54.1 us -> none  [rotated(): lax.ppermute(value, axis, [(i, (i + by) % count) for i in range(count)])]
    ppermute x15 -> x0, starting transfers between devices: 32 us -> none  [rotated(): lax.ppermute(value, axis, [(i, (i + by) % count) for i in range(count)])]
    ppermute x6 -> x4, waiting for transfers between devices: 25.5 us -> 2.13 us  [shifted(): lax.ppermute(value, axis, [(i, i + by) for i in range(count) if 0 <= i +...]
    ppermute x33 -> x48, waiting for transfers between devices: 104 us -> 86 us  [swapped(): return lax.ppermute(value, axis, [(i, i ^ by) for i in range(count)])]
    all_to_all x0 -> x3, starting transfers between devices: none -> 16.6 us  [the longest x2 9.11 us: exchanged(): return lax.all_to_all(array_in, axis, 0, 0, tiled=True)]
    dynamic_update_slice x17 -> x7, local copies, waits for them, and re-layouts: 18.2 us -> 2.79 us  [put(): return lax.dynamic_update_slice(buffer, piece, starts)]
    unnamed x108 -> x217, local copies, waits for them, and re-layouts: 7.92 us -> 22.3 us
    all_to_all x0 -> x3, waiting for transfers between devices: none -> 13.3 us  [the longest x2 13.3 us: exchanged(): return lax.all_to_all(array_in, axis, 0, 0, tiled=True)]
  transfers between devices with their start and end apart: 57 -> 59, of which waited for: 24 -> 28; matrix products, arithmetic and copies ran while one was open for 17% -> 25% of each run, Pallas kernels for 15% -> 17%
where the time goes in v3:
time: 469 us; the launch traced here: 463 us
  Pallas kernels  113 us (24%)
  waiting for transfers between devices  104 us (22%)
  starting transfers between devices  73.2 us (16%)
  local copies, waits for them, and re-layouts  68.4 us (15%)
  other arithmetic  55.2 us (12%)
  matrix products  29.5 us (6%)
  between operations  20.3 us (4%)
    pallas_call x17, Pallas kernels, call(): pl.pallas_call(body, out_shape=[jax.ShapeDtypeStruct(o[2], o[3]) for o in...  113 us
    ppermute x48, waiting for transfers between devices, swapped(): return lax.ppermute(value, axis, [(i, i ^ by) for i in range(count)])  86 us
    ppermute x48, starting transfers between devices, swapped(): return lax.ppermute(value, axis, [(i, i ^ by) for i in range(count)])  45.5 us
    unnamed x217, local copies, waits for them, and re-layouts  22.3 us
    dot_general x20, matrix products, t_dot(): lax.dot_general(a, b, (((0,), (0,)), ((), ())), preferred_element_type=f32)  20.1 us
    all_to_all x2, waiting for transfers between devices, exchanged(): return lax.all_to_all(array_in, axis, 0, 0, tiled=True)  13.3 us
    ppermute x4, starting transfers between devices, shifted(): lax.ppermute(value, axis, [(i, i + by) for i in range(count) if 0 <= i +...  10.1 us
  transfers between devices with their start and end apart: 59, of which 28 were waited for; matrix products, arithmetic and copies ran while one was open for 25% of the time, Pallas kernels for 17%

profile of v3, /device:TPU:0, one launch (start us, length us, event | category | flops | bytes accessed | tf_op | source)
XLA Modules:
  0.0 463.3 jit_solution(17105148222320354708)
XLA Ops:
  9.3 2.9 collective-permute-start.1
  15.1 3.9 collective-permute-start
  19.0 3.4 collective-permute-start.4
  24.9 4.9 %all-to-all-start = ((bf16[4,56,1664]{2,1,0:T(8,128)(2,1)}), bf16[4,56,1664]{2,1,0:T(8,128)(2,1)S(1)}, u32[]{:S(2)}, u32[]{:S(2)}) async-start(bf16[4,56,1664]{2,1,0:T(8,128)(2,1)} %broadcast_in_dim.26), calls=%async_computation | async-start | bytes 1490944 | tf_op jit(solution)/shard_map/all_to_all | solution.py:120
  32.2 2.1 collective-permute-done.4
  34.3 13.3 %all-to-all-done = bf16[4,56,1664]{2,1,0:T(8,128)(2,1)S(1)} async-done(((bf16[4,56,1664]{2,1,0:T(8,128)(2,1)}), bf16[4,56,1664]{2,1,0:T(8,128)(2,1)S(1)}, u32[]{:S(2)}, u32[]{:S(2)}) %all-to-all-start) | async-done | bytes 745504 | tf_op jit(solution)/shard_map/all_to_all | solution.py:120
  47.8 3.4 collective-permute-start.8
  61.0 1.8 fusion.refs_1_.refs_4_.refs_6_
  63.1 2.0 pad_add_fusion.1
  70.5 3.0 turn_kernel.3.refs_2_
  75.5 3.1 fusion.107
  82.1 5.0 %turn_kernel.4.refs_0_ = bf16[768,896]{1,0:T(8,128)(2,1)} custom-call(bf16[768,896]{1,0:T(8,128)(2,1)} %copy-done.24, bf16[896,896]{1,0:T(8,128)(2,1)} %fusion.refs_1_.refs_4_.refs_6_), custom_call_target="tpu_custom_call" | custom-call | tf_op jit(solution)/shard_map/turn_kernel/pallas_call | solution.py:213
  89.9 2.0 slice.385
  99.5 1.8 slice_reduce_fusion.2
  102.0 6.8 %turn_kernel.5.refs_0_ = bf16[1280,896]{1,0:T(8,128)(2,1)} custom-call(bf16[1280,896]{1,0:T(8,128)(2,1)} %pad_maximum_fusion.refs_0_, bf16[896,896]{1,0:T(8,128)(2,1)} %fusion.refs_1_.refs_4_.refs_6_), custom_call_target="tpu_custom_call" | custom-call | tf_op jit(solution)/shard_map/turn_kernel/pallas_call | solution.py:213
  108.8 6.5 %qkv_kernel.1 = (bf16[768,896]{1,0:T(8,128)(2,1)}, bf16[256,512]{1,0:T(8,128)(2,1)}, bf16[768,512]{1,0:T(8,128)(2,1)}, bf16[768,512]{1,0:T(8,128)(2,1)}) custom-call(bf16[768,896]{1,0:T(8,128)(2,1)} %turn_kernel.4.refs_0_, f32[1,896]{1,0:T(1,128)} %copy.175.refs_1_, bf16[224,1664]{1,0:T(8,128)(2,1)} %bitcast.171, bf16[224,1664]{1,0:T(8,128)(2,1)} %copy-done.2, ...), custom_call_target="tpu_custom_call" | custom-call | tf_op jit(solution)/shard_map/qkv_kernel/pallas_call | solution.py:213
  115.4 9.6 %collective-permute-done.11.refs_8_.refs_4_ = bf16[224,1536]{1,0:T(8,128)(2,1)} collective-permute-done((bf16[224,1536]{1,0:T(8,128)(2,1)}, bf16[224,1536]{1,0:T(8,128)(2,1)}, u32[]{:S(2)}, u32[]{:S(2)}) %collective-permute-start.11) | collective-permute-done | bytes 688160 | tf_op jit(solution)/shard_map/ppermute | solution.py:53
  129.5 1.9 collective-permute-start.14
  131.9 3.0 collective-permute-done.15
  138.3 6.7 %rows_kernel.1.refs_9_.refs_10_.refs_13_.refs_14_ = bf16[1280,1024]{1,0:T(8,128)(2,1)} custom-call(bf16[1280,896]{1,0:T(8,128)(2,1)} %turn_kernel.5.refs_0_, bf16[224,2560]{1,0:T(8,128)(2,1)} %all-gather.3.cloned.1.call-done.refs_5_.refs_1_, bf16[224,1536]{1,0:T(8,128)(2,1)} %collective-permute-done.9.refs_6_.refs_2_, ...), custom_call_target="tpu_custom_call" | custom-call | tf_op jit(solution)/shard_map/rows_kernel/pallas_call | solution.py:213
  145.1 10.2 %self_kernel.1 = (bf16[256,512]{1,0:T(8,128)(2,1)}, f32[4,2,256]{2,1,0:T(2,128)}, f32[256,896]{1,0:T(8,128)}) custom-call(bf16[256,512]{1,0:T(8,128)(2,1)} %get-tuple-element.187.refs_0_.refs_9_, bf16[768,512]{1,0:T(8,128)(2,1)} %get-tuple-element.188.refs_1_.refs_10_, bf16[768,512]{1,0:T(8,128)(2,1)} %get-tuple-element.189.refs_2_.refs_11_, ...), custom_call_target="tpu_custom_call" | custom-call | tf_op jit(solution)/shard_map/self_kernel/pallas_call | solution.py:213
  155.2 1.7 collective-permute-done.16
  157.7 2.2 pad_maximum_fusion.7
  163.6 1.8 slice.386.refs_1_
  170.3 9.3 %cross_kernel.1 = (f32[256,896]{1,0:T(8,128)}, bf16[256,896]{1,0:T(8,128)(2,1)}, bf16[256,512]{1,0:T(8,128)(2,1)}, bf16[256,512]{1,0:T(8,128)(2,1)}, f32[4,4,128]{2,1,0:T(4,128)}, /*index=5*/f32[256,896]{1,0:T(8,128)}) custom-call(s32[5,2]{1,0:T(8,128)} %copy.180.refs_0_, bf16[256,896]{1,0:T(8,128)(2,1)} %slice.386.refs_1_, ...), custom_call_target="tpu_custom_call" | custom-call | tf_op jit(solution)/shard_map/cross_kernel/pallas_call | solution.py:213
  180.5 1.9 collective-permute-done.20.refs_2_
  183.3 3.9 norm_kernel.1
  191.8 5.0 %collective-permute-done.21 = bf16[128,896]{1,0:T(8,128)(2,1)S(1)} collective-permute-done((bf16[128,896]{1,0:T(8,128)(2,1)S(1)}, bf16[128,896]{1,0:T(8,128)(2,1)S(1)}, u32[]{:S(2)}, u32[]{:S(2)}) %collective-permute-start.21) | collective-permute-done | bytes 229408 | tf_op jit(solution)/shard_map/ppermute | solution.py:53
  196.7 4.5 collective-permute-done.22
  201.5 2.4 collective-permute-done.24
  205.2 10.1 %feed_kernel.1 = (bf16[1024,512]{1,0:T(8,128)(2,1)}, bf16[1024,512]{1,0:T(8,128)(2,1)}, bf16[512,896]{1,0:T(8,128)(2,1)}, bf16[512,896]{1,0:T(8,128)(2,1)}, f32[512,896]{1,0:T(8,128)}, /*index=5*/f32[512,896]{1,0:T(8,128)}) custom-call(bf16[1024,896]{1,0:T(8,128)(2,1)} %copy-done.20, bf16[1024,896]{1,0:T(8,128)(2,1)} %copy-done.18, ...), custom_call_target="tpu_custom_call" | custom-call | tf_op jit(solution)/shard_map/feed_kernel/pallas_call | solution.py:213
  215.5 3.8 collective-permute-done.25
  226.2 3.3 collective-permute-done.26
  229.6 3.4 collective-permute-done.27
  233.0 1.8 collective-permute-done.28
  237.6 14.3 %cross_back_kernel.1 = (f32[256,896]{1,0:T(8,128)}, bf16[256,896]{1,0:T(8,128)(2,1)}, f32[1,896]{1,0:T(1,128)}, bf16[256,512]{1,0:T(8,128)(2,1)}, bf16[1280,512]...) custom-call(s32[5,2]{1,0:T(8,128)} %copy.180.refs_0_, s32[1]{0:T(128)} %bitcast.27.refs_1_, ...), custom_call_target="tpu_custom_call" | custom-call | tf_op jit(solution)/shard_map/cross_back_kernel/pallas_call | solution.py:213
  251.9 2.6 convolution_convert_fusion.15
  261.9 2.3 convolution_convert_fusion.4
  266.9 12.2 %self_back_kernel.1 = (f32[256,896]{1,0:T(8,128)}, bf16[256,896]{1,0:T(8,128)(2,1)}, f32[1,896]{1,0:T(1,128)}, bf16[256,512]{1,0:T(8,128)(2,1)}, bf16[768,512]{1,0:T(8,128)(2,1)}, /*index=5*/bf16[768,512]{1,0:T(8,128)(2,1)}) custom-call(f32[256,896]{1,0:T(8,128)} %get-tuple-element.235.refs_0_, f32[256,896]{1,0:T(8,128)} %get-tuple-element.209.refs_0_.refs_1_, ...), custom_call_target="tpu_custom_call" | custom-call | tf_op jit(solution)/shard_map/self_back_kernel/pallas_call | solution.py:213
  279.9 2.1 collective-permute-done.31.refs_1_
  282.3 2.4 convolution_convert_fusion.9
  285.8 7.3 %inner_kernel.1 = (f32[768,896]{1,0:T(8,128)}, f32[1,896]{1,0:T(1,128)}) custom-call(bf16[768,896]{1,0:T(8,128)(2,1)} %turn_kernel.4.refs_0_, bf16[256,512]{1,0:T(8,128)(2,1)} %get-tuple-element.242.refs_1_, bf16[768,512]{1,0:T(8,128)(2,1)} %get-tuple-element.245.refs_2_, bf16[768,512]{1,0:T(8,128)(2,1)} %get-tuple-element.246.refs_3_, ...), custom_call_target="tpu_custom_call" | custom-call | tf_op jit(solution)/shard_map/inner_kernel/pallas_call | solution.py:213
  293.6 3.8 half_sum_kernel.2
  303.4 7.1 %collective-permute-done.34 = bf16[224,1024]{1,0:T(8,128)(2,1)S(1)} collective-permute-done((bf16[224,1024]{1,0:T(8,128)(2,1)}, bf16[224,1024]{1,0:T(8,128)(2,1)S(1)}, u32[]{:S(2)}, u32[]{:S(2)}) %collective-permute-start.34) | collective-permute-done | bytes 458784 | tf_op jit(solution)/shard_map/ppermute | solution.py:53
  314.0 2.7 convolution_convert_fusion.1
  318.1 2.5 copy.199
  330.4 15.9 %collective-permute-done.36.refs_1_ = bf16[448,1024]{1,0:T(8,128)(2,1)S(1)} collective-permute-done((bf16[448,1024]{1,0:T(8,128)(2,1)}, bf16[448,1024]{1,0:T(8,128)(2,1)S(1)}, u32[]{:S(2)}, u32[]{:S(2)}) %collective-permute-start.36) | collective-permute-done | bytes 917536 | tf_op jit(solution)/shard_map/ppermute | solution.py:53
  346.3 2.1 collective-permute-done.37.refs_3_
  349.5 3.7 half_sum_kernel.3
  357.4 7.2 %collective-permute-done.38 = bf16[224,1024]{1,0:T(8,128)(2,1)S(1)} collective-permute-done((bf16[224,1024]{1,0:T(8,128)(2,1)}, bf16[224,1024]{1,0:T(8,128)(2,1)S(1)}, u32[]{:S(2)}, u32[]{:S(2)}) %collective-permute-start.38) | collective-permute-done | bytes 458784 | tf_op jit(solution)/shard_map/ppermute | solution.py:53
  369.1 4.2 all-to-all-start.1
  373.3 1.7 convert_element_type.336.refs_2_
  378.3 2.0 copy.200
  380.3 1.9 multiply_reduce_fusion
  383.5 1.8 dynamic-slice_bitcast_fusion.2
  393.6 2.6 collective-permute-start.41
  396.2 3.3 collective-permute-start.42
  405.9 4.0 collective-permute-done.42
  410.5 7.5 %all-to-all-start.2 = ((f32[32,8,128]{2,1,0:T(8,128)}), f32[32,8,128]{2,1,0:T(8,128)}, u32[]{:S(2)}, u32[]{:S(2)}) async-start(f32[32,8,128]{2,1,0:T(8,128)} %broadcast_in_dim.62), calls=%async_computation.3 | async-start | bytes 262144 | tf_op jit(solution)/shard_map/all_to_all | solution.py:71
  418.0 1.8 collective-permute-start.49
  423.2 2.0 add_add_fusion
  436.8 2.8 adam_kernel.3
  439.6 3.8 adam_kernel.5
  443.4 2.9 adam_kernel.4
  (461 shorter events, 160.0 us)
Async XLA Ops:
  9.3 22.9 %collective-permute-start.1 = (bf16[56,1024]{1,0:T(8,128)(2,1)}, bf16[56,1024]{1,0:T(8,128)(2,1)}, u32[]{:S(2)}, u32[]{:S(2)}) collective-permute-start(bf16[56,1024]{1,0:T(8,128)(2,1)} %get-tuple-element.437), channel_id=1, source_target_pairs={{0,2},{2,0},{4,6},{6,4},{1,3},{3,1},{5,7},{7,5},{8,10},{10,8},{12,... | collective-permute-start | bytes 344072 | tf_op jit(solution)/shard_map/ppermute | solution.py:53
  12.3 19.9 %collective-permute-start.2 = (bf16[56,1024]{1,0:T(8,128)(2,1)}, bf16[56,1024]{1,0:T(8,128)(2,1)}, u32[]{:S(2)}, u32[]{:S(2)}) collective-permute-start(bf16[56,1024]{1,0:T(8,128)(2,1)} %get-tuple-element.436), channel_id=1, source_target_pairs={{0,4},{2,6},{4,0},{6,2},{1,5},{3,7},{5,1},{7,3},{8,12},{10,14},{12... | collective-permute-start | bytes 344072 | tf_op jit(solution)/shard_map/ppermute | solution.py:53
  13.8 18.4 %collective-permute-start.3 = (bf16[56,1024]{1,0:T(8,128)(2,1)S(1)}, bf16[56,1024]{1,0:T(8,128)(2,1)}, u32[]{:S(2)}, u32[]{:S(2)}) collective-permute-start(bf16[56,1024]{1,0:T(8,128)(2,1)S(1)} %get-tuple-element.435), channel_id=1, source_target_pairs={{0,6},{2,4},{4,2},{6,0},{1,7},{3,5},{5,3},{7,1},{8,14},{10,12},{12... | collective-permute-start | bytes 344072 | tf_op jit(solution)/shard_map/ppermute | solution.py:53
  15.1 19.3 %collective-permute-start = (bf16[264,896]{1,0:T(8,128)(2,1)S(1)}, bf16[264,896]{1,0:T(8,128)(2,1)S(1)}, u32[]{:S(2)}, u32[]{:S(2)}) collective-permute-start(bf16[264,896]{1,0:T(8,128)(2,1)S(1)} %pad_maximum_fusion.27), channel_id=1, source_target_pairs={{0,2},{2,4},{4,6},{1,3},{3,5},{5,7},{8,10},{10,12},{12,14},{9,11},... | collective-permute-start | bytes 1419272 | tf_op jit(solution)/shard_map/ppermute | solution.py:43
  19.0 15.3 %collective-permute-start.4 = (bf16[136,896]{1,0:T(8,128)(2,1)S(1)}, bf16[136,896]{1,0:T(8,128)(2,1)S(1)}, u32[]{:S(2)}, u32[]{:S(2)}) collective-permute-start(bf16[136,896]{1,0:T(8,128)(2,1)S(1)} %pad_maximum_fusion.28), channel_id=1, source_target_pairs={{0,4},{2,6},{1,5},{3,7},{8,12},{10,14},{9,13},{11,15},{16,20},{18,... | collective-permute-start | bytes 731144 | tf_op jit(solution)/shard_map/ppermute | solution.py:43
  24.9 22.7 %all-to-all-start = ((bf16[4,56,1664]{2,1,0:T(8,128)(2,1)}), bf16[4,56,1664]{2,1,0:T(8,128)(2,1)S(1)}, u32[]{:S(2)}, u32[]{:S(2)}) async-start(bf16[4,56,1664]{2,1,0:T(8,128)(2,1)} %broadcast_in_dim.26), calls=%async_computation | async-start | bytes 1490944 | tf_op jit(solution)/shard_map/all_to_all | solution.py:120
  29.8 60.2 %all-gather.3.cloned.1.call-start = ((), (), s32[]{:S(2)}) async-start(), calls=%async_computation.5 | async-start | bytes 1433600 | tf_op jit(solution)/shard_map/all_gather | solution.py:947
  47.6 41.2 %collective-permute-start.6 = (bf16[224,1664]{1,0:T(8,128)(2,1)S(1)}, bf16[224,1664]{1,0:T(8,128)(2,1)S(1)}, u32[]{:S(2)}, u32[]{:S(2)}) collective-permute-start(bf16[224,1664]{1,0:T(8,128)(2,1)S(1)} %bitcast.167), channel_id=1, source_target_pairs={{0,4},{2,6},{4,0},{6,2},{1,5},{3,7},{5,1},{7,3},{8,12},{10,14},{12... | collective-permute-start | bytes 2236424 | tf_op jit(solution)/shard_map/ppermute | solution.py:53
  47.7 41.1 %collective-permute-start.7 = (bf16[224,1664]{1,0:T(8,128)(2,1)S(1)}, bf16[224,1664]{1,0:T(8,128)(2,1)S(1)}, u32[]{:S(2)}, u32[]{:S(2)}) collective-permute-start(bf16[224,1664]{1,0:T(8,128)(2,1)S(1)} %bitcast.168), channel_id=1, source_target_pairs={{0,2},{2,0},{4,6},{6,4},{1,3},{3,1},{5,7},{7,5},{8,10},{10,8},{12,... | collective-permute-start | bytes 2236424 | tf_op jit(solution)/shard_map/ppermute | solution.py:53
  47.8 41.0 %collective-permute-start.8 = (bf16[224,1664]{1,0:T(8,128)(2,1)S(1)}, bf16[224,1664]{1,0:T(8,128)(2,1)S(1)}, u32[]{:S(2)}, u32[]{:S(2)}) collective-permute-start(bf16[224,1664]{1,0:T(8,128)(2,1)S(1)} %bitcast.169), channel_id=1, source_target_pairs={{0,6},{2,4},{4,2},{6,0},{1,7},{3,5},{5,3},{7,1},{8,14},{10,12},{12... | collective-permute-start | bytes 2236424 | tf_op jit(solution)/shard_map/ppermute | solution.py:53
  61.0 17.5 %collective-permute-start.5 = (bf16[384,896]{1,0:T(8,128)(2,1)}, bf16[384,896]{1,0:T(8,128)(2,1)}, u32[]{:S(2)}, u32[]{:S(2)}) collective-permute-start(bf16[384,896]{1,0:T(8,128)(2,1)} %pad_maximum_fusion.22), channel_id=1, source_target_pairs={{0,1},{1,0},{2,3},{3,2},{4,5},{5,4},{6,7},{7,6},{8,9},{9,8},{10,11... | collective-permute-start | bytes 2064392 | tf_op jit(solution)/shard_map/ppermute | solution.py:53
  62.8 141.2 %all-gather.5.cloned.1.call-start = ((), (), s32[]{:S(2)}) async-start(), calls=%async_computation.6 | async-start | bytes 2293760 | tf_op jit(solution)/shard_map/all_gather | solution.py:983
  91.9 23.5 %collective-permute-start.10 = (bf16[224,1536]{1,0:T(8,128)(2,1)}, bf16[224,1536]{1,0:T(8,128)(2,1)}, u32[]{:S(2)}, u32[]{:S(2)}) collective-permute-start(bf16[224,1536]{1,0:T(8,128)(2,1)} %slice.385), channel_id=1, source_target_pairs={{0,2},{2,0},{4,6},{6,4},{1,3},{3,1},{5,7},{7,5},{8,10},{10,8},{12,... | collective-permute-start | bytes 2064392 | tf_op jit(solution)/shard_map/ppermute | solution.py:53
  93.4 31.6 %collective-permute-start.11 = (bf16[224,1536]{1,0:T(8,128)(2,1)}, bf16[224,1536]{1,0:T(8,128)(2,1)}, u32[]{:S(2)}, u32[]{:S(2)}) collective-permute-start(bf16[224,1536]{1,0:T(8,128)(2,1)} %slice.385), channel_id=1, source_target_pairs={{0,6},{2,4},{4,2},{6,0},{1,7},{3,5},{5,3},{7,1},{8,14},{10,12},{12... | collective-permute-start | bytes 2064392 | tf_op jit(solution)/shard_map/ppermute | solution.py:53
  94.8 31.5 %collective-permute-start.9 = (bf16[224,1536]{1,0:T(8,128)(2,1)}, bf16[224,1536]{1,0:T(8,128)(2,1)}, u32[]{:S(2)}, u32[]{:S(2)}) collective-permute-start(bf16[224,1536]{1,0:T(8,128)(2,1)} %slice.385), channel_id=1, source_target_pairs={{0,4},{2,6},{4,0},{6,2},{1,5},{3,7},{5,1},{7,3},{8,12},{10,14},{12... | collective-permute-start | bytes 2064392 | tf_op jit(solution)/shard_map/ppermute | solution.py:53
  98.5 31.0 %copy-start.7 = (bf16[224,1024]{1,0:T(8,128)(2,1)}, bf16[224,1024]{1,0:T(8,128)(2,1)S(1)}, u32[]{:S(2)}) copy-start(bf16[224,1024]{1,0:T(8,128)(2,1)S(1)} %slice.384.refs_5_.refs_12_.refs_8_.refs_17_) | copy-start | bytes 1376260
  108.8 28.5 %copy-start.82 = (s32[768,1]{0,1:T(1,128)S(1)}, s32[768,1]{0,1:T(1,128)}, u32[]{:S(2)}) copy-start(s32[768,1]{0,1:T(1,128)} %add_bitcast_fusion) | copy-start | bytes 9220
  126.3 8.6 %collective-permute-start.15 = (bf16[128,896]{1,0:T(8,128)(2,1)S(1)}, bf16[128,896]{1,0:T(8,128)(2,1)S(1)}, u32[]{:S(2)}, u32[]{:S(2)}) collective-permute-start(bf16[128,896]{1,0:T(8,128)(2,1)S(1)} %constant_dynamic-slice_fusion.1), channel_id=1, source_target_pairs={{0,2},{2,0},{4,6},{6,4},{1,3},{3,1},{5,7},{7,5},{8,10},{10,8},{12,... | collective-permute-start | bytes 688136 | tf_op jit(solution)/shard_map/ppermute | solution.py:53
  127.9 29.1 %collective-permute-start.12 = (bf16[224,1024]{1,0:T(8,128)(2,1)S(1)}, bf16[224,1024]{1,0:T(8,128)(2,1)S(1)}, u32[]{:S(2)}, u32[]{:S(2)}) collective-permute-start(bf16[224,1024]{1,0:T(8,128)(2,1)S(1)} %slice.384.refs_5_.refs_12_.refs_8_.refs_17_), channel_id=1, source_target_pairs={{0,4},{2,6},{4,0},{6,2},{1,5},{3,7},{5,1},{7,3},{8,12},{10,14},{12... | collective-permute-start | bytes 1376264 | tf_op jit(solution)/shard_map/ppermute | solution.py:53
  128.4 28.6 %collective-permute-start.13 = (bf16[224,1024]{1,0:T(8,128)(2,1)S(1)}, bf16[224,1024]{1,0:T(8,128)(2,1)S(1)}, u32[]{:S(2)}, u32[]{:S(2)}) collective-permute-start(bf16[224,1024]{1,0:T(8,128)(2,1)S(1)} %slice.384.refs_5_.refs_12_.refs_8_.refs_17_), channel_id=1, source_target_pairs={{0,2},{2,0},{4,6},{6,4},{1,3},{3,1},{5,7},{7,5},{8,10},{10,8},{12,... | collective-permute-start | bytes 1376264 | tf_op jit(solution)/shard_map/ppermute | solution.py:53
  129.5 27.5 %collective-permute-start.14 = (bf16[224,1024]{1,0:T(8,128)(2,1)S(1)}, bf16[224,1024]{1,0:T(8,128)(2,1)S(1)}, u32[]{:S(2)}, u32[]{:S(2)}) collective-permute-start(bf16[224,1024]{1,0:T(8,128)(2,1)S(1)} %slice.384.refs_5_.refs_12_.refs_8_.refs_17_), channel_id=1, source_target_pairs={{0,6},{2,4},{4,2},{6,0},{1,7},{3,5},{5,3},{7,1},{8,14},{10,12},{12... | collective-permute-start | bytes 1376264 | tf_op jit(solution)/shard_map/ppermute | solution.py:53
  131.3 25.6 %collective-permute-start.16 = (bf16[128,896]{1,0:T(8,128)(2,1)S(1)}, bf16[128,896]{1,0:T(8,128)(2,1)S(1)}, u32[]{:S(2)}, u32[]{:S(2)}) collective-permute-start(bf16[128,896]{1,0:T(8,128)(2,1)S(1)} %constant_dynamic-slice_fusion.1), channel_id=1, source_target_pairs={{0,4},{2,6},{4,0},{6,2},{1,5},{3,7},{5,1},{7,3},{8,12},{10,14},{12... | collective-permute-start | bytes 688136 | tf_op jit(solution)/shard_map/ppermute | solution.py:53
  134.9 22.8 %copy-start.44 = (bf16[128,896]{1,0:T(8,128)(2,1)}, bf16[128,896]{1,0:T(8,128)(2,1)S(1)}, u32[]{:S(2)}) copy-start(bf16[128,896]{1,0:T(8,128)(2,1)S(1)} %collective-permute-done.15) | copy-start | bytes 688132
  134.9 22.0 %collective-permute-start.17 = (bf16[128,896]{1,0:T(8,128)(2,1)S(1)}, bf16[128,896]{1,0:T(8,128)(2,1)S(1)}, u32[]{:S(2)}, u32[]{:S(2)}) collective-permute-start(bf16[128,896]{1,0:T(8,128)(2,1)S(1)} %constant_dynamic-slice_fusion.1), channel_id=1, source_target_pairs={{0,6},{2,4},{4,2},{6,0},{1,7},{3,5},{5,3},{7,1},{8,14},{10,12},{12... | collective-permute-start | bytes 688136 | tf_op jit(solution)/shard_map/ppermute | solution.py:53
  159.9 8.1 %collective-permute-start.19 = (bf16[512,896]{1,0:T(8,128)(2,1)}, bf16[512,896]{1,0:T(8,128)(2,1)}, u32[]{:S(2)}, u32[]{:S(2)}) collective-permute-start(bf16[512,896]{1,0:T(8,128)(2,1)} %pad_maximum_fusion.7), channel_id=1, source_target_pairs={{0,1},{1,0},{2,3},{3,2},{4,5},{5,4},{6,7},{7,6},{8,9},{9,8},{10,11... | collective-permute-start | bytes 2752520 | tf_op jit(solution)/shard_map/ppermute | solution.py:53
  159.9 9.5 %collective-permute-start.18 = (f32[256,896]{1,0:T(8,128)}, f32[256,896]{1,0:T(8,128)S(1)}, u32[]{:S(2)}, u32[]{:S(2)}) collective-permute-start(f32[256,896]{1,0:T(8,128)} %get-tuple-element.198.refs_2_), channel_id=1, source_target_pairs={{0,1},{1,0},{2,3},{3,2},{4,5},{5,4},{6,7},{7,6},{8,9},{9,8},{10,11... | collective-permute-start | bytes 2752520 | tf_op jit(solution)/shard_map/ppermute | solution.py:53
  163.0 210.3 %reduce-scatter.5.cloned.1.call-start = ((), (), s32[]{:S(2)}) async-start(), calls=%async_computation.7 | async-start | bytes 1146880 | tf_op jit(solution)/shard_map/reduce_scatter | solution.py:1086
  179.7 2.7 collective-permute-start.20
  188.2 8.5 %collective-permute-start.21 = (bf16[128,896]{1,0:T(8,128)(2,1)S(1)}, bf16[128,896]{1,0:T(8,128)(2,1)S(1)}, u32[]{:S(2)}, u32[]{:S(2)}) collective-permute-start(bf16[128,896]{1,0:T(8,128)(2,1)S(1)} %get-tuple-element.398), channel_id=1, source_target_pairs={{0,2},{2,0},{4,6},{6,4},{1,3},{3,1},{5,7},{7,5},{8,10},{10,8},{12,... | collective-permute-start | bytes 688136 | tf_op jit(solution)/shard_map/ppermute | solution.py:53
  188.9 12.3 %collective-permute-start.22 = (bf16[128,896]{1,0:T(8,128)(2,1)S(1)}, bf16[128,896]{1,0:T(8,128)(2,1)S(1)}, u32[]{:S(2)}, u32[]{:S(2)}) collective-permute-start(bf16[128,896]{1,0:T(8,128)(2,1)S(1)} %get-tuple-element.398), channel_id=1, source_target_pairs={{0,4},{2,6},{4,0},{6,2},{1,5},{3,7},{5,1},{7,3},{8,12},{10,14},{12... | collective-permute-start | bytes 688136 | tf_op jit(solution)/shard_map/ppermute | solution.py:53
  190.6 10.6 %collective-permute-start.23 = (bf16[128,896]{1,0:T(8,128)(2,1)S(1)}, bf16[128,896]{1,0:T(8,128)(2,1)S(1)}, u32[]{:S(2)}, u32[]{:S(2)}) collective-permute-start(bf16[128,896]{1,0:T(8,128)(2,1)S(1)} %get-tuple-element.398), channel_id=1, source_target_pairs={{0,6},{2,4},{4,2},{6,0},{1,7},{3,5},{5,3},{7,1},{8,14},{10,12},{12... | collective-permute-start | bytes 688136 | tf_op jit(solution)/shard_map/ppermute | solution.py:53
  201.3 2.5 collective-permute-start.24
  215.3 4.0 collective-permute-start.25
  221.1 8.5 %collective-permute-start.26 = (bf16[128,896]{1,0:T(8,128)(2,1)S(1)}, bf16[128,896]{1,0:T(8,128)(2,1)S(1)}, u32[]{:S(2)}, u32[]{:S(2)}) collective-permute-start(bf16[128,896]{1,0:T(8,128)(2,1)S(1)} %get-tuple-element.416), channel_id=1, source_target_pairs={{0,2},{2,0},{4,6},{6,4},{1,3},{3,1},{5,7},{7,5},{8,10},{10,8},{12,... | collective-permute-start | bytes 688136 | tf_op jit(solution)/shard_map/ppermute | solution.py:53
  222.5 10.5 %collective-permute-start.27 = (bf16[128,896]{1,0:T(8,128)(2,1)S(1)}, bf16[128,896]{1,0:T(8,128)(2,1)S(1)}, u32[]{:S(2)}, u32[]{:S(2)}) collective-permute-start(bf16[128,896]{1,0:T(8,128)(2,1)S(1)} %get-tuple-element.418), channel_id=1, source_target_pairs={{0,4},{2,6},{4,0},{6,2},{1,5},{3,7},{5,1},{7,3},{8,12},{10,14},{12... | collective-permute-start | bytes 688136 | tf_op jit(solution)/shard_map/ppermute | solution.py:53
  223.2 11.6 %collective-permute-start.28 = (bf16[128,896]{1,0:T(8,128)(2,1)S(1)}, bf16[128,896]{1,0:T(8,128)(2,1)S(1)}, u32[]{:S(2)}, u32[]{:S(2)}) collective-permute-start(bf16[128,896]{1,0:T(8,128)(2,1)S(1)} %get-tuple-element.417), channel_id=1, source_target_pairs={{0,6},{2,4},{4,2},{6,0},{1,7},{3,5},{5,3},{7,1},{8,14},{10,12},{12... | collective-permute-start | bytes 688136 | tf_op jit(solution)/shard_map/ppermute | solution.py:53
  234.9 1.9 collective-permute-start.29
  255.9 3.6 collective-permute-start.30
  259.5 22.5 %collective-permute-start.31 = (bf16[448,1024]{1,0:T(8,128)(2,1)S(1)}, bf16[448,1024]{1,0:T(8,128)(2,1)S(1)}, u32[]{:S(2)}, u32[]{:S(2)}) collective-permute-start(bf16[448,1024]{1,0:T(8,128)(2,1)S(1)} %pad_maximum_fusion.9), channel_id=1, source_target_pairs={{0,2},{2,0},{4,6},{6,4},{1,3},{3,1},{5,7},{7,5},{8,10},{10,8},{12,... | collective-permute-start | bytes 2752520 | tf_op jit(solution)/shard_map/ppermute | solution.py:53
  260.2 22.1 %collective-permute-start.32 = (bf16[448,1024]{1,0:T(8,128)(2,1)S(1)}, bf16[448,1024]{1,0:T(8,128)(2,1)S(1)}, u32[]{:S(2)}, u32[]{:S(2)}) collective-permute-start(bf16[448,1024]{1,0:T(8,128)(2,1)S(1)} %pad_maximum_fusion.10), channel_id=1, source_target_pairs={{0,4},{2,6},{4,0},{6,2},{1,5},{3,7},{5,1},{7,3},{8,12},{10,14},{12... | collective-permute-start | bytes 2752520 | tf_op jit(solution)/shard_map/ppermute | solution.py:53
  293.5 7.7 %collective-permute-start.33 = (f32[1,896]{1,0:T(1,128)}, f32[1,896]{1,0:T(1,128)S(1)}, u32[]{:S(2)}, u32[]{:S(2)}) collective-permute-start(f32[1,896]{1,0:T(1,128)} %get-tuple-element.247), channel_id=1, source_target_pairs={{0,1},{1,0},{2,3},{3,2},{4,5},{5,4},{6,7},{7,6},{8,9},{9,8},{10,11... | collective-permute-start | bytes 10760 | tf_op jit(solution)/shard_map/ppermute | solution.py:53
  297.5 13.1 %collective-permute-start.34 = (bf16[224,1024]{1,0:T(8,128)(2,1)}, bf16[224,1024]{1,0:T(8,128)(2,1)S(1)}, u32[]{:S(2)}, u32[]{:S(2)}) collective-permute-start(bf16[224,1024]{1,0:T(8,128)(2,1)} %get-tuple-element.252), channel_id=1, source_target_pairs={{0,4},{2,6},{4,0},{6,2},{1,5},{3,7},{5,1},{7,3},{8,12},{10,14},{12... | collective-permute-start | bytes 1376264 | tf_op jit(solution)/shard_map/ppermute | solution.py:53
  299.1 12.8 %collective-permute-start.35 = (bf16[224,1024]{1,0:T(8,128)(2,1)}, bf16[224,1024]{1,0:T(8,128)(2,1)S(1)}, u32[]{:S(2)}, u32[]{:S(2)}) collective-permute-start(bf16[224,1024]{1,0:T(8,128)(2,1)} %get-tuple-element.253), channel_id=1, source_target_pairs={{0,2},{2,0},{4,6},{6,4},{1,3},{3,1},{5,7},{7,5},{8,10},{10,8},{12,... | collective-permute-start | bytes 1376264 | tf_op jit(solution)/shard_map/ppermute | solution.py:53
  313.3 65.0 %reduce-scatter.7.cloned.1.call-start = ((), (), s32[]{:S(2)}) async-start(), calls=%async_computation.8 | async-start | bytes 2293760 | tf_op jit(solution)/shard_map/reduce_scatter | solution.py:1092
  324.1 24.4 %collective-permute-start.37 = (bf16[448,1152]{1,0:T(8,128)(2,1)}, bf16[448,1152]{1,0:T(8,128)(2,1)S(1)}, u32[]{:S(2)}, u32[]{:S(2)}) collective-permute-start(bf16[448,1152]{1,0:T(8,128)(2,1)} %pad_maximum_fusion.4), channel_id=1, source_target_pairs={{0,4},{2,6},{4,0},{6,2},{1,5},{3,7},{5,1},{7,3},{8,12},{10,14},{12... | collective-permute-start | bytes 3096584 | tf_op jit(solution)/shard_map/ppermute | solution.py:53
  324.5 21.8 %collective-permute-start.36 = (bf16[448,1024]{1,0:T(8,128)(2,1)}, bf16[448,1024]{1,0:T(8,128)(2,1)S(1)}, u32[]{:S(2)}, u32[]{:S(2)}) collective-permute-start(bf16[448,1024]{1,0:T(8,128)(2,1)} %pad_maximum_fusion.12), channel_id=1, source_target_pairs={{0,2},{2,0},{4,6},{6,4},{1,3},{3,1},{5,7},{7,5},{8,10},{10,8},{12,... | collective-permute-start | bytes 2752520 | tf_op jit(solution)/shard_map/ppermute | solution.py:53
  330.4 24.6 %copy-start = (bf16[896,896]{1,0:T(8,128)(2,1)S(1)}, bf16[896,896]{1,0:T(8,128)(2,1)}, u32[]{:S(2)}) copy-start(bf16[896,896]{1,0:T(8,128)(2,1)} %fusion.refs_1_.refs_4_.refs_6_) | copy-start | bytes 4816900
  330.4 24.6 %copy-start.8 = (f32[256,896]{1,0:T(8,128)S(1)}, f32[256,896]{1,0:T(8,128)}, u32[]{:S(2)}) copy-start(f32[256,896]{1,0:T(8,128)} %get-tuple-element.211.refs_3_) | copy-start | bytes 2752516
  353.2 12.3 %collective-permute-start.39 = (bf16[224,1152]{1,0:T(8,128)(2,1)}, bf16[224,1152]{1,0:T(8,128)(2,1)S(1)}, u32[]{:S(2)}, u32[]{:S(2)}) collective-permute-start(bf16[224,1152]{1,0:T(8,128)(2,1)} %get-tuple-element.260), channel_id=1, source_target_pairs={{0,2},{2,0},{4,6},{6,4},{1,3},{3,1},{5,7},{7,5},{8,10},{10,8},{12,... | collective-permute-start | bytes 1548296 | tf_op jit(solution)/shard_map/ppermute | solution.py:53
  353.8 10.8 %collective-permute-start.38 = (bf16[224,1024]{1,0:T(8,128)(2,1)}, bf16[224,1024]{1,0:T(8,128)(2,1)S(1)}, u32[]{:S(2)}, u32[]{:S(2)}) collective-permute-start(bf16[224,1024]{1,0:T(8,128)(2,1)} %get-tuple-element.259), channel_id=1, source_target_pairs={{0,4},{2,6},{4,0},{6,2},{1,5},{3,7},{5,1},{7,3},{8,12},{10,14},{12... | collective-permute-start | bytes 1376264 | tf_op jit(solution)/shard_map/ppermute | solution.py:53
  367.2 18.2 %collective-permute-start.44 = (f32[2,128,896]{2,1,0:T(8,128)}, f32[2,128,896]{2,1,0:T(8,128)}, u32[]{:S(2)}, u32[]{:S(2)}) collective-permute-start(f32[2,128,896]{2,1,0:T(8,128)} %dynamic-slice_bitcast_fusion), channel_id=1, source_target_pairs={{0,1},{1,0},{2,3},{3,2},{4,5},{5,4},{6,7},{7,6},{8,9},{9,8},{10,11... | collective-permute-start | bytes 2752520 | tf_op jit(solution)/shard_map/ppermute | solution.py:53
  367.2 24.1 %collective-permute-start.40 = (bf16[512,896]{1,0:T(8,128)(2,1)}, bf16[512,896]{1,0:T(8,128)(2,1)}, u32[]{:S(2)}, u32[]{:S(2)}) collective-permute-start(bf16[512,896]{1,0:T(8,128)(2,1)} %get-tuple-element.276), channel_id=1, source_target_pairs={{0,1},{1,0},{2,3},{3,2},{4,5},{5,4},{6,7},{7,6},{8,9},{9,8},{10,11... | collective-permute-start | bytes 2752520 | tf_op jit(solution)/shard_map/ppermute | solution.py:53
  369.1 31.3 %all-to-all-start.1 = ((bf16[4,56,2176]{2,1,0:T(8,128)(2,1)}), bf16[4,56,2176]{2,1,0:T(8,128)(2,1)}, u32[]{:S(2)}, u32[]{:S(2)}) async-start(bf16[4,56,2176]{2,1,0:T(8,128)(2,1)} %bitcast.179), calls=%async_computation.1 | async-start | bytes 1949696 | tf_op jit(solution)/shard_map/all_to_all | solution.py:120
  388.4 17.4 %collective-permute-start.45 = (bf16[128,896]{1,0:T(8,128)(2,1)}, bf16[128,896]{1,0:T(8,128)(2,1)}, u32[]{:S(2)}, u32[]{:S(2)}) collective-permute-start(bf16[128,896]{1,0:T(8,128)(2,1)} %get-tuple-element.434), channel_id=1, source_target_pairs={{2,0},{4,2},{6,4},{3,1},{5,3},{7,5},{10,8},{12,10},{14,12},{11,9},... | collective-permute-start | bytes 688136 | tf_op jit(solution)/shard_map/ppermute | solution.py:43
  389.7 16.2 %collective-permute-start.46 = (bf16[128,896]{1,0:T(8,128)(2,1)}, bf16[128,896]{1,0:T(8,128)(2,1)}, u32[]{:S(2)}, u32[]{:S(2)}) collective-permute-start(bf16[128,896]{1,0:T(8,128)(2,1)} %get-tuple-element.433), channel_id=1, source_target_pairs={{4,0},{6,2},{5,1},{7,3},{12,8},{14,10},{13,9},{15,11},{20,16},{22,... | collective-permute-start | bytes 688136 | tf_op jit(solution)/shard_map/ppermute | solution.py:43
  393.6 12.3 %collective-permute-start.41 = (bf16[128,896]{1,0:T(8,128)(2,1)}, bf16[128,896]{1,0:T(8,128)(2,1)}, u32[]{:S(2)}, u32[]{:S(2)}) collective-permute-start(bf16[128,896]{1,0:T(8,128)(2,1)} %get-tuple-element.415), channel_id=1, source_target_pairs={{0,2},{2,0},{4,6},{6,4},{1,3},{3,1},{5,7},{7,5},{8,10},{10,8},{12,... | collective-permute-start | bytes 688136 | tf_op jit(solution)/shard_map/ppermute | solution.py:53
  396.2 13.7 %collective-permute-start.42 = (bf16[128,896]{1,0:T(8,128)(2,1)}, bf16[128,896]{1,0:T(8,128)(2,1)}, u32[]{:S(2)}, u32[]{:S(2)}) collective-permute-start(bf16[128,896]{1,0:T(8,128)(2,1)} %get-tuple-element.414), channel_id=1, source_target_pairs={{0,4},{2,6},{4,0},{6,2},{1,5},{3,7},{5,1},{7,3},{8,12},{10,14},{12... | collective-permute-start | bytes 688136 | tf_op jit(solution)/shard_map/ppermute | solution.py:53
  399.5 10.3 %collective-permute-start.43 = (bf16[128,896]{1,0:T(8,128)(2,1)}, bf16[128,896]{1,0:T(8,128)(2,1)}, u32[]{:S(2)}, u32[]{:S(2)}) collective-permute-start(bf16[128,896]{1,0:T(8,128)(2,1)} %get-tuple-element.413), channel_id=1, source_target_pairs={{0,6},{2,4},{4,2},{6,0},{1,7},{3,5},{5,3},{7,1},{8,14},{10,12},{12... | collective-permute-start | bytes 688136 | tf_op jit(solution)/shard_map/ppermute | solution.py:53
  410.5 18.9 %all-to-all-start.2 = ((f32[32,8,128]{2,1,0:T(8,128)}), f32[32,8,128]{2,1,0:T(8,128)}, u32[]{:S(2)}, u32[]{:S(2)}) async-start(f32[32,8,128]{2,1,0:T(8,128)} %broadcast_in_dim.62), calls=%async_computation.3 | async-start | bytes 262144 | tf_op jit(solution)/shard_map/all_to_all | solution.py:71
  418.0 7.7 %collective-permute-start.49 = (bf16[56,1024]{1,0:T(8,128)(2,1)}, bf16[56,1024]{1,0:T(8,128)(2,1)S(1)}, u32[]{:S(2)}, u32[]{:S(2)}) collective-permute-start(bf16[56,1024]{1,0:T(8,128)(2,1)} %get-tuple-element.289), channel_id=1, source_target_pairs={{0,2},{2,0},{4,6},{6,4},{1,3},{3,1},{5,7},{7,5},{8,10},{10,8},{12,... | collective-permute-start | bytes 344072 | tf_op jit(solution)/shard_map/ppermute | solution.py:53
  419.8 7.3 %collective-permute-start.50 = (bf16[56,1024]{1,0:T(8,128)(2,1)}, bf16[56,1024]{1,0:T(8,128)(2,1)S(1)}, u32[]{:S(2)}, u32[]{:S(2)}) collective-permute-start(bf16[56,1024]{1,0:T(8,128)(2,1)} %get-tuple-element.290), channel_id=1, source_target_pairs={{0,4},{2,6},{4,0},{6,2},{1,5},{3,7},{5,1},{7,3},{8,12},{10,14},{12... | collective-permute-start | bytes 344072 | tf_op jit(solution)/shard_map/ppermute | solution.py:53
  421.2 7.1 %collective-permute-start.51 = (bf16[56,1024]{1,0:T(8,128)(2,1)}, bf16[56,1024]{1,0:T(8,128)(2,1)S(1)}, u32[]{:S(2)}, u32[]{:S(2)}) collective-permute-start(bf16[56,1024]{1,0:T(8,128)(2,1)} %get-tuple-element.291), channel_id=1, source_target_pairs={{0,6},{2,4},{4,2},{6,0},{1,7},{3,5},{5,3},{7,1},{8,14},{10,12},{12... | collective-permute-start | bytes 344072 | tf_op jit(solution)/shard_map/ppermute | solution.py:53
  423.1 26.0 %collective-permute-start.48 = (f32[256,896]{1,0:T(8,128)S(1)}, f32[256,896]{1,0:T(8,128)}, u32[]{:S(2)}, u32[]{:S(2)}) collective-permute-start(f32[256,896]{1,0:T(8,128)S(1)} %add_dynamic-update-slice_fusion), channel_id=1, source_target_pairs={{0,1},{1,0},{2,3},{3,2},{4,5},{5,4},{6,7},{7,6},{8,9},{9,8},{10,11... | collective-permute-start | bytes 2752520 | tf_op jit(solution)/shard_map/ppermute | solution.py:53
  425.2 21.2 %collective-permute-start.47 = (f32[128,896]{1,0:T(8,128)}, f32[128,896]{1,0:T(8,128)}, u32[]{:S(2)}, u32[]{:S(2)}) collective-permute-start(f32[128,896]{1,0:T(8,128)} %add_add_fusion), channel_id=1, source_target_pairs={{0,1},{1,0},{2,3},{3,2},{4,5},{5,4},{6,7},{7,6},{8,9},{9,8},{10,11... | collective-permute-start | bytes 1376264 | tf_op jit(solution)/shard_map/ppermute | solution.py:53
  (90 other events, 511.6 us)
Sparse Core Ops, SparseCore 0:
  62.9 26.9 all-gather.2
  163.1 40.3 all-gather.4
  313.5 24.2 reduce-scatter.4
  339.9 38.3 reduce-scatter.6

commit v4 on v3

--- a/solution.py
+++ b/solution.py
@@ -87,10 +87,6 @@
     return lax.optimization_barrier(values)
 
 
-def token_of(array_in):
-    return array_in[:8, :PAIR]
-
-
 ORDER = (0, 2, 1, 3)
 
 
@@ -135,12 +131,6 @@
 def reduce_second(kept, got):
     keep_a, keep_b, sent_a, sent_b = half_sum_call(kept, got)
     return (keep_a, keep_b), (swapped(sent_a, "seq", 2), swapped(sent_b, "seq", 1))
-
-
-def last_sum(kept, got):
-    return jnp.concatenate(
-        [to_low(k.astype(f32) + g.astype(f32)) for k, g in zip(kept, got)], axis=1
-    )
 
 
 def reduce_last(got):
@@ -771,29 +761,74 @@
     )
 
 
-def adam_call(factor, weights, grads, first, second, order):
-    count, rows, width = weights.shape
-
-    def adam_kernel(factor_ref, w_ref, g_ref, m_ref, v_ref, wo_ref, mo_ref, vo_ref):
-        for j, at in enumerate(order):
-            wo_ref[j], mo_ref[j], vo_ref[j] = adam_step(
-                w_ref[j],
-                g_ref[:, at * width : (at + 1) * width],
-                m_ref[j],
-                v_ref[j],
-                factor_ref[0],
-                learn_rate,
-                weight_decay,
-            )
-
-    block = (weights.shape, lambda i, *_: (0, 0, 0))
-    return call(
-        adam_kernel,
+def adam_call(factor, groups):
+    orders = [g[4] for g in groups]
+    counts = len(groups)
+
+    def adam_kernel(factor_ref, *refs):
+        ins, outs = refs[: 4 * counts], refs[4 * counts :]
+        for n, order in enumerate(orders):
+            w_ref, g_ref, m_ref, v_ref = ins[4 * n : 4 * n + 4]
+            wo_ref, mo_ref, vo_ref = outs[3 * n : 3 * n + 3]
+            width = w_ref.shape[2]
+            for j, at in enumerate(order):
+                wo_ref[j], mo_ref[j], vo_ref[j] = adam_step(
+                    w_ref[j],
+                    g_ref[:, at * width : (at + 1) * width],
+                    m_ref[j],
+                    v_ref[j],
+                    factor_ref[0],
+                    learn_rate,
+                    weight_decay,
+                )
+
+    def whole(a):
+        return (a.shape, lambda i, *_, n=a.ndim: (0,) * n)
+
+    arrays = [a for g in groups for a in g[:4]]
+    results = [whole(g[0]) + (g[0].shape, f32) for g in groups for _ in range(3)]
+    return call(
+        adam_kernel, (1,), [whole(a) for a in arrays], results, (factor, *arrays), prefetch=1
+    )
+
+
+def last_sum_kernel(ka, ga, kb, gb, o_ref, mark_ref):
+    mark_ref[...] = jnp.zeros_like(mark_ref)
+    wide = ka.shape[1]
+    o_ref[:, :wide] = to_low(ka[...].astype(f32) + ga[...].astype(f32))
+    o_ref[:, wide:] = to_low(kb[...].astype(f32) + gb[...].astype(f32))
+
+
+def last_sum_call(kept, got):
+    rows, wide_a = kept[0].shape
+    wide_b = kept[1].shape[1]
+    fix = lambda i: (0, 0)
+    a, b, o = (rows, wide_a), (rows, wide_b), (rows, wide_a + wide_b)
+    return call(
+        last_sum_kernel,
         (1,),
-        [block, (grads.shape, lambda i, *_: (0, 0)), block, block],
-        [block + (weights.shape, f32)] * 3,
-        (factor, weights, grads, first, second),
-        prefetch=1,
+        [(a, fix), (a, fix), (b, fix), (b, fix)],
+        [(o, fix, o, bf16), ((8, PAIR), fix, (8, PAIR), f32)],
+        (kept[0], got[0], kept[1], got[1]),
+    )
+
+
+def total_kernel(got_ref, mark_ref, o_ref, squares_ref):
+    rows = o_ref.shape[0]
+    total = got_ref[:rows].astype(f32)
+    for k in range(1, 4):
+        total = total + got_ref[k * rows : (k + 1) * rows].astype(f32)
+    o_ref[...] = total
+    squares_ref[...] = jnp.sum(jnp.sum(total * total, axis=0, keepdims=True), axis=1, keepdims=True)
+
+
+def total_call(got, mark):
+    rows, cols = got.shape
+    fix = lambda i: (0, 0)
+    out = (rows // 4, cols)
+    return call(
+        total_kernel, (1,), [((rows, cols), fix), ((8, PAIR), fix)],
+        [(out, fix, out, f32), ((1, 1), fix, (1, 1), f32)], (got, mark),
     )
 
 
@@ -824,6 +859,36 @@
         [(a, turn), (a, turn), (b, turn), (b, turn)],
         [(a, fix, a, bf16), (b, fix, b, bf16), (a, fix, a, bf16), (b, fix, b, bf16)],
         (kept[0], got[0], kept[1], got[1]),
+    )
+
+
+def pack_call(place, own, cross, feed, gain_cols, firsts, spans, wide):
+    _, rows, width = own.shape
+    plane = len(spans)
+
+    def pack_kernel(place_ref, own_ref, cross_ref, feed_ref, gain_ref, q_ref, c_ref, f_ref):
+        for j in range(3):
+            q_ref[:, j * width : (j + 1) * width] = to_low(own_ref[j])
+        q_ref[:, 3 * width :] = to_low(gain_ref[...])
+        for j, part in enumerate((cross_ref[1], cross_ref[2], own_ref[3], cross_ref[0], cross_ref[3])):
+            c_ref[:, j * width : (j + 1) * width] = to_low(part)
+        for k in range(plane):
+            pieces = []
+            for m in range(2):
+                pieces.append(to_low(feed_ref[m, :, firsts[k] : firsts[k] + spans[k]]))
+                if spans[k] < wide:
+                    pieces.append(jnp.zeros((rows, wide - spans[k]), bf16))
+            f_ref[place_ref[k]] = jnp.concatenate(pieces, axis=1)
+
+    whole = lambda a: (a.shape, lambda i, *_: (0,) * a.ndim)
+    outs = [(rows, 3 * width + PAIR), (rows, 5 * width), (plane, rows, 2 * wide)]
+    return call(
+        pack_kernel,
+        (1,),
+        [whole(own), whole(cross), whole(feed), whole(gain_cols)],
+        [(o, lambda i, *_, n=len(o): (0,) * n, o, bf16) for o in outs],
+        (place, own, cross, feed, gain_cols),
+        prefetch=1,
     )
 
 
@@ -891,7 +956,6 @@
         return jnp.concatenate([to_low(p) for p in parts], axis=1)
 
     gain_cols = jnp.zeros((shard_rows, PAIR), f32).at[:, :3].set(norm_gains.T)
-    block_q = columns(self_weights[0], self_weights[1], self_weights[2], gain_cols)
     small = small_mesh()
     x_own, cot = tokens.reshape(span, model), out_grad.reshape(span, model)
     flat_own = neighbours.reshape(-1, model)
@@ -912,35 +976,23 @@
     spans = [(groups + plane - 1 - k) // plane * PAIR for k in range(plane)]
     firsts = [sum(spans[:k]) for k in range(plane)]
 
-    def share_of(matrix, k):
-        return jnp.pad(
-            matrix[:, firsts[k] : firsts[k] + spans[k]], ((0, 0), (0, wide - spans[k]))
-        )
-
+    small = small_mesh()
+    places_of = [s_index ^ k if small else k for k in range(plane)]
+    block_q, block_c, block_f = pack_call(
+        jnp.stack([jnp.asarray(p, jnp.int32) for p in places_of]),
+        self_weights, cross_weights, feed_weights, gain_cols, firsts, spans, wide,
+    )
     near = shifted(jnp.concatenate([mine, edge, ints], axis=0), "seq", 1)
     far = [shifted(jnp.concatenate([mine, ints], axis=0), "seq", k) for k in range(2, halo + 1)]
-    low_f = to_low(feed_weights)
-    block_f = jnp.concatenate(
-        [
-            jnp.concatenate([share_of(low_f[0], k), share_of(low_f[1], k)], axis=1)
-            for k in range(plane)
-        ],
-        axis=0,
-    )
-    block_c = columns(
-        cross_weights[1], cross_weights[2], self_weights[3], cross_weights[0], cross_weights[3]
-    )
     if small:
         col_q = exchanged(wide_for_dp(block_q), "dp")
         spots = [s_index ^ k for k in range(plane)]
-        shares = block_f.reshape(plane, shard_rows, 2 * wide)
-        shares = [take(shares, spot, 0) for spot in spots]
+        col_q, near, block_c, block_f, angles, s_index, *far = meet(
+            col_q, near, block_c, block_f, angles, s_index, *far
+        )
+        shares = [block_f[k] for k in range(plane)]
+        xy_q = from_seq(col_q)
         shares = shares[:1] + [swapped(shares[k], "seq", k) for k in range(1, plane)]
-        col_q, near, block_c, angles, s_index, *rest = meet(
-            col_q, near, block_c, angles, s_index, *shares, *far
-        )
-        shares, far = rest[:plane], rest[plane:]
-        xy_q = from_seq(col_q)
     cos, sin = jnp.cos(angles), jnp.sin(angles)
     if small:
         turn = own_order(model, s_index)
@@ -975,15 +1027,16 @@
     keep = keep.astype(f32).reshape(span, 1)
 
     if small:
+        x_ext = turn_call(x_ext, turn)
+        col_c, turn, cot_turned, cos, sin, x_ext, flat_ext, cot, *rest = meet(
+            col_c, turn, cot_turned, cos, sin, x_ext, flat_ext, cot, *xy_q, *shares
+        )
+        xy_q, shares = rest[:3], rest[3:]
         w_feed = jnp.broadcast_to(shares[0], (plane, shard_rows, 2 * wide))
         for spot, piece in zip(spots[1:], shares[1:]):
             w_feed = put(w_feed, piece[None], (spot, 0, 0))
         w_feed = w_feed.reshape(plane * shard_rows, 2 * wide)
-        x_ext = turn_call(x_ext, turn)
         w_feed = lax.all_gather(w_feed, "dp", axis=0, tiled=True)
-        col_c, turn, cot_turned, cos, sin, x_ext, flat_ext, cot, *xy_q = meet(
-            col_c, turn, cot_turned, cos, sin, x_ext, flat_ext, cot, *xy_q
-        )
         lead = 3 * width
         lead_c = from_seq(col_c[:, :lead])
         flat_ext = turn_call(flat_ext, turn)
@@ -996,7 +1049,7 @@
         full_q, full_c = (
             lax.all_gather(b, ("dp", "seq"), axis=0, tiled=True) for b in (block_q, block_c)
         )
-        w_feed = lax.all_to_all(block_f, "seq", 0, 0, tiled=True)
+        w_feed = exchanged(block_f.reshape(plane * shard_rows, 2 * wide), "seq")
         w_feed = lax.all_gather(w_feed, "dp", axis=0, tiled=True)
         s_q, s_k, s_v = ([(full_q, j * width)] for j in range(3))
         gain_rows = full_q[:, 3 * width :]
@@ -1032,20 +1085,19 @@
             [got[k, :, at : at + spans[k]] for at in (0, wide) for k in range(plane)], axis=1
         ).astype(f32)
 
-    cot_rows = over_plane(cot)
     attn, lse, part = self_call(q, k, v, seg_here, seg_keys, s_o, model)
     kv2 = rows_call(flat_ext, c_kv, 2 * width)
     if small:
-        part, kv2, *rest = meet(part, kv2, *tail_c, *cot_rows)
-        tail_c, cot_rows = rest[:3], rest[3:]
+        part, kv2, cot, *tail_c = meet(part, kv2, cot, *tail_c)
         c_q, c_o = (weight([rest_c] + tail_c, j * width) for j in (0, 1))
-    cot_rows = with_other(cot_rows)
+    cot_rows = over_plane(cot)
     other = swapped(part, "mp", 1)
-    if small:
-        other, cot_rows = meet(other, cot_rows)
     h1, n2, q2, cross, lse2, part2 = cross_call(
         lens, x, part, other, gains[1:2], c_q, c_o, kv2, keep
     )
+    if small:
+        part2, *cot_rows = meet(part2, *cot_rows)
+    cot_rows = with_other(cot_rows)
     other = swapped(part2, "mp", 1)
     h2, n3 = norm_call(h1, part2, other, gains[2:3], turn)
 
@@ -1071,29 +1123,39 @@
         *cross_got, low1, dq, dk, dv = meet(*cross_got, low1, dq, dk, dv)
         cross_kept, cross_got = reduce_second(cross_kept, cross_got)
     dn1, dgain1 = inner_call(x_ext, dq, dk, dv, s_q, s_k, s_v)
-    dgain1 = core_sum(dgain1)
-    dgains = jnp.concatenate(
-        [dgain1, dgain2, dgain3, jnp.zeros((PAIR - 3, model), f32)], axis=0
-    )
+    if small:
+        dn1, dgain1, dq, dk, dv, low1, *cross_got = meet(
+            dn1, dgain1, dq, dk, dv, low1, *cross_got
+        )
+    dgains = jnp.concatenate([dgain1, 0.5 * dgain2, 0.5 * dgain3], axis=0)
+    if small:
+        dgains = jnp.dot(dgains, turn.T.astype(f32), precision=lax.Precision.HIGHEST)
+        slots = jnp.pad(
+            dgains.reshape(3, -1, shard_rows).transpose(1, 0, 2),
+            ((0, 0), (0, 5), (0, PAIR - shard_rows)),
+        )
+        slots = jnp.repeat(slots, lax.axis_size("mp"), axis=0)
     self_sent, self_kept = halves(
         [(n1[halo * span :], dq), (low1, attn)],
-        [(n1, dk), (n1, dv), (to_low(dgains), jnp.eye(PAIR, dtype=bf16))],
-    )
-    if small:
-        sent_a, sent_b, got_a, got_b = meet(*self_sent, *cross_got)
-        du, act, _ = meet(du, act, token_of(sent_a))
+        [(n1, dk), (n1, dv)],
+    )
+    if small:
+        sent_a, sent_b, slots, du, act = meet(*self_sent, slots, du, act)
         self_got = reduce_first((sent_a, sent_b))
+        slots = lax.all_to_all(slots, ("dp", "seq", "mp"), 0, 0, tiled=True)
+        gains_part = jnp.sum(slots, axis=0)[:3, :shard_rows]
         cross_part = lax.psum_scatter(
-            last_sum(cross_kept, (got_a, got_b)), "dp", scatter_dimension=0, tiled=True
+            last_sum_call(cross_kept, cross_got)[0], "dp", scatter_dimension=0, tiled=True
         ).astype(f32)
         feed_grads = jnp.concatenate(
             [to_low(t_dot(n_rows, du)), to_low(t_dot(cot_rows, act))], axis=1
         )
         feed_low = lax.psum_scatter(feed_grads, "dp", scatter_dimension=0, tiled=True)
-        *self_got, _ = meet(*self_got, token_of(feed_grads))
+        *self_got, gains_part = meet(*self_got, gains_part)
         self_kept, self_got = reduce_second(self_kept, self_got)
-        got_a, got_b, dn1, y_own, y_other = meet(*self_got, dn1, y_own, y_other)
-        self_got = exchanged(last_sum(self_kept, (got_a, got_b)), "dp")
+        self_col, mark = last_sum_call(self_kept, meet(*self_got))
+        dn1, y_own, y_other, mark = meet(dn1, y_own, y_other, mark)
+        self_got = exchanged(self_col, "dp")
     y_sums = back_to_owner(y_own, y_other)
     own = dn1[halo * span :]
     if halo:
@@ -1104,7 +1166,8 @@
     back_parts = [shifted(summed[halo - k], "seq", -k) for k in range(1, halo + 1)]
     if small:
         squares = jnp.sum(cross_part * cross_part) + jnp.sum(jnp.square(feed_low.astype(f32)))
-        self_part = reduce_last(self_got)
+        self_got, squares = meet(self_got, squares)
+        self_part, self_squares = total_call(self_got, mark)
     else:
         feed_grads = jnp.concatenate(
             [to_low(t_dot(n_rows, du)), to_low(t_dot(cot_rows, act))], axis=1
@@ -1113,14 +1176,17 @@
         feed_part = f_assembled(exchanged(feed_low, "seq"))
         cross_part, self_part = reduce_plain(cross_kept), reduce_plain(self_kept)
         squares = jnp.sum(feed_part * feed_part) + jnp.sum(cross_part * cross_part)
-    gains_part = self_part[:, 4 * width : 4 * width + 3].T
+        self_squares = jnp.sum(jnp.square(self_part)).reshape(1, 1)
+    if not small:
+        gain_sums = butterfly(dgains, ("mp", "seq", "dp"))
+        shard = lax.axis_index("dp") * lax.axis_size("seq") + s_index
+        gains_part = lax.dynamic_slice_in_dim(gain_sums, shard * shard_rows, shard_rows, axis=1)
     first_model = (core == 0).astype(f32)
     local_squares = (
-        jnp.sum(jnp.square(self_part[:, : 4 * width]))
+        self_squares
         + squares
         + first_model * jnp.sum(gains_part * gains_part)
     )
-    local_squares = local_squares.reshape(1, 1)
     if small:
         shares = [take(feed_low.reshape(plane, shard_rows, 2 * wide), spot, 0) for spot in spots]
         local_squares, *rest = meet(local_squares, *y_sums, *back_parts, *shares)
@@ -1161,14 +1227,17 @@
         result = to_low(h2 + y_all)
     in_grad = in_grad.reshape(row_count, span, model)
     out = result.reshape(row_count, span, model)
-    self_new, self_first_new, self_second_new = adam_call(
-        scalar, self_weights, self_part, self_first, self_second, mixed_order
-    )
-    cross_new, cross_first_new, cross_second_new = adam_call(
-        scalar, cross_weights, cross_part, cross_first, cross_second, mixed_order
-    )
-    feed_new, feed_first_new, feed_second_new = adam_call(
-        scalar, feed_weights, feed_part, feed_first, feed_second, plain
+    (
+        self_new, self_first_new, self_second_new,
+        cross_new, cross_first_new, cross_second_new,
+        feed_new, feed_first_new, feed_second_new,
+    ) = adam_call(
+        scalar,
+        [
+            (self_weights, self_part, self_first, self_second, mixed_order),
+            (cross_weights, cross_part, cross_first, cross_second, mixed_order),
+            (feed_weights, feed_part, feed_first, feed_second, plain),
+        ],
     )
     gains_new, gains_first_new, gains_second_new = adam_step(
         norm_gains, gains_part, gains_first, gains_second, factor, gain_rate, 0.0

time: 469 us -> 443 us (0.945)
  waiting for transfers between devices: 104 us -> 72.5 us
  other arithmetic: 55.2 us -> 45.2 us
  Pallas kernels: 113 us -> 120 us
  matrix products: 29.5 us -> 36.1 us
  starting transfers between devices: 73.2 us -> 78.4 us
    ppermute x48 -> x47, waiting for transfers between devices: 86 us -> 61.5 us  [swapped(): return lax.ppermute(value, axis, [(i, i ^ by) for i in range(count)])]
    all_to_all x2, waiting for transfers between devices: 13.3 us -> 0.01 us  [exchanged(): return lax.all_to_all(array_in, axis, 0, 0, tiled=True)]
    ppermute x4, waiting for transfers between devices: 2.13 us -> 10.2 us  [shifted(): lax.ppermute(value, axis, [(i, i + by) for i in range(count) if 0 <= i +...]
    pallas_call x17 -> x19, Pallas kernels: 113 us -> 120 us  [call(): pl.pallas_call(body, out_shape=[jax.ShapeDtypeStruct(o[2], o[3]) for o in...]
    dot_general x20 -> x18, matrix products: 20.1 us -> 24.7 us  [t_dot(): lax.dot_general(a, b, (((0,), (0,)), ((), ())), preferred_element_type=f32)]
    unnamed x217 -> x182, local copies, waits for them, and re-layouts: 22.3 us -> 19.7 us
    ppermute x48 -> x47, starting transfers between devices: 45.5 us -> 44.4 us  [swapped(): return lax.ppermute(value, axis, [(i, i ^ by) for i in range(count)])]
  transfers between devices with their start and end apart: 59 -> 59, of which waited for: 28 -> 20; matrix products, arithmetic and copies ran while one was open for 25% -> 26% of each run, Pallas kernels for 17% -> 20%
where the time goes in v4:
time: 443 us; the launch traced here: 438 us
  Pallas kernels  120 us (27%)
  starting transfers between devices  78.4 us (18%)
  waiting for transfers between devices  72.5 us (16%)
  local copies, waits for them, and re-layouts  66.1 us (15%)
  other arithmetic  45.2 us (10%)
  matrix products  36.1 us (8%)
  between operations  20.1 us (5%)
    pallas_call x19, Pallas kernels, call(): pl.pallas_call(body, out_shape=[jax.ShapeDtypeStruct(o[2], o[3]) for o in...  120 us
    ppermute x47, waiting for transfers between devices, swapped(): return lax.ppermute(value, axis, [(i, i ^ by) for i in range(count)])  61.5 us
    ppermute x47, starting transfers between devices, swapped(): return lax.ppermute(value, axis, [(i, i ^ by) for i in range(count)])  44.4 us
    dot_general x18, matrix products, t_dot(): lax.dot_general(a, b, (((0,), (0,)), ((), ())), preferred_element_type=f32)  24.7 us
    unnamed x182, local copies, waits for them, and re-layouts  19.7 us
    all_to_all x2, starting transfers between devices, exchanged(): return lax.all_to_all(array_in, axis, 0, 0, tiled=True)  11.1 us
    ppermute x4, waiting for transfers between devices, shifted(): lax.ppermute(value, axis, [(i, i + by) for i in range(count) if 0 <= i +...  10.2 us
    ppermute x4, starting transfers between devices, shifted(): lax.ppermute(value, axis, [(i, i + by) for i in range(count) if 0 <= i +...  9.66 us
  transfers between devices with their start and end apart: 59, of which 20 were waited for; matrix products, arithmetic and copies ran while one was open for 26% of the time, Pallas kernels for 20%

profile of v4, /device:TPU:0, one launch (start us, length us, event | category | flops | bytes accessed | tf_op | source)
XLA Modules:
  0.0 438.4 jit_solution(431575301480802114)
XLA Ops:
  10.5 3.2 pack_kernel.1
  13.7 1.8 broadcast_in_dim.26
  15.5 6.3 %all-to-all-start = ((bf16[4,56,1664]{2,1,0:T(8,128)(2,1)}), bf16[4,56,1664]{2,1,0:T(8,128)(2,1)S(1)}, u32[]{:S(2)}, u32[]{:S(2)}) async-start(bf16[4,56,1664]{2,1,0:T(8,128)(2,1)} %broadcast_in_dim.26), calls=%async_computation | async-start | bytes 1490944 | tf_op jit(solution)/shard_map/all_to_all | solution.py:116
  23.1 3.4 collective-permute-start
  26.6 3.4 collective-permute-start.1
  32.3 10.2 %collective-permute-done.1 = bf16[136,896]{1,0:T(8,128)(2,1)S(1)} collective-permute-done((bf16[136,896]{1,0:T(8,128)(2,1)S(1)}, bf16[136,896]{1,0:T(8,128)(2,1)S(1)}, u32[]{:S(2)}, u32[]{:S(2)}) %collective-permute-start.1) | collective-permute-done | bytes 243744 | tf_op jit(solution)/shard_map/ppermute | solution.py:43
  43.3 2.5 collective-permute-start.3
  54.1 1.7 fusion.refs_1_.refs_4_.refs_6_
  57.5 1.9 pad_add_fusion.1
  64.9 3.1 turn_kernel.3.refs_2_
  70.0 3.1 fusion.88
  79.0 3.7 collective-permute-done.6
  83.9 5.0 %turn_kernel.4.refs_0_ = bf16[768,896]{1,0:T(8,128)(2,1)} custom-call(bf16[768,896]{1,0:T(8,128)(2,1)} %copy-done.20, bf16[896,896]{1,0:T(8,128)(2,1)} %fusion.refs_1_.refs_4_.refs_6_), custom_call_target="tpu_custom_call" | custom-call | tf_op jit(solution)/shard_map/turn_kernel/pallas_call | solution.py:203
  89.6 2.5 slice.298
  92.1 1.8 collective-permute-start.10
  99.6 1.8 slice_reduce_fusion.2
  102.1 6.8 %turn_kernel.5.refs_0_ = bf16[1280,896]{1,0:T(8,128)(2,1)} custom-call(bf16[1280,896]{1,0:T(8,128)(2,1)} %pad_maximum_fusion.refs_0_, bf16[896,896]{1,0:T(8,128)(2,1)} %fusion.refs_1_.refs_4_.refs_6_), custom_call_target="tpu_custom_call" | custom-call | tf_op jit(solution)/shard_map/turn_kernel/pallas_call | solution.py:203
  109.0 6.5 %qkv_kernel.1 = (bf16[768,896]{1,0:T(8,128)(2,1)}, bf16[256,512]{1,0:T(8,128)(2,1)}, bf16[768,512]{1,0:T(8,128)(2,1)}, bf16[768,512]{1,0:T(8,128)(2,1)}) custom-call(bf16[768,896]{1,0:T(8,128)(2,1)} %turn_kernel.4.refs_0_, f32[1,896]{1,0:T(1,128)} %copy.182.refs_1_, bf16[224,1664]{1,0:T(8,128)(2,1)} %bitcast.142, bf16[224,1664]{1,0:T(8,128)(2,1)} %copy-done.2, ...), custom_call_target="tpu_custom_call" | custom-call | tf_op jit(solution)/shard_map/qkv_kernel/pallas_call | solution.py:203
  115.4 9.2 %collective-permute-done.11.refs_8_.refs_4_ = bf16[224,1536]{1,0:T(8,128)(2,1)} collective-permute-done((bf16[224,1536]{1,0:T(8,128)(2,1)}, bf16[224,1536]{1,0:T(8,128)(2,1)}, u32[]{:S(2)}, u32[]{:S(2)}) %collective-permute-start.11) | collective-permute-done | bytes 688160 | tf_op jit(solution)/shard_map/ppermute | solution.py:53
  124.6 2.0 collective-permute-done.9.refs_6_.refs_2_
  127.0 1.8 collective-permute-start.13
  131.1 6.8 %rows_kernel.1.refs_9_.refs_10_.refs_13_.refs_14_ = bf16[1280,1024]{1,0:T(8,128)(2,1)} custom-call(bf16[1280,896]{1,0:T(8,128)(2,1)} %turn_kernel.5.refs_0_, bf16[224,2560]{1,0:T(8,128)(2,1)} %all-gather.3.cloned.1.call-done.refs_5_.refs_1_, bf16[224,1536]{1,0:T(8,128)(2,1)} %collective-permute-done.9.refs_6_.refs_2_, ...), custom_call_target="tpu_custom_call" | custom-call | tf_op jit(solution)/shard_map/rows_kernel/pallas_call | solution.py:203
  137.9 10.2 %self_kernel.1 = (bf16[256,512]{1,0:T(8,128)(2,1)}, f32[4,2,256]{2,1,0:T(2,128)}, f32[256,896]{1,0:T(8,128)}) custom-call(bf16[256,512]{1,0:T(8,128)(2,1)} %get-tuple-element.211.refs_0_.refs_9_, bf16[768,512]{1,0:T(8,128)(2,1)} %get-tuple-element.212.refs_1_.refs_10_, bf16[768,512]{1,0:T(8,128)(2,1)} %get-tuple-element.213.refs_2_.refs_11_, ...), custom_call_target="tpu_custom_call" | custom-call | tf_op jit(solution)/shard_map/self_kernel/pallas_call | solution.py:203
  151.3 1.8 collective-permute-start.16
  154.8 1.8 slice.299.refs_1_
  158.8 9.6 %cross_kernel.1 = (f32[256,896]{1,0:T(8,128)}, bf16[256,896]{1,0:T(8,128)(2,1)}, bf16[256,512]{1,0:T(8,128)(2,1)}, bf16[256,512]{1,0:T(8,128)(2,1)}, f32[4,4,128]{2,1,0:T(4,128)}, /*index=5*/f32[256,896]{1,0:T(8,128)}) custom-call(s32[5,2]{1,0:T(8,128)} %copy.187.refs_0_, bf16[256,896]{1,0:T(8,128)(2,1)} %slice.299.refs_1_, ...), custom_call_target="tpu_custom_call" | custom-call | tf_op jit(solution)/shard_map/cross_kernel/pallas_call | solution.py:203
  172.1 3.9 norm_kernel.1
  177.7 1.8 collective-permute-start.20
  181.2 4.9 %collective-permute-done.20 = bf16[128,896]{1,0:T(8,128)(2,1)S(1)} collective-permute-done((bf16[128,896]{1,0:T(8,128)(2,1)S(1)}, bf16[128,896]{1,0:T(8,128)(2,1)S(1)}, u32[]{:S(2)}, u32[]{:S(2)}) %collective-permute-start.20) | collective-permute-done | bytes 229408 | tf_op jit(solution)/shard_map/ppermute | solution.py:53
  186.2 5.7 %collective-permute-done.21 = bf16[128,896]{1,0:T(8,128)(2,1)S(1)} collective-permute-done((bf16[128,896]{1,0:T(8,128)(2,1)S(1)}, bf16[128,896]{1,0:T(8,128)(2,1)S(1)}, u32[]{:S(2)}, u32[]{:S(2)}) %collective-permute-start.21) | collective-permute-done | bytes 229408 | tf_op jit(solution)/shard_map/ppermute | solution.py:53
  195.5 10.2 %feed_kernel.1 = (bf16[1024,512]{1,0:T(8,128)(2,1)}, bf16[1024,512]{1,0:T(8,128)(2,1)}, bf16[512,896]{1,0:T(8,128)(2,1)}, bf16[512,896]{1,0:T(8,128)(2,1)}, f32[512,896]{1,0:T(8,128)}, /*index=5*/f32[512,896]{1,0:T(8,128)}) custom-call(bf16[1024,896]{1,0:T(8,128)(2,1)} %constant_dynamic-update-slice_fusion.refs_0_, bf16[1024,896]{1,0:T(8,128)(2,1)} %copy-done.16, ...), custom_call_target="tpu_custom_call" | custom-call | tf_op jit(solution)/shard_map/feed_kernel/pallas_call | solution.py:203
  206.2 3.6 collective-permute-done.25
  213.4 1.8 collective-permute-start.28
  215.2 4.9 %collective-permute-done.26 = bf16[128,896]{1,0:T(8,128)(2,1)S(1)} collective-permute-done((bf16[128,896]{1,0:T(8,128)(2,1)S(1)}, bf16[128,896]{1,0:T(8,128)(2,1)S(1)}, u32[]{:S(2)}, u32[]{:S(2)}) %collective-permute-start.26) | collective-permute-done | bytes 229408 | tf_op jit(solution)/shard_map/ppermute | solution.py:53
  220.1 4.4 %collective-permute-done.27 = bf16[128,896]{1,0:T(8,128)(2,1)S(1)} collective-permute-done((bf16[128,896]{1,0:T(8,128)(2,1)S(1)}, bf16[128,896]{1,0:T(8,128)(2,1)S(1)}, u32[]{:S(2)}, u32[]{:S(2)}) %collective-permute-start.27) | collective-permute-done | bytes 229408 | tf_op jit(solution)/shard_map/ppermute | solution.py:53
  227.3 14.5 %cross_back_kernel.1 = (f32[256,896]{1,0:T(8,128)}, bf16[256,896]{1,0:T(8,128)(2,1)}, f32[1,896]{1,0:T(1,128)}, bf16[256,512]{1,0:T(8,128)(2,1)}, bf16[1280,512]...) custom-call(s32[5,2]{1,0:T(8,128)} %copy.187.refs_0_, s32[1]{0:T(128)} %bitcast.20.refs_1_, ...), custom_call_target="tpu_custom_call" | custom-call | tf_op jit(solution)/shard_map/cross_back_kernel/pallas_call | solution.py:203
  243.5 2.7 convolution_convert_fusion.15
  255.6 12.1 %self_back_kernel.1 = (f32[256,896]{1,0:T(8,128)}, bf16[256,896]{1,0:T(8,128)(2,1)}, f32[1,896]{1,0:T(1,128)}, bf16[256,512]{1,0:T(8,128)(2,1)}, bf16[768,512]{1,0:T(8,128)(2,1)}, /*index=5*/bf16[768,512]{1,0:T(8,128)(2,1)}) custom-call(f32[256,896]{1,0:T(8,128)} %get-tuple-element.259.refs_0_, f32[256,896]{1,0:T(8,128)} %get-tuple-element.228.refs_0_.refs_1_, ...), custom_call_target="tpu_custom_call" | custom-call | tf_op jit(solution)/shard_map/self_back_kernel/pallas_call | solution.py:203
  267.8 4.0 collective-permute-done.31.refs_1_
  274.1 3.7 half_sum_kernel.2
  281.3 7.5 %inner_kernel.1 = (f32[768,896]{1,0:T(8,128)}, f32[1,896]{1,0:T(1,128)}) custom-call(bf16[768,896]{1,0:T(8,128)(2,1)} %turn_kernel.4.refs_0_, bf16[256,512]{1,0:T(8,128)(2,1)} %get-tuple-element.276.refs_1_, bf16[768,512]{1,0:T(8,128)(2,1)} %get-tuple-element.279.refs_2_, bf16[768,512]{1,0:T(8,128)(2,1)} %get-tuple-element.280.refs_3_, ...), custom_call_target="tpu_custom_call" | custom-call | tf_op jit(solution)/shard_map/inner_kernel/pallas_call | solution.py:203
  290.2 2.0 fusion.35
  293.1 3.1 convolution_convert_fusion.5
  296.2 1.7 convolution_convert_fusion.4
  298.0 2.6 last_sum_kernel.3
  300.6 2.3 pad_maximum_fusion.12
  307.8 4.6 %all-to-all-start.1 = ((f32[32,8,128]{2,1,0:T(8,128)}), f32[32,8,128]{2,1,0:T(8,128)}, u32[]{:S(2)}, u32[]{:S(2)}) async-start(f32[32,8,128]{2,1,0:T(8,128)} %bitcast.26), calls=%async_computation.1 | async-start | bytes 262144 | tf_op jit(solution)/shard_map/all_to_all | solution.py:1145
  312.5 3.2 convolution_convert_fusion.1
  317.2 2.5 copy.197
  322.5 2.0 convolution_convert_fusion.3
  329.4 3.6 half_sum_kernel.3
  335.4 10.2 %collective-permute-done.37.refs_1_ = bf16[224,1024]{1,0:T(8,128)(2,1)S(1)} collective-permute-done((bf16[224,1024]{1,0:T(8,128)(2,1)}, bf16[224,1024]{1,0:T(8,128)(2,1)S(1)}, u32[]{:S(2)}, u32[]{:S(2)}) %collective-permute-start.37) | collective-permute-done | bytes 458784 | tf_op jit(solution)/shard_map/ppermute | solution.py:53
  347.7 2.6 last_sum_kernel.2
  359.6 4.8 %all-to-all-start.2 = ((bf16[4,56,2048]{2,1,0:T(8,128)(2,1)}), bf16[4,56,2048]{2,1,0:T(8,128)(2,1)}, u32[]{:S(2)}, u32[]{:S(2)}) async-start(bf16[4,56,2048]{2,1,0:T(8,128)(2,1)} %bitcast.156), calls=%async_computation.2 | async-start | bytes 1835008 | tf_op jit(solution)/shard_map/all_to_all | solution.py:116
  376.1 2.6 collective-permute-start.40
  378.7 3.3 collective-permute-start.41
  382.9 2.0 copy.198
  384.9 1.9 multiply_reduce_fusion
  388.1 2.2 total_kernel.1
  390.9 1.8 dynamic-slice_bitcast_fusion.2
  393.4 7.6 %all-to-all-start.3 = ((f32[32,8,128]{2,1,0:T(8,128)}), f32[32,8,128]{2,1,0:T(8,128)}, u32[]{:S(2)}, u32[]{:S(2)}) async-start(f32[32,8,128]{2,1,0:T(8,128)} %broadcast_in_dim.62), calls=%async_computation.4 | async-start | bytes 262144 | tf_op jit(solution)/shard_map/all_to_all | solution.py:71
  401.1 1.8 collective-permute-start.48
  406.2 2.0 add_add_fusion
  414.8 5.9 %adam_kernel.1 = (f32[4,56,512]{2,1,0:T(8,128)}, f32[4,56,512]{2,1,0:T(8,128)}, f32[4,56,512]{2,1,0:T(8,128)}, f32[4,56,512]{2,1,0:T(8,128)}, f32[4,56,512]{2,1,...) custom-call(f32[1]{0:T(128)} %bitcast.43.refs_0_, ...), custom_call_target="tpu_custom_call" | custom-call | tf_op jit(solution)/shard_map/adam_kernel/pallas_call | solution.py:203
  (400 shorter events, 144.0 us)
Async XLA Ops:
  15.5 27.0 %all-to-all-start = ((bf16[4,56,1664]{2,1,0:T(8,128)(2,1)}), bf16[4,56,1664]{2,1,0:T(8,128)(2,1)S(1)}, u32[]{:S(2)}, u32[]{:S(2)}) async-start(bf16[4,56,1664]{2,1,0:T(8,128)(2,1)} %broadcast_in_dim.26), calls=%async_computation | async-start | bytes 1490944 | tf_op jit(solution)/shard_map/all_to_all | solution.py:116
  21.8 67.8 %all-gather.3.cloned.1.call-start = ((), (), s32[]{:S(2)}) async-start(), calls=%async_computation.6 | async-start | bytes 1433600 | tf_op jit(solution)/shard_map/all_gather | solution.py:999
  21.8 24.0 %copy-start.65 = (s32[1,256]{1,0:T(1,128)}, s32[1,256]{1,0:T(1,128)S(1)}, u32[]{:S(2)}) copy-start(s32[1,256]{1,0:T(1,128)S(1)} %get-tuple-element.467.refs_3_.refs_13_) | copy-start | bytes 3076
  23.1 19.3 %collective-permute-start = (bf16[264,896]{1,0:T(8,128)(2,1)S(1)}, bf16[264,896]{1,0:T(8,128)(2,1)S(1)}, u32[]{:S(2)}, u32[]{:S(2)}) collective-permute-start(bf16[264,896]{1,0:T(8,128)(2,1)S(1)} %pad_maximum_fusion.25), channel_id=1, source_target_pairs={{0,2},{2,4},{4,6},{1,3},{3,5},{5,7},{8,10},{10,12},{12,14},{9,11},... | collective-permute-start | bytes 1419272 | tf_op jit(solution)/shard_map/ppermute | solution.py:43
  26.6 15.9 %collective-permute-start.1 = (bf16[136,896]{1,0:T(8,128)(2,1)S(1)}, bf16[136,896]{1,0:T(8,128)(2,1)S(1)}, u32[]{:S(2)}, u32[]{:S(2)}) collective-permute-start(bf16[136,896]{1,0:T(8,128)(2,1)S(1)} %pad_maximum_fusion.26), channel_id=1, source_target_pairs={{0,4},{2,6},{1,5},{3,7},{8,12},{10,14},{9,13},{11,15},{16,20},{18,... | collective-permute-start | bytes 731144 | tf_op jit(solution)/shard_map/ppermute | solution.py:43
  43.3 45.6 %collective-permute-start.3 = (bf16[224,1664]{1,0:T(8,128)(2,1)S(1)}, bf16[224,1664]{1,0:T(8,128)(2,1)S(1)}, u32[]{:S(2)}, u32[]{:S(2)}) collective-permute-start(bf16[224,1664]{1,0:T(8,128)(2,1)S(1)} %bitcast.138), channel_id=1, source_target_pairs={{0,4},{2,6},{4,0},{6,2},{1,5},{3,7},{5,1},{7,3},{8,12},{10,14},{12... | collective-permute-start | bytes 2236424 | tf_op jit(solution)/shard_map/ppermute | solution.py:53
  45.8 43.1 %collective-permute-start.4 = (bf16[224,1664]{1,0:T(8,128)(2,1)S(1)}, bf16[224,1664]{1,0:T(8,128)(2,1)S(1)}, u32[]{:S(2)}, u32[]{:S(2)}) collective-permute-start(bf16[224,1664]{1,0:T(8,128)(2,1)S(1)} %bitcast.139), channel_id=1, source_target_pairs={{0,2},{2,0},{4,6},{6,4},{1,3},{3,1},{5,7},{7,5},{8,10},{10,8},{12,... | collective-permute-start | bytes 2236424 | tf_op jit(solution)/shard_map/ppermute | solution.py:53
  45.8 43.8 %collective-permute-start.5 = (bf16[224,1664]{1,0:T(8,128)(2,1)S(1)}, bf16[224,1664]{1,0:T(8,128)(2,1)S(1)}, u32[]{:S(2)}, u32[]{:S(2)}) collective-permute-start(bf16[224,1664]{1,0:T(8,128)(2,1)S(1)} %bitcast.140), channel_id=1, source_target_pairs={{0,6},{2,4},{4,2},{6,0},{1,7},{3,5},{5,3},{7,1},{8,14},{10,12},{12... | collective-permute-start | bytes 2236424 | tf_op jit(solution)/shard_map/ppermute | solution.py:53
  54.1 19.0 %collective-permute-start.2 = (bf16[384,896]{1,0:T(8,128)(2,1)}, bf16[384,896]{1,0:T(8,128)(2,1)}, u32[]{:S(2)}, u32[]{:S(2)}) collective-permute-start(bf16[384,896]{1,0:T(8,128)(2,1)} %pad_maximum_fusion.20), channel_id=1, source_target_pairs={{0,1},{1,0},{2,3},{3,2},{4,5},{5,4},{6,7},{7,6},{8,9},{9,8},{10,11... | collective-permute-start | bytes 2064392 | tf_op jit(solution)/shard_map/ppermute | solution.py:53
  56.5 26.1 %collective-permute-start.6 = (bf16[56,1024]{1,0:T(8,128)(2,1)}, bf16[56,1024]{1,0:T(8,128)(2,1)}, u32[]{:S(2)}, u32[]{:S(2)}) collective-permute-start(bf16[56,1024]{1,0:T(8,128)(2,1)} %get-tuple-element.459), channel_id=1, source_target_pairs={{0,2},{2,0},{4,6},{6,4},{1,3},{3,1},{5,7},{7,5},{8,10},{10,8},{12,... | collective-permute-start | bytes 344072 | tf_op jit(solution)/shard_map/ppermute | solution.py:53
  57.1 138.4 %all-gather.5.cloned.1.call-start = ((), (), s32[]{:S(2)}) async-start(), calls=%async_computation.7 | async-start | bytes 2293760 | tf_op jit(solution)/shard_map/all_gather | solution.py:1039
  73.0 15.9 %collective-permute-start.7 = (bf16[56,1024]{1,0:T(8,128)(2,1)}, bf16[56,1024]{1,0:T(8,128)(2,1)S(1)}, u32[]{:S(2)}, u32[]{:S(2)}) collective-permute-start(bf16[56,1024]{1,0:T(8,128)(2,1)} %get-tuple-element.458), channel_id=1, source_target_pairs={{0,4},{2,6},{4,0},{6,2},{1,5},{3,7},{5,1},{7,3},{8,12},{10,14},{12... | collective-permute-start | bytes 344072 | tf_op jit(solution)/shard_map/ppermute | solution.py:53
  82.7 6.2 %collective-permute-start.8 = (bf16[56,1024]{1,0:T(8,128)(2,1)S(1)}, bf16[56,1024]{1,0:T(8,128)(2,1)S(1)}, u32[]{:S(2)}, u32[]{:S(2)}) collective-permute-start(bf16[56,1024]{1,0:T(8,128)(2,1)S(1)} %copy-done.59), channel_id=1, source_target_pairs={{0,6},{2,4},{4,2},{6,0},{1,7},{3,5},{5,3},{7,1},{8,14},{10,12},{12... | collective-permute-start | bytes 344072 | tf_op jit(solution)/shard_map/ppermute | solution.py:53
  92.1 23.4 %collective-permute-start.10 = (bf16[224,1536]{1,0:T(8,128)(2,1)}, bf16[224,1536]{1,0:T(8,128)(2,1)}, u32[]{:S(2)}, u32[]{:S(2)}) collective-permute-start(bf16[224,1536]{1,0:T(8,128)(2,1)} %slice.298), channel_id=1, source_target_pairs={{0,2},{2,0},{4,6},{6,4},{1,3},{3,1},{5,7},{7,5},{8,10},{10,8},{12,... | collective-permute-start | bytes 2064392 | tf_op jit(solution)/shard_map/ppermute | solution.py:53
  93.8 30.8 %collective-permute-start.11 = (bf16[224,1536]{1,0:T(8,128)(2,1)}, bf16[224,1536]{1,0:T(8,128)(2,1)}, u32[]{:S(2)}, u32[]{:S(2)}) collective-permute-start(bf16[224,1536]{1,0:T(8,128)(2,1)} %slice.298), channel_id=1, source_target_pairs={{0,6},{2,4},{4,2},{6,0},{1,7},{3,5},{5,3},{7,1},{8,14},{10,12},{12... | collective-permute-start | bytes 2064392 | tf_op jit(solution)/shard_map/ppermute | solution.py:53
  95.2 31.4 %collective-permute-start.9 = (bf16[224,1536]{1,0:T(8,128)(2,1)}, bf16[224,1536]{1,0:T(8,128)(2,1)}, u32[]{:S(2)}, u32[]{:S(2)}) collective-permute-start(bf16[224,1536]{1,0:T(8,128)(2,1)} %slice.298), channel_id=1, source_target_pairs={{0,4},{2,6},{4,0},{6,2},{1,5},{3,7},{5,1},{7,3},{8,12},{10,14},{12... | collective-permute-start | bytes 2064392 | tf_op jit(solution)/shard_map/ppermute | solution.py:53
  98.6 30.2 %copy-start.7 = (bf16[224,1024]{1,0:T(8,128)(2,1)}, bf16[224,1024]{1,0:T(8,128)(2,1)S(1)}, u32[]{:S(2)}) copy-start(bf16[224,1024]{1,0:T(8,128)(2,1)S(1)} %slice.297.refs_5_.refs_12_.refs_8_.refs_17_) | copy-start | bytes 1376260
  109.0 21.2 %copy-start.68 = (s32[768,1]{0,1:T(1,128)S(1)}, s32[768,1]{0,1:T(1,128)}, u32[]{:S(2)}) copy-start(s32[768,1]{0,1:T(1,128)} %add_bitcast_fusion) | copy-start | bytes 9220
  126.7 21.5 %collective-permute-start.12 = (bf16[224,1024]{1,0:T(8,128)(2,1)S(1)}, bf16[224,1024]{1,0:T(8,128)(2,1)S(1)}, u32[]{:S(2)}, u32[]{:S(2)}) collective-permute-start(bf16[224,1024]{1,0:T(8,128)(2,1)S(1)} %slice.297.refs_5_.refs_12_.refs_8_.refs_17_), channel_id=1, source_target_pairs={{0,4},{2,6},{4,0},{6,2},{1,5},{3,7},{5,1},{7,3},{8,12},{10,14},{12... | collective-permute-start | bytes 1376264 | tf_op jit(solution)/shard_map/ppermute | solution.py:53
  127.0 21.2 %collective-permute-start.13 = (bf16[224,1024]{1,0:T(8,128)(2,1)S(1)}, bf16[224,1024]{1,0:T(8,128)(2,1)S(1)}, u32[]{:S(2)}, u32[]{:S(2)}) collective-permute-start(bf16[224,1024]{1,0:T(8,128)(2,1)S(1)} %slice.297.refs_5_.refs_12_.refs_8_.refs_17_), channel_id=1, source_target_pairs={{0,2},{2,0},{4,6},{6,4},{1,3},{3,1},{5,7},{7,5},{8,10},{10,8},{12,... | collective-permute-start | bytes 1376264 | tf_op jit(solution)/shard_map/ppermute | solution.py:53
  128.8 19.4 %collective-permute-start.14 = (bf16[224,1024]{1,0:T(8,128)(2,1)S(1)}, bf16[224,1024]{1,0:T(8,128)(2,1)S(1)}, u32[]{:S(2)}, u32[]{:S(2)}) collective-permute-start(bf16[224,1024]{1,0:T(8,128)(2,1)S(1)} %slice.297.refs_5_.refs_12_.refs_8_.refs_17_), channel_id=1, source_target_pairs={{0,6},{2,4},{4,2},{6,0},{1,7},{3,5},{5,3},{7,1},{8,14},{10,12},{12... | collective-permute-start | bytes 1376264 | tf_op jit(solution)/shard_map/ppermute | solution.py:53
  148.2 10.6 %collective-permute-start.15 = (f32[256,896]{1,0:T(8,128)}, f32[256,896]{1,0:T(8,128)}, u32[]{:S(2)}, u32[]{:S(2)}) collective-permute-start(f32[256,896]{1,0:T(8,128)} %get-tuple-element.222.refs_2_), channel_id=1, source_target_pairs={{0,1},{1,0},{2,3},{3,2},{4,5},{5,4},{6,7},{7,6},{8,9},{9,8},{10,11... | collective-permute-start | bytes 2752520 | tf_op jit(solution)/shard_map/ppermute | solution.py:53
  150.7 213.8 %reduce-scatter.5.cloned.1.call-start = ((), (), s32[]{:S(2)}) async-start(), calls=%async_computation.8 | async-start | bytes 1146880 | tf_op jit(solution)/shard_map/reduce_scatter | solution.py:1147
  151.3 17.1 %collective-permute-start.16 = (bf16[128,896]{1,0:T(8,128)(2,1)S(1)}, bf16[128,896]{1,0:T(8,128)(2,1)S(1)}, u32[]{:S(2)}, u32[]{:S(2)}) collective-permute-start(bf16[128,896]{1,0:T(8,128)(2,1)S(1)} %constant_dynamic-slice_fusion.1), channel_id=1, source_target_pairs={{0,2},{2,0},{4,6},{6,4},{1,3},{3,1},{5,7},{7,5},{8,10},{10,8},{12,... | collective-permute-start | bytes 688136 | tf_op jit(solution)/shard_map/ppermute | solution.py:53
  153.1 15.3 %collective-permute-start.17 = (bf16[128,896]{1,0:T(8,128)(2,1)S(1)}, bf16[128,896]{1,0:T(8,128)(2,1)S(1)}, u32[]{:S(2)}, u32[]{:S(2)}) collective-permute-start(bf16[128,896]{1,0:T(8,128)(2,1)S(1)} %constant_dynamic-slice_fusion.1), channel_id=1, source_target_pairs={{0,4},{2,6},{4,0},{6,2},{1,5},{3,7},{5,1},{7,3},{8,12},{10,14},{12... | collective-permute-start | bytes 688136 | tf_op jit(solution)/shard_map/ppermute | solution.py:53
  153.4 15.0 %collective-permute-start.18 = (bf16[128,896]{1,0:T(8,128)(2,1)S(1)}, bf16[128,896]{1,0:T(8,128)(2,1)S(1)}, u32[]{:S(2)}, u32[]{:S(2)}) collective-permute-start(bf16[128,896]{1,0:T(8,128)(2,1)S(1)} %constant_dynamic-slice_fusion.1), channel_id=1, source_target_pairs={{0,6},{2,4},{4,2},{6,0},{1,7},{3,5},{5,3},{7,1},{8,14},{10,12},{12... | collective-permute-start | bytes 688136 | tf_op jit(solution)/shard_map/ppermute | solution.py:53
  168.4 2.7 collective-permute-start.19
  169.4 22.7 %collective-permute-start.24 = (bf16[512,896]{1,0:T(8,128)(2,1)S(1)}, bf16[512,896]{1,0:T(8,128)(2,1)S(1)}, u32[]{:S(2)}, u32[]{:S(2)}) collective-permute-start(bf16[512,896]{1,0:T(8,128)(2,1)S(1)} %pad_maximum_fusion.5), channel_id=1, source_target_pairs={{0,1},{1,0},{2,3},{3,2},{4,5},{5,4},{6,7},{7,6},{8,9},{9,8},{10,11... | collective-permute-start | bytes 2752520 | tf_op jit(solution)/shard_map/ppermute | solution.py:53
  177.7 8.4 %collective-permute-start.20 = (bf16[128,896]{1,0:T(8,128)(2,1)S(1)}, bf16[128,896]{1,0:T(8,128)(2,1)S(1)}, u32[]{:S(2)}, u32[]{:S(2)}) collective-permute-start(bf16[128,896]{1,0:T(8,128)(2,1)S(1)} %get-tuple-element.422), channel_id=1, source_target_pairs={{0,2},{2,0},{4,6},{6,4},{1,3},{3,1},{5,7},{7,5},{8,10},{10,8},{12,... | collective-permute-start | bytes 688136 | tf_op jit(solution)/shard_map/ppermute | solution.py:53
  179.5 12.3 %collective-permute-start.21 = (bf16[128,896]{1,0:T(8,128)(2,1)S(1)}, bf16[128,896]{1,0:T(8,128)(2,1)S(1)}, u32[]{:S(2)}, u32[]{:S(2)}) collective-permute-start(bf16[128,896]{1,0:T(8,128)(2,1)S(1)} %get-tuple-element.422), channel_id=1, source_target_pairs={{0,4},{2,6},{4,0},{6,2},{1,5},{3,7},{5,1},{7,3},{8,12},{10,14},{12... | collective-permute-start | bytes 688136 | tf_op jit(solution)/shard_map/ppermute | solution.py:53
  180.0 11.8 %collective-permute-start.22 = (bf16[128,896]{1,0:T(8,128)(2,1)S(1)}, bf16[128,896]{1,0:T(8,128)(2,1)S(1)}, u32[]{:S(2)}, u32[]{:S(2)}) collective-permute-start(bf16[128,896]{1,0:T(8,128)(2,1)S(1)} %get-tuple-element.422), channel_id=1, source_target_pairs={{0,6},{2,4},{4,2},{6,0},{1,7},{3,5},{5,3},{7,1},{8,14},{10,12},{12... | collective-permute-start | bytes 688136 | tf_op jit(solution)/shard_map/ppermute | solution.py:53
  191.9 2.6 collective-permute-start.23
  205.7 4.1 collective-permute-start.25
  211.6 8.5 %collective-permute-start.26 = (bf16[128,896]{1,0:T(8,128)(2,1)S(1)}, bf16[128,896]{1,0:T(8,128)(2,1)S(1)}, u32[]{:S(2)}, u32[]{:S(2)}) collective-permute-start(bf16[128,896]{1,0:T(8,128)(2,1)S(1)} %get-tuple-element.440), channel_id=1, source_target_pairs={{0,2},{2,0},{4,6},{6,4},{1,3},{3,1},{5,7},{7,5},{8,10},{10,8},{12,... | collective-permute-start | bytes 688136 | tf_op jit(solution)/shard_map/ppermute | solution.py:53
  212.0 12.6 %collective-permute-start.27 = (bf16[128,896]{1,0:T(8,128)(2,1)S(1)}, bf16[128,896]{1,0:T(8,128)(2,1)S(1)}, u32[]{:S(2)}, u32[]{:S(2)}) collective-permute-start(bf16[128,896]{1,0:T(8,128)(2,1)S(1)} %get-tuple-element.442), channel_id=1, source_target_pairs={{0,4},{2,6},{4,0},{6,2},{1,5},{3,7},{5,1},{7,3},{8,12},{10,14},{12... | collective-permute-start | bytes 688136 | tf_op jit(solution)/shard_map/ppermute | solution.py:53
  213.4 11.1 %collective-permute-start.28 = (bf16[128,896]{1,0:T(8,128)(2,1)S(1)}, bf16[128,896]{1,0:T(8,128)(2,1)S(1)}, u32[]{:S(2)}, u32[]{:S(2)}) collective-permute-start(bf16[128,896]{1,0:T(8,128)(2,1)S(1)} %get-tuple-element.441), channel_id=1, source_target_pairs={{0,6},{2,4},{4,2},{6,0},{1,7},{3,5},{5,3},{7,1},{8,14},{10,12},{12... | collective-permute-start | bytes 688136 | tf_op jit(solution)/shard_map/ppermute | solution.py:53
  224.7 1.9 collective-permute-start.29
  227.3 14.7 %copy-start.42 = (bf16[256,896]{1,0:T(8,128)(2,1)S(1)}, bf16[256,896]{1,0:T(8,128)(2,1)}, u32[]{:S(2)}) copy-start(bf16[256,896]{1,0:T(8,128)(2,1)} %get-tuple-element.234) | copy-start | bytes 1376260
  241.8 7.3 %collective-permute-start.30 = (f32[256,896]{1,0:T(8,128)}, f32[256,896]{1,0:T(8,128)S(1)}, u32[]{:S(2)}, u32[]{:S(2)}) collective-permute-start(f32[256,896]{1,0:T(8,128)} %get-tuple-element.254.refs_2_), channel_id=1, source_target_pairs={{0,1},{1,0},{2,3},{3,2},{4,5},{5,4},{6,7},{7,6},{8,9},{9,8},{10,11... | collective-permute-start | bytes 2752520 | tf_op jit(solution)/shard_map/ppermute | solution.py:53
  249.1 22.7 %collective-permute-start.31 = (bf16[448,1024]{1,0:T(8,128)(2,1)S(1)}, bf16[448,1024]{1,0:T(8,128)(2,1)S(1)}, u32[]{:S(2)}, u32[]{:S(2)}) collective-permute-start(bf16[448,1024]{1,0:T(8,128)(2,1)S(1)} %get-tuple-element.257), channel_id=1, source_target_pairs={{0,2},{2,0},{4,6},{6,4},{1,3},{3,1},{5,7},{7,5},{8,10},{10,8},{12,... | collective-permute-start | bytes 2752520 | tf_op jit(solution)/shard_map/ppermute | solution.py:53
  250.8 22.3 %collective-permute-start.32 = (bf16[448,1024]{1,0:T(8,128)(2,1)S(1)}, bf16[448,1024]{1,0:T(8,128)(2,1)S(1)}, u32[]{:S(2)}, u32[]{:S(2)}) collective-permute-start(bf16[448,1024]{1,0:T(8,128)(2,1)S(1)} %get-tuple-element.258), channel_id=1, source_target_pairs={{0,4},{2,6},{4,0},{6,2},{1,5},{3,7},{5,1},{7,3},{8,12},{10,14},{12... | collective-permute-start | bytes 2752520 | tf_op jit(solution)/shard_map/ppermute | solution.py:53
  277.8 11.9 %collective-permute-start.33 = (bf16[224,1024]{1,0:T(8,128)(2,1)}, bf16[224,1024]{1,0:T(8,128)(2,1)S(1)}, u32[]{:S(2)}, u32[]{:S(2)}) collective-permute-start(bf16[224,1024]{1,0:T(8,128)(2,1)} %get-tuple-element.274), channel_id=1, source_target_pairs={{0,4},{2,6},{4,0},{6,2},{1,5},{3,7},{5,1},{7,3},{8,12},{10,14},{12... | collective-permute-start | bytes 1376264 | tf_op jit(solution)/shard_map/ppermute | solution.py:53
  278.3 11.9 %collective-permute-start.34 = (bf16[224,1024]{1,0:T(8,128)(2,1)}, bf16[224,1024]{1,0:T(8,128)(2,1)}, u32[]{:S(2)}, u32[]{:S(2)}) collective-permute-start(bf16[224,1024]{1,0:T(8,128)(2,1)} %get-tuple-element.275), channel_id=1, source_target_pairs={{0,2},{2,0},{4,6},{6,4},{1,3},{3,1},{5,7},{7,5},{8,10},{10,8},{12,... | collective-permute-start | bytes 1376264 | tf_op jit(solution)/shard_map/ppermute | solution.py:53
  305.5 23.9 %collective-permute-start.35 = (bf16[448,1024]{1,0:T(8,128)(2,1)}, bf16[448,1024]{1,0:T(8,128)(2,1)}, u32[]{:S(2)}, u32[]{:S(2)}) collective-permute-start(bf16[448,1024]{1,0:T(8,128)(2,1)} %pad_maximum_fusion.11), channel_id=1, source_target_pairs={{0,2},{2,0},{4,6},{6,4},{1,3},{3,1},{5,7},{7,5},{8,10},{10,8},{12,... | collective-permute-start | bytes 2752520 | tf_op jit(solution)/shard_map/ppermute | solution.py:53
  306.6 22.8 %collective-permute-start.36 = (bf16[448,1024]{1,0:T(8,128)(2,1)}, bf16[448,1024]{1,0:T(8,128)(2,1)}, u32[]{:S(2)}, u32[]{:S(2)}) collective-permute-start(bf16[448,1024]{1,0:T(8,128)(2,1)} %pad_maximum_fusion.12), channel_id=1, source_target_pairs={{0,4},{2,6},{4,0},{6,2},{1,5},{3,7},{5,1},{7,3},{8,12},{10,14},{12... | collective-permute-start | bytes 2752520 | tf_op jit(solution)/shard_map/ppermute | solution.py:53
  307.8 20.6 %all-to-all-start.1 = ((f32[32,8,128]{2,1,0:T(8,128)}), f32[32,8,128]{2,1,0:T(8,128)}, u32[]{:S(2)}, u32[]{:S(2)}) async-start(f32[32,8,128]{2,1,0:T(8,128)} %bitcast.26), calls=%async_computation.1 | async-start | bytes 262144 | tf_op jit(solution)/shard_map/all_to_all | solution.py:1145
  312.4 70.5 %reduce-scatter.7.cloned.1.call-start = ((), (), s32[]{:S(2)}) async-start(), calls=%async_computation.9 | async-start | bytes 2293760 | tf_op jit(solution)/shard_map/reduce_scatter | solution.py:1153
  329.3 27.8 %copy-start.66 = (f32[3,56]{1,0:T(4,128)}, f32[3,56]{1,0:T(4,128)S(1)}, u32[]{:S(2)}) copy-start(f32[3,56]{1,0:T(4,128)S(1)} %slice.320) | copy-start | bytes 2020
  333.0 12.6 %collective-permute-start.37 = (bf16[224,1024]{1,0:T(8,128)(2,1)}, bf16[224,1024]{1,0:T(8,128)(2,1)S(1)}, u32[]{:S(2)}, u32[]{:S(2)}) collective-permute-start(bf16[224,1024]{1,0:T(8,128)(2,1)} %get-tuple-element.292), channel_id=1, source_target_pairs={{0,4},{2,6},{4,0},{6,2},{1,5},{3,7},{5,1},{7,3},{8,12},{10,14},{12... | collective-permute-start | bytes 1376264 | tf_op jit(solution)/shard_map/ppermute | solution.py:53
  334.4 12.5 %collective-permute-start.38 = (bf16[224,1024]{1,0:T(8,128)(2,1)}, bf16[224,1024]{1,0:T(8,128)(2,1)S(1)}, u32[]{:S(2)}, u32[]{:S(2)}) collective-permute-start(bf16[224,1024]{1,0:T(8,128)(2,1)} %get-tuple-element.293), channel_id=1, source_target_pairs={{0,2},{2,0},{4,6},{6,4},{1,3},{3,1},{5,7},{7,5},{8,10},{10,8},{12,... | collective-permute-start | bytes 1376264 | tf_op jit(solution)/shard_map/ppermute | solution.py:53
  354.2 13.7 %collective-permute-start.43 = (f32[2,128,896]{2,1,0:T(8,128)}, f32[2,128,896]{2,1,0:T(8,128)}, u32[]{:S(2)}, u32[]{:S(2)}) collective-permute-start(f32[2,128,896]{2,1,0:T(8,128)} %dynamic-slice_bitcast_fusion), channel_id=1, source_target_pairs={{0,1},{1,0},{2,3},{3,2},{4,5},{5,4},{6,7},{7,6},{8,9},{9,8},{10,11... | collective-permute-start | bytes 2752520 | tf_op jit(solution)/shard_map/ppermute | solution.py:53
  356.6 17.2 %collective-permute-start.39 = (bf16[512,896]{1,0:T(8,128)(2,1)}, bf16[512,896]{1,0:T(8,128)(2,1)}, u32[]{:S(2)}, u32[]{:S(2)}) collective-permute-start(bf16[512,896]{1,0:T(8,128)(2,1)} %get-tuple-element.315), channel_id=1, source_target_pairs={{0,1},{1,0},{2,3},{3,2},{4,5},{5,4},{6,7},{7,6},{8,9},{9,8},{10,11... | collective-permute-start | bytes 2752520 | tf_op jit(solution)/shard_map/ppermute | solution.py:53
  359.6 28.5 %all-to-all-start.2 = ((bf16[4,56,2048]{2,1,0:T(8,128)(2,1)}), bf16[4,56,2048]{2,1,0:T(8,128)(2,1)}, u32[]{:S(2)}, u32[]{:S(2)}) async-start(bf16[4,56,2048]{2,1,0:T(8,128)(2,1)} %bitcast.156), calls=%async_computation.2 | async-start | bytes 1835008 | tf_op jit(solution)/shard_map/all_to_all | solution.py:116
  371.0 21.8 %collective-permute-start.44 = (bf16[128,896]{1,0:T(8,128)(2,1)}, bf16[128,896]{1,0:T(8,128)(2,1)}, u32[]{:S(2)}, u32[]{:S(2)}) collective-permute-start(bf16[128,896]{1,0:T(8,128)(2,1)} %get-tuple-element.456), channel_id=1, source_target_pairs={{2,0},{4,2},{6,4},{3,1},{5,3},{7,5},{10,8},{12,10},{14,12},{11,9},... | collective-permute-start | bytes 688136 | tf_op jit(solution)/shard_map/ppermute | solution.py:43
  372.3 20.5 %collective-permute-start.45 = (bf16[128,896]{1,0:T(8,128)(2,1)}, bf16[128,896]{1,0:T(8,128)(2,1)}, u32[]{:S(2)}, u32[]{:S(2)}) collective-permute-start(bf16[128,896]{1,0:T(8,128)(2,1)} %get-tuple-element.455), channel_id=1, source_target_pairs={{4,0},{6,2},{5,1},{7,3},{12,8},{14,10},{13,9},{15,11},{20,16},{22,... | collective-permute-start | bytes 688136 | tf_op jit(solution)/shard_map/ppermute | solution.py:43
  376.1 16.7 %collective-permute-start.40 = (bf16[128,896]{1,0:T(8,128)(2,1)}, bf16[128,896]{1,0:T(8,128)(2,1)}, u32[]{:S(2)}, u32[]{:S(2)}) collective-permute-start(bf16[128,896]{1,0:T(8,128)(2,1)} %get-tuple-element.439), channel_id=1, source_target_pairs={{0,2},{2,0},{4,6},{6,4},{1,3},{3,1},{5,7},{7,5},{8,10},{10,8},{12,... | collective-permute-start | bytes 688136 | tf_op jit(solution)/shard_map/ppermute | solution.py:53
  378.7 14.0 %collective-permute-start.41 = (bf16[128,896]{1,0:T(8,128)(2,1)}, bf16[128,896]{1,0:T(8,128)(2,1)}, u32[]{:S(2)}, u32[]{:S(2)}) collective-permute-start(bf16[128,896]{1,0:T(8,128)(2,1)} %get-tuple-element.438), channel_id=1, source_target_pairs={{0,4},{2,6},{4,0},{6,2},{1,5},{3,7},{5,1},{7,3},{8,12},{10,14},{12... | collective-permute-start | bytes 688136 | tf_op jit(solution)/shard_map/ppermute | solution.py:53
  382.1 10.7 %collective-permute-start.42 = (bf16[128,896]{1,0:T(8,128)(2,1)}, bf16[128,896]{1,0:T(8,128)(2,1)}, u32[]{:S(2)}, u32[]{:S(2)}) collective-permute-start(bf16[128,896]{1,0:T(8,128)(2,1)} %get-tuple-element.437), channel_id=1, source_target_pairs={{0,6},{2,4},{4,2},{6,0},{1,7},{3,5},{5,3},{7,1},{8,14},{10,12},{12... | collective-permute-start | bytes 688136 | tf_op jit(solution)/shard_map/ppermute | solution.py:53
  393.4 19.1 %all-to-all-start.3 = ((f32[32,8,128]{2,1,0:T(8,128)}), f32[32,8,128]{2,1,0:T(8,128)}, u32[]{:S(2)}, u32[]{:S(2)}) async-start(f32[32,8,128]{2,1,0:T(8,128)} %broadcast_in_dim.62), calls=%async_computation.4 | async-start | bytes 262144 | tf_op jit(solution)/shard_map/all_to_all | solution.py:71
  401.1 7.7 %collective-permute-start.48 = (bf16[56,1024]{1,0:T(8,128)(2,1)}, bf16[56,1024]{1,0:T(8,128)(2,1)S(1)}, u32[]{:S(2)}, u32[]{:S(2)}) collective-permute-start(bf16[56,1024]{1,0:T(8,128)(2,1)} %get-tuple-element.327), channel_id=1, source_target_pairs={{0,2},{2,0},{4,6},{6,4},{1,3},{3,1},{5,7},{7,5},{8,10},{10,8},{12,... | collective-permute-start | bytes 344072 | tf_op jit(solution)/shard_map/ppermute | solution.py:53
  402.8 7.3 %collective-permute-start.49 = (bf16[56,1024]{1,0:T(8,128)(2,1)}, bf16[56,1024]{1,0:T(8,128)(2,1)S(1)}, u32[]{:S(2)}, u32[]{:S(2)}) collective-permute-start(bf16[56,1024]{1,0:T(8,128)(2,1)} %get-tuple-element.328), channel_id=1, source_target_pairs={{0,4},{2,6},{4,0},{6,2},{1,5},{3,7},{5,1},{7,3},{8,12},{10,14},{12... | collective-permute-start | bytes 344072 | tf_op jit(solution)/shard_map/ppermute | solution.py:53
  404.3 7.1 %collective-permute-start.50 = (bf16[56,1024]{1,0:T(8,128)(2,1)}, bf16[56,1024]{1,0:T(8,128)(2,1)S(1)}, u32[]{:S(2)}, u32[]{:S(2)}) collective-permute-start(bf16[56,1024]{1,0:T(8,128)(2,1)} %get-tuple-element.329), channel_id=1, source_target_pairs={{0,6},{2,4},{4,2},{6,0},{1,7},{3,5},{5,3},{7,1},{8,14},{10,12},{12... | collective-permute-start | bytes 344072 | tf_op jit(solution)/shard_map/ppermute | solution.py:53
  406.1 18.1 %collective-permute-start.47 = (f32[256,896]{1,0:T(8,128)S(1)}, f32[256,896]{1,0:T(8,128)}, u32[]{:S(2)}, u32[]{:S(2)}) collective-permute-start(f32[256,896]{1,0:T(8,128)S(1)} %fusion.5), channel_id=1, source_target_pairs={{0,1},{1,0},{2,3},{3,2},{4,5},{5,4},{6,7},{7,6},{8,9},{9,8},{10,11... | collective-permute-start | bytes 2752520 | tf_op jit(solution)/shard_map/ppermute | solution.py:53
  408.2 13.2 %collective-permute-start.46 = (f32[128,896]{1,0:T(8,128)}, f32[128,896]{1,0:T(8,128)}, u32[]{:S(2)}, u32[]{:S(2)}) collective-permute-start(f32[128,896]{1,0:T(8,128)} %add_add_fusion), channel_id=1, source_target_pairs={{0,1},{1,0},{2,3},{3,2},{4,5},{5,4},{6,7},{7,6},{8,9},{9,8},{10,11... | collective-permute-start | bytes 1376264 | tf_op jit(solution)/shard_map/ppermute | solution.py:53
  (76 other events, 377.3 us)
Sparse Core Ops, SparseCore 0:
  57.2 31.2 all-gather.2
  150.8 41.9 all-gather.4
  300.7 27.6 reduce-scatter.4
  330.6 38.2 reduce-scatter.6
